TPU v7x, 256 devices: a whole 4x4x8 slice. The times are simulated.
256 devices in a mesh: seq: 64 (over z, y, core), chan: 4 (over x).
Axes of the slice: x: 4, y: 4, z: 8, core: 2. Of those that a mesh axis runs over, the one named last changes fastest.
Arguments:
- features: bfloat16 [32768, 512], P('seq', 'chan'), may hold values from -600 to 600
- pre_gate: bfloat16 [32768, 512], P('seq', 'chan'), may hold values from -6 to 6
- post_gate: bfloat16 [32768, 512], P('seq', 'chan'), may hold values from -6 to 6
- norm_gain: float32 [512], P('chan'), may hold values from 0.1 to 1.9
- skip_weight: float32 [512], P('chan'), may hold values from -4 to 4
- spectrum: float32 [2, 128, 512, 512], P(None, 'seq', None, 'chan'), may hold values from -6 to 6
Outputs:
- gated_out: bfloat16 [32768, 512], P('seq', 'chan')
All inputs are finite; a program needn't handle non-finite values.
Results may differ from a plain program's by a relative error of at most 0.007.
Values may be sent and summed in bfloat16 or wider, within the bound.
A program may use at most 64 MiB of HBM per device.

v0:
```python
import math

import jax
import jax.numpy as jnp
from jax import lax
from jax.sharding import PartitionSpec as P

CHANNELS = 512


PRECISE = lax.Precision.HIGHEST
FULL_TURN = 2.0 * math.pi


def partner_2(value, axis, apart):
    mask = 2**apart
    pairs = [(source, source ^ mask) for source in range(lax.axis_size(axis))]
    return lax.ppermute(value, axis, pairs)


def traced_reverse(seq_index, levels):
    summed = jnp.zeros((), jnp.int32)
    for bit_pos in range(levels):
        summed = summed + (seq_index >> bit_pos & 1) * (1 << levels - 1 - bit_pos)
    return summed


def rotation(numerator, denominator):
    angle = (numerator % denominator).astype(jnp.float32) * (FULL_TURN / denominator)
    return (jnp.cos(angle), jnp.sin(angle))


def turn_by(pair_data, cos_angle, sin_angle, direction):
    real_part, imag_part = (pair_data[0], pair_data[1])
    return jnp.stack(
        [
            real_part * cos_angle + direction * imag_part * sin_angle,
            imag_part * cos_angle - direction * real_part * sin_angle,
        ]
    )


def dft_rows(pair_data, cos_table, sin_table, direction):
    cos_prod = jnp.einsum("tj,ubjc->ubtc", cos_table, pair_data, precision=PRECISE)
    sin_prod = jnp.einsum("tj,ubjc->ubtc", sin_table, pair_data, precision=PRECISE)
    return jnp.stack([cos_prod[0] + direction * sin_prod[1], cos_prod[1] - direction * sin_prod[0]])


def apply_filter(current, spectrum, cos_table, sin_table, cos_own, sin_own):
    spectral = dft_rows(current, cos_table, sin_table, 1.0)
    product = jnp.stack(
        [
            spectral[0] * spectrum[0] - spectral[1] * spectrum[1],
            spectral[0] * spectrum[1] + spectral[1] * spectrum[0],
        ]
    )
    restored = dft_rows(product, cos_table, sin_table, -1.0)
    return turn_by(restored, cos_own, sin_own, -1.0)


def local(features, pre_gate, post_gate, norm_gain, skip_weight, spectrum):
    tok_rows, chan_width = features.shape
    seq_count = lax.axis_size("seq")
    levels = seq_count.bit_length() - 1
    seq_place = lax.axis_index("seq")
    stride = 2 * seq_count
    all_bins = stride * tok_rows
    widened = features.astype(jnp.float32)
    squares = lax.psum(jnp.sum(widened * widened, axis=1), "chan")
    scaled = widened * lax.rsqrt(squares / CHANNELS + 1e-06)[:, None] * norm_gain
    signal = (scaled * pre_gate.astype(jnp.float32)).astype(jnp.bfloat16)
    series = jnp.arange(tok_rows, dtype=jnp.int32)
    cos_table, sin_table = rotation(series[:, None] * series[None, :], tok_rows)
    own_bins = 2 * traced_reverse(seq_place, levels) + jnp.arange(2, dtype=jnp.int32)
    cos_own, sin_own = rotation(own_bins[:, None] * series[None, :], all_bins)
    cos_own = cos_own[:, :, None]
    sin_own = sin_own[:, :, None]
    cos_place, sin_place = rotation(seq_place, stride)
    flattened = signal.astype(jnp.float32)
    blank_part = jnp.zeros_like(flattened)
    current = jnp.stack(
        [
            jnp.stack([flattened, flattened * cos_place]),
            jnp.stack([blank_part, -flattened * sin_place]),
        ]
    )
    for level in reversed(range(levels)):
        half_span = 1 << level
        partner = partner_2(current, "seq", level)
        upper_bit = seq_place // half_span % 2
        cos_section, sin_section = rotation(seq_place % half_span, 2 * half_span)
        summed = current + partner
        twisted = turn_by(partner - current, cos_section, sin_section, 1.0)
        current = jnp.where(upper_bit == 0, summed, twisted)
    current = turn_by(current, cos_own, sin_own, 1.0)
    current = apply_filter(current, spectrum, cos_table, sin_table, cos_own, sin_own)
    for level in range(levels):
        half_span = 1 << level
        partner = partner_2(current, "seq", level)
        upper_bit = seq_place // half_span % 2
        cos_section, sin_section = rotation(seq_place % half_span, 2 * half_span)
        own_term = turn_by(current, cos_section, sin_section, -1.0)
        their_term = turn_by(partner, cos_section, sin_section, -1.0)
        current = jnp.where(upper_bit == 0, current + their_term, partner - own_term)
    result = (current[0, 0] + cos_place * current[0, 1] - sin_place * current[1, 1]) / all_bins
    gated = post_gate.astype(jnp.float32) * (result + skip_weight * signal.astype(jnp.float32))
    return gated.astype(jnp.bfloat16)


def solution(mesh):
    return jax.shard_map(
        local,
        mesh=mesh,
        in_specs=(
            P("seq", "chan"),
            P("seq", "chan"),
            P("seq", "chan"),
            P("chan"),
            P("chan"),
            P(None, "seq", None, "chan"),
        ),
        out_specs=P("seq", "chan"),
        check_vma=False,
    )
```

profile of v0, /device:TPU:1, one launch (start us, length us, event | category | flops | bytes accessed | tf_op | source)
XLA Modules:
  0.0 407.1 jit_solution(12001557013403921074)
XLA Ops:
  1.2 9.3 %psum.7 = f32[512]{0:T(512)S(1)} all-reduce(f32[512]{0:T(512)S(1)} %fusion.24), channel_id=1, replica_groups=mesh['seq'=64,'chan'=4] {'chan'}, use_global_device_ids=true, to_apply=%region_1.0 | all-reduce | flops 512 | bytes 4096 | tf_op jit(solution)/shard_map/psum | solution.py:69
  11.6 7.0 %collective-permute-start = (f32[2,2,512,128]{2,3,1,0:T(8,128)S(1)}, f32[2,2,512,128]{2,3,1,0:T(8,128)S(1)}, u32[]{:S(2)}, u32[]{:S(2)}) collective-permute-start(f32[2,2,512,128]{2,3,1,0:T(8,128)S(1)} %pad_maximum_fusion), channel_id=1, source_target_pairs={{0,128},{4,132},{8,136},{12,140},{16,144},{20,148},{24,152},{28,15... | collective-permute-start | bytes 3145736 | tf_op jit(solution)/shard_map/ppermute | solution.py:18
  18.8 25.2 %collective-permute-done = f32[2,2,512,128]{2,3,1,0:T(8,128)S(1)} collective-permute-done((f32[2,2,512,128]{2,3,1,0:T(8,128)S(1)}, f32[2,2,512,128]{2,3,1,0:T(8,128)S(1)}, u32[]{:S(2)}, u32[]{:S(2)}) %collective-permute-start) | collective-permute-done | bytes 1048608 | tf_op jit(solution)/shard_map/ppermute | solution.py:18
  45.8 21.4 %collective-permute-start.1 = (f32[2,2,512,128]{2,3,1,0:T(8,128)}, f32[2,2,512,128]{2,3,1,0:T(8,128)}, u32[]{:S(2)}, u32[]{:S(2)}) collective-permute-start(f32[2,2,512,128]{2,3,1,0:T(8,128)} %maximum_select_fusion), channel_id=1, source_target_pairs={{0,64},{4,68},{8,72},{12,76},{16,80},{20,84},{24,88},{28,92},{32,9... | collective-permute-start | bytes 3145736 | tf_op jit(solution)/shard_map/ppermute | solution.py:18
  67.4 46.1 %collective-permute-done.1 = f32[2,2,512,128]{2,3,1,0:T(8,128)} collective-permute-done((f32[2,2,512,128]{2,3,1,0:T(8,128)}, f32[2,2,512,128]{2,3,1,0:T(8,128)}, u32[]{:S(2)}, u32[]{:S(2)}) %collective-permute-start.1) | collective-permute-done | bytes 1048608 | tf_op jit(solution)/shard_map/ppermute | solution.py:18
  116.5 1.8 maximum_select_fusion.1
  118.6 24.0 %collective-permute-done.2 = f32[2,2,512,128]{2,3,1,0:T(8,128)S(1)} collective-permute-done((f32[2,2,512,128]{2,3,1,0:T(8,128)S(1)}, f32[2,2,512,128]{2,3,1,0:T(8,128)S(1)}, u32[]{:S(2)}, u32[]{:S(2)}) %collective-permute-start.2) | collective-permute-done | bytes 1048608 | tf_op jit(solution)/shard_map/ppermute | solution.py:18
  143.3 3.0 collective-permute-start.3
  146.5 21.7 %collective-permute-done.3 = f32[2,2,512,128]{2,3,1,0:T(8,128)S(1)} collective-permute-done((f32[2,2,512,128]{2,3,1,0:T(8,128)S(1)}, f32[2,2,512,128]{2,3,1,0:T(8,128)S(1)}, u32[]{:S(2)}, u32[]{:S(2)}) %collective-permute-start.3) | collective-permute-done | bytes 1048608 | tf_op jit(solution)/shard_map/ppermute | solution.py:18
  170.5 20.9 %collective-permute-done.4 = f32[2,2,512,128]{2,3,1,0:T(8,128)S(1)} collective-permute-done((f32[2,2,512,128]{2,3,1,0:T(8,128)S(1)}, f32[2,2,512,128]{2,3,1,0:T(8,128)S(1)}, u32[]{:S(2)}, u32[]{:S(2)}) %collective-permute-start.4) | collective-permute-done | bytes 1048608 | tf_op jit(solution)/shard_map/ppermute | solution.py:18
  192.2 3.7 collective-permute-start.5
  200.3 5.7 %convolution_bitcast_fusion.3 = f32[2,2,512,128]{2,3,1,0:T(8,128)S(1)} fusion(f32[1,2,512,128]{2,3,1,0:T(8,128)S(1)} %get-tuple-element.13, f32[1,2,512,128]{2,3,1,0:T(8,128)S(1)} %get-tuple-element.12), kind=kOutput, calls=%fused_computation.6 | convolution fusion | flops 1614544896 | bytes 2097152 | tf_op jit(solution)/shard_map/tj,ubjc->ubtc/dot_general | solution.py:44
  206.0 5.9 %convolution_bitcast_fusion.2 = f32[2,2,512,128]{2,3,1,0:T(8,128)S(1)} fusion(f32[1,2,512,128]{2,3,1,0:T(8,128)S(1)} %get-tuple-element.13, f32[1,2,512,128]{2,3,1,0:T(8,128)S(1)} %get-tuple-element.12), kind=kOutput, calls=%fused_computation.5 | convolution fusion | flops 1614544896 | bytes 2097152 | tf_op jit(solution)/shard_map/tj,ubjc->ubtc/dot_general | solution.py:45
  212.3 5.7 %convolution_bitcast_fusion.1 = f32[2,2,512,128]{2,3,1,0:T(8,128)S(1)} fusion(f32[1,2,512,128]{2,3,1,0:T(8,128)S(1)} %get-tuple-element.11, f32[1,2,512,128]{2,3,1,0:T(8,128)S(1)} %get-tuple-element.10), kind=kOutput, calls=%fused_computation.4 | convolution fusion | flops 1614544896 | bytes 2097152 | tf_op jit(solution)/shard_map/tj,ubjc->ubtc/dot_general | solution.py:44
  217.9 5.9 %convolution_bitcast_fusion = f32[2,2,512,128]{2,3,1,0:T(8,128)S(1)} fusion(f32[1,2,512,128]{2,3,1,0:T(8,128)S(1)} %get-tuple-element.11, f32[1,2,512,128]{2,3,1,0:T(8,128)S(1)} %get-tuple-element.10), kind=kOutput, calls=%fused_computation.3 | convolution fusion | flops 1614544896 | bytes 2097152 | tf_op jit(solution)/shard_map/tj,ubjc->ubtc/dot_general | solution.py:45
  224.5 2.5 collective-permute-done.6
  231.3 22.1 %collective-permute-done.7 = f32[2,2,512,128]{2,3,1,0:T(8,128)S(1)} collective-permute-done((f32[2,2,512,128]{2,3,1,0:T(8,128)}, f32[2,2,512,128]{2,3,1,0:T(8,128)S(1)}, u32[]{:S(2)}, u32[]{:S(2)}) %collective-permute-start.7) | collective-permute-done | bytes 1048608 | tf_op jit(solution)/shard_map/ppermute | solution.py:18
  254.5 2.1 fusion.4
  256.6 3.0 collective-permute-start.8
  259.7 22.1 %collective-permute-done.8 = f32[2,2,512,128]{2,3,1,0:T(8,128)S(1)} collective-permute-done((f32[2,2,512,128]{2,3,1,0:T(8,128)S(1)}, f32[2,2,512,128]{2,3,1,0:T(8,128)S(1)}, u32[]{:S(2)}, u32[]{:S(2)}) %collective-permute-start.8) | collective-permute-done | bytes 1048608 | tf_op jit(solution)/shard_map/ppermute | solution.py:18
  283.4 22.0 %collective-permute-done.9 = f32[2,2,512,128]{2,3,1,0:T(8,128)S(1)} collective-permute-done((f32[2,2,512,128]{2,3,1,0:T(8,128)S(1)}, f32[2,2,512,128]{2,3,1,0:T(8,128)S(1)}, u32[]{:S(2)}, u32[]{:S(2)}) %collective-permute-start.9) | collective-permute-done | bytes 1048608 | tf_op jit(solution)/shard_map/ppermute | solution.py:18
  306.3 47.9 %collective-permute-done.10 = f32[2,2,512,128]{2,3,1,0:T(8,128)S(1)} collective-permute-done((f32[2,2,512,128]{2,3,1,0:T(8,128)S(1)}, f32[2,2,512,128]{2,3,1,0:T(8,128)S(1)}, u32[]{:S(2)}, u32[]{:S(2)}) %collective-permute-start.10) | collective-permute-done | bytes 1048608 | tf_op jit(solution)/shard_map/ppermute | solution.py:18
  354.8 1.9 collective-permute-start.11
  357.0 48.1 %collective-permute-done.11 = f32[2,2,512,128]{2,3,1,0:T(8,128)S(1)} collective-permute-done((f32[2,2,512,128]{2,3,1,0:T(8,128)S(1)}, f32[2,2,512,128]{2,3,1,0:T(8,128)S(1)}, u32[]{:S(2)}, u32[]{:S(2)}) %collective-permute-start.11) | collective-permute-done | bytes 1048608 | tf_op jit(solution)/shard_map/ppermute | solution.py:18
  (99 shorter events, 25.9 us)
Async XLA Ops:
  1.2 9.4 %copy-start.15 = (bf16[512,128]{1,0:T(8,128)(2,1)S(1)}, bf16[512,128]{1,0:T(8,128)(2,1)}, u32[]{:S(2)}) copy-start(bf16[512,128]{1,0:T(8,128)(2,1)} %param.7) | copy-start | bytes 393220
  11.6 32.4 %collective-permute-start = (f32[2,2,512,128]{2,3,1,0:T(8,128)S(1)}, f32[2,2,512,128]{2,3,1,0:T(8,128)S(1)}, u32[]{:S(2)}, u32[]{:S(2)}) collective-permute-start(f32[2,2,512,128]{2,3,1,0:T(8,128)S(1)} %pad_maximum_fusion), channel_id=1, source_target_pairs={{0,128},{4,132},{8,136},{12,140},{16,144},{20,148},{24,152},{28,15... | collective-permute-start | bytes 3145736 | tf_op jit(solution)/shard_map/ppermute | solution.py:18
  44.4 69.1 %copy-start = (f32[1,2,512,128]{2,3,1,0:T(8,128)}, f32[1,2,512,128]{2,3,1,0:T(8,128)S(1)}, u32[]{:S(2)}) copy-start(f32[1,2,512,128]{2,3,1,0:T(8,128)S(1)} %get-tuple-element.46) | copy-start | bytes 1572868
  44.4 69.1 %copy-start.2 = (f32[1,2,512,128]{2,3,1,0:T(8,128)}, f32[1,2,512,128]{2,3,1,0:T(8,128)S(1)}, u32[]{:S(2)}) copy-start(f32[1,2,512,128]{2,3,1,0:T(8,128)S(1)} %get-tuple-element.47) | copy-start | bytes 1572868
  45.8 67.8 %collective-permute-start.1 = (f32[2,2,512,128]{2,3,1,0:T(8,128)}, f32[2,2,512,128]{2,3,1,0:T(8,128)}, u32[]{:S(2)}, u32[]{:S(2)}) collective-permute-start(f32[2,2,512,128]{2,3,1,0:T(8,128)} %maximum_select_fusion), channel_id=1, source_target_pairs={{0,64},{4,68},{8,72},{12,76},{16,80},{20,84},{24,88},{28,92},{32,9... | collective-permute-start | bytes 3145736 | tf_op jit(solution)/shard_map/ppermute | solution.py:18
  118.3 24.3 %collective-permute-start.2 = (f32[2,2,512,128]{2,3,1,0:T(8,128)S(1)}, f32[2,2,512,128]{2,3,1,0:T(8,128)S(1)}, u32[]{:S(2)}, u32[]{:S(2)}) collective-permute-start(f32[2,2,512,128]{2,3,1,0:T(8,128)S(1)} %maximum_select_fusion.1), channel_id=1, source_target_pairs={{0,32},{4,36},{8,40},{12,44},{16,48},{20,52},{24,56},{28,60},{32,0... | collective-permute-start | bytes 3145736 | tf_op jit(solution)/shard_map/ppermute | solution.py:18
  143.3 24.9 %collective-permute-start.3 = (f32[2,2,512,128]{2,3,1,0:T(8,128)S(1)}, f32[2,2,512,128]{2,3,1,0:T(8,128)S(1)}, u32[]{:S(2)}, u32[]{:S(2)}) collective-permute-start(f32[2,2,512,128]{2,3,1,0:T(8,128)S(1)} %maximum_select_fusion.2), channel_id=1, source_target_pairs={{0,16},{4,20},{8,24},{12,28},{16,0},{20,4},{24,8},{28,12},{32,48},... | collective-permute-start | bytes 3145736 | tf_op jit(solution)/shard_map/ppermute | solution.py:18
  169.0 22.5 %collective-permute-start.4 = (f32[2,2,512,128]{2,3,1,0:T(8,128)S(1)}, f32[2,2,512,128]{2,3,1,0:T(8,128)S(1)}, u32[]{:S(2)}, u32[]{:S(2)}) collective-permute-start(f32[2,2,512,128]{2,3,1,0:T(8,128)S(1)} %maximum_select_fusion.3), channel_id=1, source_target_pairs={{0,8},{4,12},{8,0},{12,4},{16,24},{20,28},{24,16},{28,20},{32,40},... | collective-permute-start | bytes 3145736 | tf_op jit(solution)/shard_map/ppermute | solution.py:18
  192.2 7.2 %collective-permute-start.5 = (f32[2,2,512,128]{2,3,1,0:T(8,128)S(1)}, f32[2,2,512,128]{2,3,1,0:T(8,128)S(1)}, u32[]{:S(2)}, u32[]{:S(2)}) collective-permute-start(f32[2,2,512,128]{2,3,1,0:T(8,128)S(1)} %maximum_select_fusion.4), channel_id=1, source_target_pairs={{0,4},{4,0},{8,12},{12,8},{16,20},{20,16},{24,28},{28,24},{32,36},... | collective-permute-start | bytes 3145736 | tf_op jit(solution)/shard_map/ppermute | solution.py:18
  205.9 5.9 %copy-start.13 = (f32[1,2,512,128]{2,3,1,0:T(8,128)S(1)}, f32[1,2,512,128]{2,3,1,0:T(8,128)}, u32[]{:S(2)}) copy-start(f32[1,2,512,128]{2,3,1,0:T(8,128)} %copy.15) | copy-start | bytes 1572868
  205.9 5.9 %copy-start.14 = (f32[1,2,512,128]{2,3,1,0:T(8,128)S(1)}, f32[1,2,512,128]{2,3,1,0:T(8,128)}, u32[]{:S(2)}) copy-start(f32[1,2,512,128]{2,3,1,0:T(8,128)} %copy.16) | copy-start | bytes 1572868
  224.1 3.0 copy-start.4
  224.2 2.7 collective-permute-start.6
  224.4 2.7 copy-start.6
  228.6 24.8 %collective-permute-start.7 = (f32[2,2,512,128]{2,3,1,0:T(8,128)}, f32[2,2,512,128]{2,3,1,0:T(8,128)S(1)}, u32[]{:S(2)}, u32[]{:S(2)}) collective-permute-start(f32[2,2,512,128]{2,3,1,0:T(8,128)} %fusion.3), channel_id=1, source_target_pairs={{0,8},{4,12},{8,0},{12,4},{16,24},{20,28},{24,16},{28,20},{32,40},... | collective-permute-start | bytes 3145736 | tf_op jit(solution)/shard_map/ppermute | solution.py:18
  231.3 23.2 %copy-start.5 = (f32[1,2,512,128]{2,3,1,0:T(8,128)S(1)}, f32[1,2,512,128]{2,3,1,0:T(8,128)}, u32[]{:S(2)}) copy-start(f32[1,2,512,128]{2,3,1,0:T(8,128)} %copy-done.4) | copy-start | bytes 1572868
  231.3 23.1 %copy-start.7 = (f32[1,2,512,128]{2,3,1,0:T(8,128)S(1)}, f32[1,2,512,128]{2,3,1,0:T(8,128)}, u32[]{:S(2)}) copy-start(f32[1,2,512,128]{2,3,1,0:T(8,128)} %copy-done.6) | copy-start | bytes 1572868
  231.3 23.1 %copy-start.9 = (f32[1,2,512,128]{2,3,1,0:T(8,128)S(1)}, f32[1,2,512,128]{2,3,1,0:T(8,128)}, u32[]{:S(2)}) copy-start(f32[1,2,512,128]{2,3,1,0:T(8,128)} %copy-done.8) | copy-start | bytes 1572868
  231.3 23.1 %copy-start.11 = (f32[1,2,512,128]{2,3,1,0:T(8,128)S(1)}, f32[1,2,512,128]{2,3,1,0:T(8,128)}, u32[]{:S(2)}) copy-start(f32[1,2,512,128]{2,3,1,0:T(8,128)} %copy-done.10) | copy-start | bytes 1572868
  256.6 25.3 %collective-permute-start.8 = (f32[2,2,512,128]{2,3,1,0:T(8,128)S(1)}, f32[2,2,512,128]{2,3,1,0:T(8,128)S(1)}, u32[]{:S(2)}, u32[]{:S(2)}) collective-permute-start(f32[2,2,512,128]{2,3,1,0:T(8,128)S(1)} %fusion.4), channel_id=1, source_target_pairs={{0,16},{4,20},{8,24},{12,28},{16,0},{20,4},{24,8},{28,12},{32,48},... | collective-permute-start | bytes 3145736 | tf_op jit(solution)/shard_map/ppermute | solution.py:18
  282.5 22.9 %collective-permute-start.9 = (f32[2,2,512,128]{2,3,1,0:T(8,128)S(1)}, f32[2,2,512,128]{2,3,1,0:T(8,128)S(1)}, u32[]{:S(2)}, u32[]{:S(2)}) collective-permute-start(f32[2,2,512,128]{2,3,1,0:T(8,128)S(1)} %fusion.5), channel_id=1, source_target_pairs={{0,32},{4,36},{8,40},{12,44},{16,48},{20,52},{24,56},{28,60},{32,0... | collective-permute-start | bytes 3145736 | tf_op jit(solution)/shard_map/ppermute | solution.py:18
  306.1 48.1 %collective-permute-start.10 = (f32[2,2,512,128]{2,3,1,0:T(8,128)S(1)}, f32[2,2,512,128]{2,3,1,0:T(8,128)S(1)}, u32[]{:S(2)}, u32[]{:S(2)}) collective-permute-start(f32[2,2,512,128]{2,3,1,0:T(8,128)S(1)} %fusion.6), channel_id=1, source_target_pairs={{0,64},{4,68},{8,72},{12,76},{16,80},{20,84},{24,88},{28,92},{32,9... | collective-permute-start | bytes 3145736 | tf_op jit(solution)/shard_map/ppermute | solution.py:18
  354.3 2.4 copy-start.16
  354.8 50.3 %collective-permute-start.11 = (f32[2,2,512,128]{2,3,1,0:T(8,128)S(1)}, f32[2,2,512,128]{2,3,1,0:T(8,128)S(1)}, u32[]{:S(2)}, u32[]{:S(2)}) collective-permute-start(f32[2,2,512,128]{2,3,1,0:T(8,128)S(1)} %fusion.7), channel_id=1, source_target_pairs={{0,128},{4,132},{8,136},{12,140},{16,144},{20,148},{24,152},{28,15... | collective-permute-start | bytes 3145736 | tf_op jit(solution)/shard_map/ppermute | solution.py:18
  (7 other events, 7.6 us)
where the time goes:
time: 414 us; the launch traced here: 407 us
  waiting for transfers between devices  303 us (73%)
  starting transfers between devices  43.8 us (11%)
  matrix products  23.1 us (6%)
  other arithmetic  18.3 us (4%)
  blocking collectives  9.3 us (2%)
  local copies, waits for them, and re-layouts  7.88 us (2%)
    ppermute x12, waiting for transfers between devices, partner_2(): return lax.ppermute(value, axis, pairs)  303 us
    ppermute x12, starting transfers between devices, partner_2(): return lax.ppermute(value, axis, pairs)  43.8 us
    dot_general x2, matrix products, dft_rows(): jnp.einsum('tj,ubjc->ubtc', sin_table, pair_data, precision=PRECISE)  11.8 us
    dot_general x2, matrix products, dft_rows(): jnp.einsum('tj,ubjc->ubtc', cos_table, pair_data, precision=PRECISE)  11.3 us
    psum x1, blocking collectives, local(): squares = lax.psum(jnp.sum(widened * widened, axis=1), 'chan')  9.3 us
  transfers between devices with their start and end apart: 12, of which 11 were waited for; matrix products, arithmetic and copies ran while one was open for 1% of the time, Pallas kernels for 0%

commit v1 on v0

v1 whole, which is shorter than its diff:
```python
import math

import jax
import jax.numpy as jnp
import numpy as np
from jax import lax
from jax.sharding import PartitionSpec as P

CHANNELS = 512
ROW_GROUP = 4


PRECISE = lax.Precision.HIGHEST
FULL_TURN = 2.0 * math.pi


def reversed_digits(count):
    levels = count.bit_length() - 1
    positions = np.arange(count)
    result = np.zeros(count, np.int64)
    for bit_pos in range(levels):
        result = result + ((positions >> bit_pos & 1) << levels - 1 - bit_pos)
    return result


def rotation(numerator, denominator):
    angle = (numerator % denominator).astype(jnp.float32) * (FULL_TURN / denominator)
    return (jnp.cos(angle), jnp.sin(angle))


def mm(spec, left, right):
    return jnp.einsum(spec, left, right, precision=PRECISE, preferred_element_type=jnp.float32)


def local(features, pre_gate, post_gate, norm_gain, skip_weight, spectrum):
    tok_rows, chan_width = features.shape
    seq_count = lax.axis_size("seq")
    stride = 2 * seq_count
    all_bins = stride * tok_rows
    group = chan_width // seq_count
    first_len = stride * ROW_GROUP
    second_len = all_bins // first_len
    half_first = first_len // 2

    spec_rows = spectrum.reshape(2, 2, second_len, ROW_GROUP, chan_width)
    spec_rows = jnp.transpose(spec_rows, (4, 0, 1, 3, 2))
    spec_chan = lax.all_to_all(spec_rows, "seq", 0, 2, tiled=True)
    spec_chan = spec_chan.reshape(group, 2, first_len, second_len)

    widened = features.astype(jnp.float32)
    squares = lax.psum(jnp.sum(widened * widened, axis=1), "chan")
    scaled = widened * lax.rsqrt(squares / CHANNELS + 1e-06)[:, None] * norm_gain
    signal = (scaled * pre_gate.astype(jnp.float32)).astype(jnp.bfloat16)

    sig_chan = lax.all_to_all(signal.T, "seq", 0, 1, tiled=True)
    sig_chan = sig_chan.astype(jnp.float32).reshape(group, half_first, second_len)

    digit_order = reversed_digits(seq_count)
    slots = np.arange(stride)
    low_bins = 2 * digit_order[slots // 2] + slots % 2
    row_bins = (low_bins[:, None] + stride * np.arange(ROW_GROUP)[None, :]).reshape(-1)
    row_bins = jnp.asarray(row_bins.astype(np.int32))

    first_in = jnp.arange(half_first, dtype=jnp.int32)
    cos_first, sin_first = rotation(row_bins[:, None] * first_in[None, :], first_len)
    second_in = jnp.arange(second_len, dtype=jnp.int32)
    cos_twist, sin_twist = rotation(row_bins[:, None] * second_in[None, :], all_bins)
    cos_second, sin_second = rotation(second_in[:, None] * second_in[None, :], second_len)

    part_re = mm("rn,cnm->crm", cos_first, sig_chan)
    part_im = -mm("rn,cnm->crm", sin_first, sig_chan)
    twist_re = part_re * cos_twist + part_im * sin_twist
    twist_im = part_im * cos_twist - part_re * sin_twist
    freq_re = mm("crn,nk->crk", twist_re, cos_second) + mm("crn,nk->crk", twist_im, sin_second)
    freq_im = mm("crn,nk->crk", twist_im, cos_second) - mm("crn,nk->crk", twist_re, sin_second)

    filt_re = spec_chan[:, 0]
    filt_im = spec_chan[:, 1]
    prod_re = freq_re * filt_re - freq_im * filt_im
    prod_im = freq_re * filt_im + freq_im * filt_re

    back_re = mm("crk,kn->crn", prod_re, cos_second) - mm("crk,kn->crn", prod_im, sin_second)
    back_im = mm("crk,kn->crn", prod_im, cos_second) + mm("crk,kn->crn", prod_re, sin_second)
    untwist_re = back_re * cos_twist - back_im * sin_twist
    untwist_im = back_im * cos_twist + back_re * sin_twist
    conv = mm("rn,crm->cnm", cos_first, untwist_re) - mm("rn,crm->cnm", sin_first, untwist_im)
    conv = (conv * (1.0 / all_bins)).reshape(group, seq_count * tok_rows)

    result = lax.all_to_all(conv, "seq", 1, 0, tiled=True).T
    gated = post_gate.astype(jnp.float32) * (result + skip_weight * signal.astype(jnp.float32))
    return gated.astype(jnp.bfloat16)


def solution(mesh):
    return jax.shard_map(
        local,
        mesh=mesh,
        in_specs=(
            P("seq", "chan"),
            P("seq", "chan"),
            P("seq", "chan"),
            P("chan"),
            P("chan"),
            P(None, "seq", None, "chan"),
        ),
        out_specs=P("seq", "chan"),
        check_vma=False,
    )
```

time: 414 us -> 105 us (0.25); the launches traced: 407 us -> 104 us
  waiting for transfers between devices: 303 us -> 38.9 us
  starting transfers between devices: 43.8 us -> 25.4 us
  other arithmetic: 18.3 us -> 1.99 us
    ppermute x12 -> x0, waiting for transfers between devices: 303 us -> none  [partner_2(): return lax.ppermute(value, axis, pairs)]
    ppermute x12 -> x0, starting transfers between devices: 43.8 us -> none  [partner_2(): return lax.ppermute(value, axis, pairs)]
    all_to_all x0 -> x3, waiting for transfers between devices: none -> 38.9 us  [the longest x1 16.1 us: local(): spec_chan = lax.all_to_all(spec_rows, 'seq', 0, 2, tiled=True)]
    all_to_all x0 -> x3, starting transfers between devices: none -> 25.4 us  [the longest x1 14.3 us: local(): sig_chan = lax.all_to_all(signal.T, 'seq', 0, 1, tiled=True)]
    select_n x12 -> x0, other arithmetic: 10.2 us -> none  [the longest x6 5.58 us: local(): jnp.where(upper_bit == 0, current + their_term, partner - own_term)]
    dot_general x4 -> x12, matrix products: 23.1 us -> 21 us  [mm(): jnp.einsum(spec, left, right, precision=PRECISE, preferred_element_type=j...]
  transfers between devices with their start and end apart: 12 -> 3, of which waited for: 11 -> 3; matrix products, arithmetic and copies ran while one was open for 1% -> 13% of each run, Pallas kernels for 0% -> 0%
where the time goes in v1:
time: 105 us; the launch traced here: 104 us
  waiting for transfers between devices  38.9 us (37%)
  starting transfers between devices  25.4 us (24%)
  matrix products  21 us (20%)
  blocking collectives  9.3 us (9%)
  local copies, waits for them, and re-layouts  7.36 us (7%)
  other arithmetic  1.99 us (2%)
    dot_general x12, matrix products, mm(): jnp.einsum(spec, left, right, precision=PRECISE, preferred_element_type=j...  21 us
    all_to_all x1, waiting for transfers between devices, local(): spec_chan = lax.all_to_all(spec_rows, 'seq', 0, 2, tiled=True)  16.1 us
    all_to_all x1, starting transfers between devices, local(): sig_chan = lax.all_to_all(signal.T, 'seq', 0, 1, tiled=True)  14.3 us
    all_to_all x1, waiting for transfers between devices, local(): result = lax.all_to_all(conv, 'seq', 1, 0, tiled=True).T  13 us
    all_to_all x1, waiting for transfers between devices, local(): sig_chan = lax.all_to_all(signal.T, 'seq', 0, 1, tiled=True)  9.77 us
    psum x1, blocking collectives, local(): squares = lax.psum(jnp.sum(widened * widened, axis=1), 'chan')  9.3 us
    all_to_all x1, starting transfers between devices, local(): result = lax.all_to_all(conv, 'seq', 1, 0, tiled=True).T  6.55 us
    all_to_all x1, starting transfers between devices, local(): spec_chan = lax.all_to_all(spec_rows, 'seq', 0, 2, tiled=True)  4.48 us
  transfers between devices with their start and end apart: 3, of which 3 were waited for; matrix products, arithmetic and copies ran while one was open for 13% of the time, Pallas kernels for 0%

profile of v1, /device:TPU:1, one launch (start us, length us, event | category | flops | bytes accessed | tf_op | source)
XLA Modules:
  0.0 104.2 jit_solution(3268081029509111856)
XLA Ops:
  0.0 1.1 %copy.75 = bf16[512,128]{0,1:T(8,128)(2,1)S(1)} copy(bf16[512,128]{1,0:T(8,128)(2,1)} %param.8) | data formatting | bytes 262144 | tf_op args[1]
  1.3 9.3 %psum.7 = f32[512]{0:T(512)S(1)} all-reduce(f32[512]{0:T(512)S(1)} %fusion.20), channel_id=1, replica_groups=mesh['seq'=64,'chan'=4] {'chan'}, use_global_device_ids=true, to_apply=%region_1.0 | all-reduce | flops 512 | bytes 4096 | tf_op jit(solution)/shard_map/psum | solution.py:51
  12.1 14.3 %all-to-all-start = ((bf16[64,2,512]{2,1,0:T(2,128)(2,1)}), bf16[64,2,512]{2,1,0:T(2,128)(2,1)S(1)}, u32[]{:S(2)}, u32[]{:S(2)}) async-start(bf16[64,2,512]{2,1,0:T(2,128)(2,1)} %all_to_all.37), calls=%async_computation | async-start | bytes 262144 | tf_op jit(solution)/shard_map/all_to_all | solution.py:55
  26.4 1.3 %copy.81 = f32[128,2,2,4,128]{4,3,2,1,0:T(4,128)} copy(f32[128,2,2,4,128]{0,3,4,2,1:T(4,128)S(1)} %bitcast.73) | data formatting | bytes 2097152 | tf_op jit(solution)/shard_map/transpose | solution.py:46
  27.8 9.8 %all-to-all-done = bf16[64,2,512]{2,1,0:T(2,128)(2,1)S(1)} async-done(((bf16[64,2,512]{2,1,0:T(2,128)(2,1)}), bf16[64,2,512]{2,1,0:T(2,128)(2,1)S(1)}, u32[]{:S(2)}, u32[]{:S(2)}) %all-to-all-start) | async-done | bytes 131104 | tf_op jit(solution)/shard_map/all_to_all | solution.py:55
  37.5 4.5 %all-to-all-start.1 = ((f32[128,2,2,4,128]{4,3,2,1,0:T(4,128)}), f32[128,2,2,4,128]{4,3,2,1,0:T(4,128)S(1)}, u32[]{:S(2)}, u32[]{:S(2)}) async-start(f32[128,2,2,4,128]{4,3,2,1,0:T(4,128)} %copy.81), calls=%async_computation.1 | async-start | bytes 2097152 | tf_op jit(solution)/shard_map/all_to_all | solution.py:47
  42.0 1.0 fusion.43
  43.2 3.1 %fusion = f32[2,512,128]{1,2,0:T(8,128)S(1)} fusion(bf16[2,256,128]{2,1,0:T(8,128)(2,1)S(1)} %reshape.68, s32[512]{0:T(512)S(1)} %copy-done.4), kind=kOutput, calls=%fused_computation.1 | convolution fusion | flops 404619264 | bytes 657408 | tf_op jit(solution)/shard_map/rn,cnm->crm/dot_general | solution.py:32
  46.3 3.2 %convolution_bitcast_fusion = f32[2,512,128]{1,2,0:T(8,128)S(1)} fusion(bf16[2,256,128]{2,1,0:T(8,128)(2,1)S(1)} %reshape.68, s32[512]{0:T(512)S(1)} %copy-done.4), kind=kOutput, calls=%fused_computation.2 | convolution fusion | flops 404488192 | bytes 657408 | tf_op jit(solution)/shard_map/rn,cnm->crm/dot_general | solution.py:32
  49.5 1.2 %fusion.57 = f32[2,512,128]{2,1,0:T(8,128)S(1)} fusion(f32[2,512,128]{1,2,0:T(8,128)S(1)} %fusion, f32[2,512,128]{1,2,0:T(8,128)S(1)} %convolution_bitcast_fusion, f32[512,128]{0,1:T(8,128)S(1)} %get-tuple-element.8, f32[512,128]{0,1:T(8,128)S(1)} %get-tuple-element.7), kind=kOutput, calls=%fused_computation.78 | convolution fusion | flops 201949184 | bytes 2097152 | tf_op jit(solution)/shard_map/crn,nk->crk/dot_general | solution.py:32
  50.8 2.1 %fusion.55 = f32[2,512,128]{2,1,0:T(8,128)} fusion(f32[2,512,128]{1,2,0:T(8,128)S(1)} %convolution_bitcast_fusion, f32[2,512,128]{1,2,0:T(8,128)S(1)} %fusion, f32[512,128]{0,1:T(8,128)S(1)} %get-tuple-element.8, f32[512,128]{0,1:T(8,128)S(1)} %get-tuple-element.7), kind=kOutput, calls=%fused_computation.76 | convolution fusion | flops 201949184 | bytes 2097152 | tf_op jit(solution)/shard_map/crn,nk->crk/dot_general | solution.py:32
  52.8 1.2 %convolution_add_fusion.1 = f32[2,512,128]{2,1,0:T(8,128)S(1)} fusion(f32[2,512,128]{2,1,0:T(8,128)S(1)} %fusion.57, f32[2,512,128]{1,2,0:T(8,128)S(1)} %convolution_bitcast_fusion, f32[2,512,128]{1,2,0:T(8,128)S(1)} %fusion, f32[512,128]{0,1:T(8,128)S(1)} %get-tuple-element.8, f32[512,128]{0,1:T(8,128)S(1)} %get-tuple-element.7), kind=kOutput, calls=%fused_computation.6 | convolution fusion | flops 202080256 | bytes 2621440 | tf_op jit(solution)/shard_map/crn,nk->crk/dot_general | solution.py:32
  54.1 16.1 %all-to-all-done.1 = f32[128,2,2,4,128]{4,3,2,1,0:T(4,128)S(1)} async-done(((f32[128,2,2,4,128]{4,3,2,1,0:T(4,128)}), f32[128,2,2,4,128]{4,3,2,1,0:T(4,128)S(1)}, u32[]{:S(2)}, u32[]{:S(2)}) %all-to-all-start.1) | async-done | bytes 1048608 | tf_op jit(solution)/shard_map/all_to_all | solution.py:47
  71.6 1.2 %multiply_subtract_fusion = (f32[2,512,128]{2,1,0:T(8,128)S(1)}, f32[2,512,128]{2,1,0:T(8,128)S(1)}) fusion(f32[2,512,128]{2,1,0:T(8,128)S(1)} %convolution_add_fusion.1, f32[2,2,512,128]{3,2,0,1:T(8,128)S(1)} %bitcast.72, f32[2,512,128]{2,1,0:T(8,128)S(1)} %copy-done, f32[2,512,128]{1,2,0:T(8,128)S(1)} %fusion, ...), kind=kOutput, calls=%fused_computation.30 | convolution fusion | flops 202866688 | bytes 4718592 | tf_op jit(solution)/shard_map/crn,nk->crk/dot_general | solution.py:32
  72.8 0.9 fusion.51
  73.7 0.9 fusion.53
  74.6 0.9 convolution_add_fusion
  75.4 0.9 convolution_subtract_fusion
  76.3 2.8 %fusion.8 = f32[2,128,256]{2,1,0:T(8,128)S(1)} fusion(f32[2,512,128]{1,2,0:T(8,128)S(1)} %convolution_add_fusion, f32[2,512,128]{1,2,0:T(8,128)S(1)} %convolution_subtract_fusion, f32[512,128]{0,1:T(8,128)S(1)} %get-tuple-element.8, f32[512,128]{0,1:T(8,128)S(1)} %get-tuple-element.7, s32[512]{0:T(512)S(1)} %copy-done.4), kind=kOutput, calls=%fused_computation.20 | convolution fusion | flops 404881408 | bytes 1837056 | tf_op jit(solution)/shard_map/rn,crm->cnm/dot_general | solution.py:32
  79.2 2.6 %fusion.2 = f32[2,256,128]{1,2,0:T(8,128)S(1)} fusion(f32[2,128,256]{2,1,0:T(8,128)S(1)} %fusion.8, f32[2,512,128]{1,2,0:T(8,128)S(1)} %convolution_subtract_fusion, f32[2,512,128]{1,2,0:T(8,128)S(1)} %convolution_add_fusion, f32[512,128]{0,1:T(8,128)S(1)} %get-tuple-element.8, f32[512,128]{0,1:T(8,128)S(1)} %get-tuple-element.7, s32[512]{0:T(512)S(1)} %copy-done.4), kind=kOutput, calls=%fused_computation.9 | convolution fusion | flops 405012480 | bytes 2099200 | tf_op jit(solution)/shard_map/rn,crm->cnm/dot_general | solution.py:32
  81.9 0.9 copy.91
  82.9 6.5 %all-to-all-start.2 = ((f32[2,64,512]{2,0,1:T(2,128)}), f32[2,64,512]{2,0,1:T(2,128)S(1)}, u32[]{:S(2)}, u32[]{:S(2)}) async-start(f32[2,64,512]{2,0,1:T(2,128)} %copy.91), calls=%async_computation.2 | async-start | bytes 524288 | tf_op jit(solution)/shard_map/all_to_all | solution.py:89
  89.5 13.0 %all-to-all-done.2 = f32[2,64,512]{2,0,1:T(2,128)S(1)} async-done(((f32[2,64,512]{2,0,1:T(2,128)}), f32[2,64,512]{2,0,1:T(2,128)S(1)}, u32[]{:S(2)}, u32[]{:S(2)}) %all-to-all-start.2) | async-done | bytes 262176 | tf_op jit(solution)/shard_map/all_to_all | solution.py:89
  103.4 0.8 copy.92
  (28 shorter events, 4.2 us)
Async XLA Ops:
  0.0 1.1 %copy-start.2 = (bf16[512,128]{1,0:T(8,128)(2,1)S(1)}, bf16[512,128]{1,0:T(8,128)(2,1)}, u32[]{:S(2)}) copy-start(bf16[512,128]{1,0:T(8,128)(2,1)} %param.7) | copy-start | bytes 393220
  0.0 26.4 %copy-start.1 = (f32[2,2,512,128]{3,2,1,0:T(8,128)S(1)}, f32[2,2,512,128]{3,2,1,0:T(8,128)}, u32[]{:S(2)}) copy-start(f32[2,2,512,128]{3,2,1,0:T(8,128)} %param.12) | copy-start | bytes 3145732
  12.1 25.5 %all-to-all-start = ((bf16[64,2,512]{2,1,0:T(2,128)(2,1)}), bf16[64,2,512]{2,1,0:T(2,128)(2,1)S(1)}, u32[]{:S(2)}, u32[]{:S(2)}) async-start(bf16[64,2,512]{2,1,0:T(2,128)(2,1)} %all_to_all.37), calls=%async_computation | async-start | bytes 262144 | tf_op jit(solution)/shard_map/all_to_all | solution.py:55
  27.8 14.3 %copy-start.4 = (s32[512]{0:T(512)S(1)}, s32[512]{0:T(512)}, u32[]{:S(2)}) copy-start(s32[512]{0:T(512)} %constant.60.clone) | copy-start | bytes 6148
  37.5 32.6 %all-to-all-start.1 = ((f32[128,2,2,4,128]{4,3,2,1,0:T(4,128)}), f32[128,2,2,4,128]{4,3,2,1,0:T(4,128)S(1)}, u32[]{:S(2)}, u32[]{:S(2)}) async-start(f32[128,2,2,4,128]{4,3,2,1,0:T(4,128)} %copy.81), calls=%async_computation.1 | async-start | bytes 2097152 | tf_op jit(solution)/shard_map/all_to_all | solution.py:47
  70.5 1.0 %copy-start = (f32[2,512,128]{2,1,0:T(8,128)S(1)}, f32[2,512,128]{2,1,0:T(8,128)}, u32[]{:S(2)}) copy-start(f32[2,512,128]{2,1,0:T(8,128)} %fusion.55) | copy-start | bytes 1572868
  82.9 6.6 %copy-start.3 = (bf16[512,128]{1,0:T(8,128)(2,1)S(1)}, bf16[512,128]{1,0:T(8,128)(2,1)}, u32[]{:S(2)}) copy-start(bf16[512,128]{1,0:T(8,128)(2,1)} %param.9) | copy-start | bytes 393220
  82.9 19.7 %all-to-all-start.2 = ((f32[2,64,512]{2,0,1:T(2,128)}), f32[2,64,512]{2,0,1:T(2,128)S(1)}, u32[]{:S(2)}, u32[]{:S(2)}) async-start(f32[2,64,512]{2,0,1:T(2,128)} %copy.91), calls=%async_computation.2 | async-start | bytes 524288 | tf_op jit(solution)/shard_map/all_to_all | solution.py:89
  102.6 0.7 copy-start.5
  102.6 0.7 copy-start.6

commit v2 on v1

--- a/solution.py
+++ b/solution.py
@@ -4,6 +4,8 @@
 import jax.numpy as jnp
 import numpy as np
 from jax import lax
+from jax.experimental import pallas as pl
+from jax.experimental.pallas import tpu as pltpu
 from jax.sharding import PartitionSpec as P
 
 CHANNELS = 512
@@ -32,6 +34,65 @@
     return jnp.einsum(spec, left, right, precision=PRECISE, preferred_element_type=jnp.float32)
 
 
+def exchange_kernel(src_ref, dst_ref, send_sem, recv_sem, local_sem):
+    count = src_ref.shape[0]
+    me = lax.axis_index("seq")
+    mesh_ids = pl.DeviceIdType.MESH
+    barrier = pltpu.get_barrier_semaphore()
+
+    def greet(step, carry):
+        peer = lax.rem(me + step, count)
+        pl.semaphore_signal(barrier, inc=1, device_id={"seq": peer}, device_id_type=mesh_ids)
+        return carry
+
+    lax.fori_loop(1, count, greet, 0)
+    pl.semaphore_wait(barrier, count - 1)
+    own = pltpu.make_async_copy(src_ref.at[me], dst_ref.at[me], local_sem)
+    own.start()
+
+    def remote(step):
+        peer = lax.rem(me + step, count)
+        return pltpu.make_async_remote_copy(
+            src_ref.at[peer],
+            dst_ref.at[me],
+            send_sem.at[step],
+            recv_sem.at[step],
+            device_id={"seq": peer},
+            device_id_type=mesh_ids,
+        )
+
+    def send(step, carry):
+        remote(step).start()
+        return carry
+
+    lax.fori_loop(1, count, send, 0)
+
+    def finish(step, carry):
+        copy = remote(step)
+        copy.wait_send()
+        copy.wait_recv()
+        return carry
+
+    lax.fori_loop(1, count, finish, 0)
+    own.wait()
+
+
+def exchange(blocks, tag):
+    count = blocks.shape[0]
+    return pl.pallas_call(
+        exchange_kernel,
+        out_shape=jax.ShapeDtypeStruct(blocks.shape, blocks.dtype),
+        in_specs=[pl.BlockSpec(memory_space=pl.ANY)],
+        out_specs=pl.BlockSpec(memory_space=pl.ANY),
+        scratch_shapes=[
+            pltpu.SemaphoreType.DMA((count,)),
+            pltpu.SemaphoreType.DMA((count,)),
+            pltpu.SemaphoreType.DMA,
+        ],
+        compiler_params=pltpu.CompilerParams(collective_id=tag, has_side_effects=True),
+    )(blocks)
+
+
 def local(features, pre_gate, post_gate, norm_gain, skip_weight, spectrum):
     tok_rows, chan_width = features.shape
     seq_count = lax.axis_size("seq")
@@ -42,18 +103,20 @@
     second_len = all_bins // first_len
     half_first = first_len // 2
 
-    spec_rows = spectrum.reshape(2, 2, second_len, ROW_GROUP, chan_width)
-    spec_rows = jnp.transpose(spec_rows, (4, 0, 1, 3, 2))
-    spec_chan = lax.all_to_all(spec_rows, "seq", 0, 2, tiled=True)
-    spec_chan = spec_chan.reshape(group, 2, first_len, second_len)
+    spec_rows = spectrum.reshape(2, 2, second_len, ROW_GROUP, seq_count, group)
+    spec_rows = jnp.transpose(spec_rows, (4, 5, 0, 1, 3, 2)).reshape(seq_count, -1, 128)
+    spec_chan = exchange(spec_rows, 0).reshape(seq_count, group, 2, 2, ROW_GROUP, second_len)
+    spec_chan = jnp.transpose(spec_chan, (1, 2, 0, 3, 4, 5)).reshape(group, 2, first_len, second_len)
 
     widened = features.astype(jnp.float32)
     squares = lax.psum(jnp.sum(widened * widened, axis=1), "chan")
     scaled = widened * lax.rsqrt(squares / CHANNELS + 1e-06)[:, None] * norm_gain
     signal = (scaled * pre_gate.astype(jnp.float32)).astype(jnp.bfloat16)
 
-    sig_chan = lax.all_to_all(signal.T, "seq", 0, 1, tiled=True)
-    sig_chan = sig_chan.astype(jnp.float32).reshape(group, half_first, second_len)
+    sig_rows = signal.astype(jnp.float32).reshape(tok_rows, seq_count, group)
+    sig_rows = jnp.transpose(sig_rows, (1, 2, 0)).reshape(seq_count, -1, 128)
+    sig_chan = exchange(sig_rows, 1).reshape(seq_count, group, tok_rows)
+    sig_chan = jnp.transpose(sig_chan, (1, 0, 2)).reshape(group, half_first, second_len)
 
     digit_order = reversed_digits(seq_count)
     slots = np.arange(stride)
@@ -84,9 +147,10 @@
     untwist_re = back_re * cos_twist - back_im * sin_twist
     untwist_im = back_im * cos_twist + back_re * sin_twist
     conv = mm("rn,crm->cnm", cos_first, untwist_re) - mm("rn,crm->cnm", sin_first, untwist_im)
-    conv = (conv * (1.0 / all_bins)).reshape(group, seq_count * tok_rows)
-
-    result = lax.all_to_all(conv, "seq", 1, 0, tiled=True).T
+    conv = (conv * (1.0 / all_bins)).reshape(group, seq_count, tok_rows)
+    conv = jnp.transpose(conv, (1, 0, 2)).reshape(seq_count, -1, 128)
+    result = exchange(conv, 2).reshape(seq_count, group, tok_rows)
+    result = jnp.transpose(result, (2, 0, 1)).reshape(tok_rows, chan_width)
     gated = post_gate.astype(jnp.float32) * (result + skip_weight * signal.astype(jnp.float32))
     return gated.astype(jnp.bfloat16)
 

time: 105 us -> 171 us (1.63)
  Pallas kernels: 0 us -> 71.5 us
  local copies, waits for them, and re-layouts: 7.36 us -> 65 us
  waiting for transfers between devices: 38.9 us -> 0 us
  starting transfers between devices: 25.4 us -> 0 us
    pallas_call x0 -> x3, Pallas kernels: none -> 71.5 us  [exchange(): pl.pallas_call(exchange_kernel, out_shape=jax.ShapeDtypeStruct(blocks.sha...]
    reshape x1 -> x10, local copies, waits for them, and re-layouts: 0.09 us -> 40.4 us  [the longest x1 36 us: local(): spec_rows = spectrum.reshape(2, 2, second_len, ROW_GROUP, seq_count, group)]
    all_to_all x3 -> x0, waiting for transfers between devices: 38.9 us -> none  [the longest x1 16.1 us: local(): spec_chan = lax.all_to_all(spec_rows, 'seq', 0, 2, tiled=True)]
    all_to_all x3 -> x0, starting transfers between devices: 25.4 us -> none  [the longest x1 14.3 us: local(): sig_chan = lax.all_to_all(signal.T, 'seq', 0, 1, tiled=True)]
    transpose x1 -> x3, local copies, waits for them, and re-layouts: 1.34 us -> 20 us  [the longest x1 18.4 us: local(): jnp.transpose(spec_rows, (4, 5, 0, 1, 3, 2)).reshape(seq_count, -1, 128)]
    all_to_all x7 -> x0, local copies, waits for them, and re-layouts: 2.87 us -> none  [the longest x3 1.12 us: local(): result = lax.all_to_all(conv, 'seq', 1, 0, tiled=True).T]
    unnamed x17 -> x10, local copies, waits for them, and re-layouts: 2.18 us -> 3.69 us
  transfers between devices with their start and end apart: 3 -> 0, of which waited for: 3 -> 0; matrix products, arithmetic and copies ran while one was open for 13% -> 0% of each run, Pallas kernels for 0% -> 0%
where the time goes in v2:
time: 171 us; the launch traced here: 170 us
  Pallas kernels  71.5 us (42%)
  local copies, waits for them, and re-layouts  65 us (38%)
  matrix products  21.7 us (13%)
  blocking collectives  9.3 us (5%)
  other arithmetic  2.64 us (2%)
    pallas_call x3, Pallas kernels, exchange(): pl.pallas_call(exchange_kernel, out_shape=jax.ShapeDtypeStruct(blocks.sha...  71.5 us
    reshape x1, local copies, waits for them, and re-layouts, local(): spec_rows = spectrum.reshape(2, 2, second_len, ROW_GROUP, seq_count, group)  36 us
    dot_general x12, matrix products, mm(): jnp.einsum(spec, left, right, precision=PRECISE, preferred_element_type=j...  21.7 us
    transpose x1, local copies, waits for them, and re-layouts, local(): jnp.transpose(spec_rows, (4, 5, 0, 1, 3, 2)).reshape(seq_count, -1, 128)  18.4 us
    psum x1, blocking collectives, local(): squares = lax.psum(jnp.sum(widened * widened, axis=1), 'chan')  9.3 us
    unnamed x10, local copies, waits for them, and re-layouts  3.69 us

profile of v2, /device:TPU:1, one launch (start us, length us, event | category | flops | bytes accessed | tf_op | source)
XLA Modules:
  0.0 170.4 jit_solution(7877043813492416073)
XLA Ops:
  0.0 1.0 copy.22
  1.0 1.0 copy.21
  2.1 9.3 %psum.7 = f32[512]{0:T(512)S(1)} all-reduce(f32[512]{0:T(512)S(1)} %fusion.20), channel_id=1, replica_groups=mesh['seq'=64,'chan'=4] {'chan'}, use_global_device_ids=true, to_apply=%region_1.0 | all-reduce | flops 512 | bytes 4096 | tf_op jit(solution)/shard_map/psum | solution.py:112
  12.3 0.9 reshape.86.src_ref
  13.2 21.9 %shard_map.73 = f32[64,8,128]{2,1,0:T(8,128)} custom-call(f32[64,8,128]{2,1,0:T(8,128)} %reshape.86.src_ref), custom_call_target="tpu_custom_call" | custom-call | tf_op jit(solution)/shard_map/pallas_call | solution.py:82
  35.1 1.1 reshape.87
  36.3 4.1 %fusion = f32[2,512,128]{1,2,0:T(8,128)S(1)} fusion(f32[2,256,128]{2,1,0:T(8,128)S(1)} %reshape.88, s32[512]{0:T(512)} %constant.60.clone), kind=kOutput, calls=%fused_computation.1 | convolution fusion | flops 404619264 | bytes 788480 | tf_op jit(solution)/shard_map/rn,cnm->crm/dot_general | solution.py:34
  40.4 4.0 %convolution_bitcast_fusion = f32[2,512,128]{1,2,0:T(8,128)S(1)} fusion(f32[2,256,128]{2,1,0:T(8,128)S(1)} %reshape.88, s32[512]{0:T(512)} %constant.60.clone), kind=kOutput, calls=%fused_computation.2 | convolution fusion | flops 404488192 | bytes 788480 | tf_op jit(solution)/shard_map/rn,cnm->crm/dot_general | solution.py:34
  44.4 1.7 %fusion.42 = (f32[512,128]{0,1:T(8,128)S(1)}, f32[512,128]{0,1:T(8,128)S(1)}) fusion(s32[512]{0:T(512)} %constant.60.clone), kind=kLoop, calls=%fused_computation.61 | loop fusion | flops 917504 | bytes 526336 | tf_op jit(solution)/shard_map/cos | solution.py:30
  46.1 1.2 fusion.56
  47.4 1.2 convolution_add_fusion.1
  48.6 1.6 copy.28
  50.2 36.0 %reshape.89 = f32[2,2,128,4,64,2]{3,2,5,4,1,0:T(8,128)} reshape(f32[2,2,512,128]{2,3,1,0:T(8,128)S(1)} %copy.28) | data formatting | bytes 2097152 | tf_op jit(solution)/shard_map/reshape | solution.py:106
  86.2 18.4 %copy.29 = f32[64,2,2,2,4,128]{5,4,3,2,1,0:T(4,128)} copy(f32[64,2,2,2,4,128]{4,5,1,0,3,2:T(8,128)} %bitcast.74) | data formatting | bytes 2097152 | tf_op jit(solution)/shard_map/transpose | solution.py:107
  104.6 31.7 %shard_map.74 = f32[64,32,128]{2,1,0:T(8,128)} custom-call(f32[64,32,128]{2,1,0:T(8,128)} %bitcast.75), custom_call_target="tpu_custom_call" | custom-call | tf_op jit(solution)/shard_map/pallas_call | solution.py:82
  136.3 1.4 copy.30
  137.7 1.2 fusion.54
  138.9 1.2 multiply_subtract_fusion
  141.9 0.9 fusion.52
  143.7 2.6 %fusion.8 = f32[2,128,256]{2,1,0:T(8,128)S(1)} fusion(f32[2,512,128]{1,2,0:T(8,128)S(1)} %convolution_add_fusion, f32[2,512,128]{1,2,0:T(8,128)S(1)} %convolution_subtract_fusion, f32[512,128]{0,1:T(8,128)S(1)} %get-tuple-element.8, f32[512,128]{0,1:T(8,128)S(1)} %get-tuple-element.7, s32[512]{0:T(512)S(1)} %copy-done.1), kind=kOutput, calls=%fused_computation.20 | convolution fusion | flops 404881408 | bytes 1837056 | tf_op jit(solution)/shard_map/rn,crm->cnm/dot_general | solution.py:34
  146.3 2.6 %fusion.2 = f32[2,256,128]{1,2,0:T(8,128)S(1)} fusion(f32[2,128,256]{2,1,0:T(8,128)S(1)} %fusion.8, f32[2,512,128]{1,2,0:T(8,128)S(1)} %convolution_subtract_fusion, f32[2,512,128]{1,2,0:T(8,128)S(1)} %convolution_add_fusion, f32[512,128]{0,1:T(8,128)S(1)} %get-tuple-element.8, f32[512,128]{0,1:T(8,128)S(1)} %get-tuple-element.7, s32[512]{0:T(512)S(1)} %copy-done.1), kind=kOutput, calls=%fused_computation.9 | convolution fusion | flops 405012480 | bytes 2099200 | tf_op jit(solution)/shard_map/rn,crm->cnm/dot_general | solution.py:34
  149.3 0.9 reshape.94.src_ref
  150.2 18.0 %shard_map.75 = f32[64,8,128]{2,1,0:T(8,128)} custom-call(f32[64,8,128]{2,1,0:T(8,128)} %reshape.94.src_ref), custom_call_target="tpu_custom_call" | custom-call | tf_op jit(solution)/shard_map/pallas_call | solution.py:82
  168.2 1.1 reshape.95
  (22 shorter events, 5.2 us)
Async XLA Ops:
  86.2 57.5 %copy-start.1 = (s32[512]{0:T(512)S(1)}, s32[512]{0:T(512)}, u32[]{:S(2)}) copy-start(s32[512]{0:T(512)} %constant.60.clone) | copy-start | bytes 6148
  86.2 83.3 %copy-start = (bf16[512,128]{1,0:T(8,128)(2,1)S(1)}, bf16[512,128]{1,0:T(8,128)(2,1)}, u32[]{:S(2)}) copy-start(bf16[512,128]{1,0:T(8,128)(2,1)} %param.9) | copy-start | bytes 393220
  86.2 83.4 %copy-start.2 = (f32[128]{0:T(128)S(1)}, f32[128]{0:T(128)}, u32[]{:S(2)}) copy-start(f32[128]{0:T(128)} %param.11) | copy-start | bytes 1540

commit v3 on v1

v3 whole, which is shorter than its diff:
```python
import math

import jax
import jax.numpy as jnp
import numpy as np
from jax import lax
from jax.experimental import pallas as pl
from jax.experimental.pallas import tpu as pltpu
from jax.sharding import PartitionSpec as P

CHANNELS = 512
ROW_GROUP = 4
HIGH_DIGIT = 8


PRECISE = lax.Precision.HIGHEST
FULL_TURN = 2.0 * math.pi


def reversed_digits(count):
    levels = count.bit_length() - 1
    positions = np.arange(count)
    result = np.zeros(count, np.int64)
    for bit_pos in range(levels):
        result = result + ((positions >> bit_pos & 1) << levels - 1 - bit_pos)
    return result


def rotation(numerator, denominator):
    angle = (numerator % denominator).astype(jnp.float32) * (FULL_TURN / denominator)
    return (jnp.cos(angle), jnp.sin(angle))


def mm(spec, left, right):
    return jnp.einsum(spec, left, right, precision=PRECISE, preferred_element_type=jnp.float32)


def exchange_kernel(src_ref, dst_ref, mid_ref, send_sem, recv_sem, own_sem):
    high, width = src_ref.shape[0], src_ref.shape[1]
    me = lax.axis_index("seq")
    top, low = me // width, me % width
    mesh_ids = pl.DeviceIdType.MESH
    barrier = pltpu.get_barrier_semaphore()
    for step in range(1, width):
        peer = top * width + lax.rem(low + step, width)
        pl.semaphore_signal(barrier, inc=1, device_id={"seq": peer}, device_id_type=mesh_ids)
    for step in range(1, high):
        peer = lax.rem(top + step, high) * width + low
        pl.semaphore_signal(barrier, inc=1, device_id={"seq": peer}, device_id_type=mesh_ids)
    pl.semaphore_wait(barrier, width + high - 2)

    own = pltpu.make_async_copy(src_ref.at[:, low], mid_ref.at[low], own_sem.at[0])
    own.start()

    def across(step):
        other = lax.rem(low + step, width)
        return pltpu.make_async_remote_copy(
            src_ref.at[:, other],
            mid_ref.at[low],
            send_sem.at[0, step],
            recv_sem.at[0, step],
            device_id={"seq": top * width + other},
            device_id_type=mesh_ids,
        )

    for step in range(1, width):
        across(step).start()
    for step in range(1, width):
        copy = across(step)
        copy.wait_send()
        copy.wait_recv()
    own.wait()

    own = pltpu.make_async_copy(mid_ref.at[:, top], dst_ref.at[top], own_sem.at[1])
    own.start()

    def along(step):
        other = lax.rem(top + step, high)
        return pltpu.make_async_remote_copy(
            mid_ref.at[:, other],
            dst_ref.at[top],
            send_sem.at[1, step],
            recv_sem.at[1, step],
            device_id={"seq": other * width + low},
            device_id_type=mesh_ids,
        )

    for step in range(1, high):
        along(step).start()
    for step in range(1, high):
        copy = along(step)
        copy.wait_send()
        copy.wait_recv()
    own.wait()


def exchange(blocks, tag):
    high, width = blocks.shape[0], blocks.shape[1]
    vmem = pl.BlockSpec(memory_space=pltpu.VMEM)
    return pl.pallas_call(
        exchange_kernel,
        out_shape=jax.ShapeDtypeStruct(blocks.shape, blocks.dtype),
        in_specs=[vmem],
        out_specs=vmem,
        scratch_shapes=[
            pltpu.VMEM((width, high) + blocks.shape[2:], blocks.dtype),
            pltpu.SemaphoreType.DMA((2, max(high, width))),
            pltpu.SemaphoreType.DMA((2, max(high, width))),
            pltpu.SemaphoreType.DMA((2,)),
        ],
        compiler_params=pltpu.CompilerParams(collective_id=tag, has_side_effects=True),
    )(blocks)


def local(features, pre_gate, post_gate, norm_gain, skip_weight, spectrum):
    tok_rows, chan_width = features.shape
    seq_count = lax.axis_size("seq")
    stride = 2 * seq_count
    all_bins = stride * tok_rows
    group = chan_width // seq_count
    first_len = stride * ROW_GROUP
    second_len = all_bins // first_len
    half_first = first_len // 2
    lanes = 128
    own_rows = first_len // seq_count
    tok_tiles = tok_rows // lanes
    high = HIGH_DIGIT
    width = seq_count // high

    spec_rows = spectrum.reshape(2, 2, second_len, ROW_GROUP, seq_count, group)
    spec_rows = jnp.transpose(spec_rows, (4, 0, 5, 1, 3, 2)).reshape(high, width, -1, lanes)
    spec_chan = exchange(spec_rows, 0).reshape(seq_count, 2, group, own_rows, second_len)
    filt_re = spec_chan[:, 0]
    filt_im = spec_chan[:, 1]

    widened = features.astype(jnp.float32)
    squares = lax.psum(jnp.sum(widened * widened, axis=1), "chan")
    scaled = widened * lax.rsqrt(squares / CHANNELS + 1e-06)[:, None] * norm_gain
    signal = (scaled * pre_gate.astype(jnp.float32)).astype(jnp.bfloat16)

    sig_rows = signal.astype(jnp.float32).reshape(tok_tiles, lanes, seq_count, group)
    sig_rows = jnp.transpose(sig_rows, (2, 3, 0, 1)).reshape(high, width, -1, lanes)
    sig_chan = exchange(sig_rows, 1).reshape(seq_count, group, tok_tiles, lanes)

    digit_order = reversed_digits(seq_count)
    slots = np.arange(stride)
    low_bins = 2 * digit_order[slots // 2] + slots % 2
    row_bins = (low_bins[:, None] + stride * np.arange(ROW_GROUP)[None, :]).reshape(-1)
    row_bins = jnp.asarray(row_bins.astype(np.int32))

    first_in = jnp.arange(half_first, dtype=jnp.int32)
    cos_first, sin_first = rotation(row_bins[:, None] * first_in[None, :], first_len)
    second_in = jnp.arange(second_len, dtype=jnp.int32)
    cos_twist, sin_twist = rotation(row_bins[:, None] * second_in[None, :], all_bins)
    cos_twist = cos_twist.reshape(seq_count, 1, own_rows, second_len)
    sin_twist = sin_twist.reshape(seq_count, 1, own_rows, second_len)
    cos_second, sin_second = rotation(second_in[:, None] * second_in[None, :], second_len)

    def rows_of(chan):
        block = sig_chan[:, chan].reshape(half_first, second_len)
        return (mm("rn,nm->rm", cos_first, block), -mm("rn,nm->rm", sin_first, block))

    firsts = [rows_of(chan) for chan in range(group)]
    part_re = jnp.stack([f[0].reshape(seq_count, own_rows, second_len) for f in firsts], axis=1)
    part_im = jnp.stack([f[1].reshape(seq_count, own_rows, second_len) for f in firsts], axis=1)
    twist_re = part_re * cos_twist + part_im * sin_twist
    twist_im = part_im * cos_twist - part_re * sin_twist
    freq_re = mm("scjn,nk->scjk", twist_re, cos_second) + mm("scjn,nk->scjk", twist_im, sin_second)
    freq_im = mm("scjn,nk->scjk", twist_im, cos_second) - mm("scjn,nk->scjk", twist_re, sin_second)

    prod_re = freq_re * filt_re - freq_im * filt_im
    prod_im = freq_re * filt_im + freq_im * filt_re

    back_re = mm("scjk,kn->scjn", prod_re, cos_second) - mm("scjk,kn->scjn", prod_im, sin_second)
    back_im = mm("scjk,kn->scjn", prod_im, cos_second) + mm("scjk,kn->scjn", prod_re, sin_second)
    untwist_re = back_re * cos_twist - back_im * sin_twist
    untwist_im = back_im * cos_twist + back_re * sin_twist

    def out_of(chan):
        w_re = untwist_re[:, chan].reshape(first_len, second_len)
        w_im = untwist_im[:, chan].reshape(first_len, second_len)
        block = mm("rn,rm->nm", cos_first, w_re) - mm("rn,rm->nm", sin_first, w_im)
        return block.reshape(seq_count, tok_tiles, lanes)

    conv = jnp.stack([out_of(chan) for chan in range(group)], axis=1) * (1.0 / all_bins)
    conv = conv.reshape(high, width, -1, lanes)
    result = exchange(conv, 2).reshape(seq_count, group, tok_tiles, lanes)
    result = jnp.transpose(result, (2, 3, 0, 1)).reshape(tok_rows, chan_width)
    gated = post_gate.astype(jnp.float32) * (result + skip_weight * signal.astype(jnp.float32))
    return gated.astype(jnp.bfloat16)


def solution(mesh):
    return jax.shard_map(
        local,
        mesh=mesh,
        in_specs=(
            P("seq", "chan"),
            P("seq", "chan"),
            P("seq", "chan"),
            P("chan"),
            P("chan"),
            P(None, "seq", None, "chan"),
        ),
        out_specs=P("seq", "chan"),
        check_vma=False,
    )
```

time: 105 us -> 199 us (1.90)
  Pallas kernels: 0 us -> 87.4 us
  local copies, waits for them, and re-layouts: 7.36 us -> 60.6 us
  waiting for transfers between devices: 38.9 us -> 0 us
  starting transfers between devices: 25.4 us -> 0 us
  matrix products: 21 us -> 35.8 us
  other arithmetic: 1.99 us -> 4.59 us
    pallas_call x0 -> x3, Pallas kernels: none -> 87.4 us  [exchange(): pl.pallas_call(exchange_kernel, out_shape=jax.ShapeDtypeStruct(blocks.sha...]
    all_to_all x3 -> x0, waiting for transfers between devices: 38.9 us -> none  [the longest x1 16.1 us: local(): spec_chan = lax.all_to_all(spec_rows, 'seq', 0, 2, tiled=True)]
    reshape x1 -> x2, local copies, waits for them, and re-layouts: 0.09 us -> 36.7 us  [the longest x1 36 us: local(): spec_rows = spectrum.reshape(2, 2, second_len, ROW_GROUP, seq_count, group)]
    all_to_all x3 -> x0, starting transfers between devices: 25.4 us -> none  [the longest x1 14.3 us: local(): sig_chan = lax.all_to_all(signal.T, 'seq', 0, 1, tiled=True)]
    transpose x1, local copies, waits for them, and re-layouts: 1.34 us -> 18.4 us  [local(): jnp.transpose(spec_rows, (4, 0, 5, 1, 3, 2)).reshape(high, width, -1, lanes)]
    dot_general x12 -> x16, matrix products: 21 us -> 35.8 us  [mm(): jnp.einsum(spec, left, right, precision=PRECISE, preferred_element_type=j...]
    all_to_all x7 -> x0, local copies, waits for them, and re-layouts: 2.87 us -> none  [the longest x3 1.12 us: local(): result = lax.all_to_all(conv, 'seq', 1, 0, tiled=True).T]
  transfers between devices with their start and end apart: 3 -> 0, of which waited for: 3 -> 0; matrix products, arithmetic and copies ran while one was open for 13% -> 0% of each run, Pallas kernels for 0% -> 0%
where the time goes in v3:
time: 199 us; the launch traced here: 198 us
  Pallas kernels  87.4 us (44%)
  local copies, waits for them, and re-layouts  60.6 us (30%)
  matrix products  35.8 us (18%)
  blocking collectives  9.3 us (5%)
  other arithmetic  4.59 us (2%)
    pallas_call x3, Pallas kernels, exchange(): pl.pallas_call(exchange_kernel, out_shape=jax.ShapeDtypeStruct(blocks.sha...  87.4 us
    reshape x1, local copies, waits for them, and re-layouts, local(): spec_rows = spectrum.reshape(2, 2, second_len, ROW_GROUP, seq_count, group)  36 us
    dot_general x16, matrix products, mm(): jnp.einsum(spec, left, right, precision=PRECISE, preferred_element_type=j...  35.8 us
    transpose x1, local copies, waits for them, and re-layouts, local(): jnp.transpose(spec_rows, (4, 0, 5, 1, 3, 2)).reshape(high, width, -1, lanes)  18.4 us
    psum x1, blocking collectives, local(): squares = lax.psum(jnp.sum(widened * widened, axis=1), 'chan')  9.3 us

profile of v3, /device:TPU:1, one launch (start us, length us, event | category | flops | bytes accessed | tf_op | source)
XLA Modules:
  0.0 197.9 jit_solution(11167433211629168259)
XLA Ops:
  0.0 1.0 copy.24
  1.1 9.3 %psum.7 = f32[512]{0:T(512)S(1)} all-reduce(f32[512]{0:T(512)S(1)} %fusion.28), channel_id=1, replica_groups=mesh['seq'=64,'chan'=4] {'chan'}, use_global_device_ids=true, to_apply=%region_1.0 | all-reduce | flops 512 | bytes 4096 | tf_op jit(solution)/shard_map/psum | solution.py:137
  10.4 1.0 copy.25
  12.9 24.2 %shard_map.73 = f32[8,8,8,128]{3,2,1,0:T(8,128)} custom-call(f32[8,8,8,128]{3,2,1,0:T(8,128)} %bitcast.114), custom_call_target="tpu_custom_call" | custom-call | tf_op jit(solution)/shard_map/pallas_call | solution.py:100
  37.1 1.0 fusion.143
  38.1 4.0 %convolution_bitcast_fusion = f32[64,1,8,128]{3,2,0,1:T(8,128)S(1)} fusion(f32[256,128,1]{1,0,2:T(8,128)S(1)} %bitcast.119, s32[64,8]{1,0:T(8,128)} %constant.64), kind=kOutput, calls=%fused_computation.8 | convolution fusion | flops 203161600 | bytes 395264 | tf_op jit(solution)/shard_map/rn,nm->rm/dot_general | solution.py:35
  42.2 4.0 %convolution_bitcast_fusion.1 = f32[64,1,8,128]{3,2,0,1:T(8,128)S(1)} fusion(f32[256,128,1]{1,0,2:T(8,128)S(1)} %bitcast.117, s32[64,8]{1,0:T(8,128)} %constant.64), kind=kOutput, calls=%fused_computation.9 | convolution fusion | flops 203161600 | bytes 395264 | tf_op jit(solution)/shard_map/rn,nm->rm/dot_general | solution.py:35
  46.2 4.1 %fusion = f32[64,1,8,128]{3,2,0,1:T(8,128)S(1)} fusion(f32[256,128]{1,0:T(8,128)S(1)} %bitcast.120, s32[512]{0:T(512)} %constant.62.clone), kind=kOutput, calls=%fused_computation.5 | convolution fusion | flops 203227136 | bytes 395264 | tf_op jit(solution)/shard_map/rn,nm->rm/dot_general | solution.py:35
  50.3 4.1 %fusion.1 = f32[64,1,8,128]{3,2,0,1:T(8,128)S(1)} fusion(f32[256,128]{1,0:T(8,128)S(1)} %bitcast.118, s32[512]{0:T(512)} %constant.62.clone), kind=kOutput, calls=%fused_computation.7 | convolution fusion | flops 203227136 | bytes 395264 | tf_op jit(solution)/shard_map/rn,nm->rm/dot_general | solution.py:35
  54.4 1.9 fusion.54
  57.2 0.8 convolution_add_fusion.1
  58.9 1.6 copy.28
  60.4 36.0 %reshape.157 = f32[2,2,128,4,64,2]{3,2,5,4,1,0:T(8,128)} reshape(f32[2,2,512,128]{2,3,1,0:T(8,128)S(1)} %copy.28) | data formatting | bytes 2097152 | tf_op jit(solution)/shard_map/reshape | solution.py:130
  96.4 18.4 %copy.29 = f32[64,2,2,2,4,128]{5,4,3,2,1,0:T(4,128)} copy(f32[64,2,2,2,4,128]{4,5,2,0,3,1:T(8,128)} %bitcast.109) | data formatting | bytes 2097152 | tf_op jit(solution)/shard_map/transpose | solution.py:131
  114.8 43.7 %shard_map.74 = f32[8,8,32,128]{3,2,1,0:T(8,128)} custom-call(f32[8,8,32,128]{3,2,1,0:T(8,128)} %bitcast.110), custom_call_target="tpu_custom_call" | custom-call | tf_op jit(solution)/shard_map/pallas_call | solution.py:100
  158.5 2.1 %multiply_subtract_fusion.1 = (f32[64,2,8,128]{3,2,1,0:T(8,128)S(1)}, f32[64,2,8,128]{3,2,1,0:T(8,128)S(1)}) fusion(f32[64,2,8,128]{3,2,1,0:T(8,128)S(1)} %convolution_add_fusion.1, f32[64,2,2,8,128]{4,3,2,1,0:T(8,128)} %bitcast.111, f32[64,2,8,128]{3,2,1,0:T(8,128)S(1)} %fusion.22, f32[64,2,8,128]{3,2,0,1:T(8,128)S(1)} %get-tuple-element.9), kind=kOutput, calls=%fused_computation.33 | convolution fusion | flops 202473472 | bytes 3670016 | tf_op jit(solution)/shard_map/scjn,nk->scjk/dot_general | solution.py:35
  161.4 0.8 convolution_add_fusion
  163.0 0.9 multiply_add_fusion
  163.9 2.9 %fusion.38 = f32[256,128]{1,0:T(8,128)S(1)} fusion(f32[64,2,8,128]{3,2,0,1:T(8,128)S(1)} %get-tuple-element.8, s32[512]{0:T(512)S(1)} %copy-done.2), kind=kOutput, calls=%fused_computation.74 | convolution fusion | flops 203161600 | bytes 395264 | tf_op jit(solution)/shard_map/rn,rm->nm/dot_general | solution.py:35
  166.8 2.9 %convolution_subtract_fusion.3 = f32[256,128]{1,0:T(8,128)S(1)} fusion(f32[256,128]{1,0:T(8,128)S(1)} %fusion.38, f32[64,2,8,128]{3,2,0,1:T(8,128)S(1)} %get-tuple-element.7, s32[512]{0:T(512)S(1)} %copy-done.2), kind=kOutput, calls=%fused_computation.11 | convolution fusion | flops 203194368 | bytes 526336 | tf_op jit(solution)/shard_map/rn,rm->nm/dot_general | solution.py:35
  169.7 3.1 %fusion.37 = f32[256,128]{1,0:T(8,128)S(1)} fusion(f32[64,2,8,128]{3,2,0,1:T(8,128)S(1)} %get-tuple-element.8, s32[512]{0:T(512)S(1)} %copy-done.2), kind=kOutput, calls=%fused_computation.71 | convolution fusion | flops 203161600 | bytes 395264 | tf_op jit(solution)/shard_map/rn,rm->nm/dot_general | solution.py:35
  172.8 2.9 %convolution_subtract_fusion.2 = f32[256,128]{1,0:T(8,128)S(1)} fusion(f32[256,128]{1,0:T(8,128)S(1)} %fusion.37, f32[64,2,8,128]{3,2,0,1:T(8,128)S(1)} %get-tuple-element.7, s32[512]{0:T(512)S(1)} %copy-done.2), kind=kOutput, calls=%fused_computation.10 | convolution fusion | flops 203194368 | bytes 526336 | tf_op jit(solution)/shard_map/rn,rm->nm/dot_general | solution.py:35
  176.4 19.5 %shard_map.75 = f32[8,8,8,128]{3,2,1,0:T(8,128)} custom-call(f32[8,8,8,128]{3,2,1,0:T(8,128)} %bitcast.113), custom_call_target="tpu_custom_call" | custom-call | tf_op jit(solution)/shard_map/pallas_call | solution.py:100
  196.1 1.1 fusion.36
  (18 shorter events, 6.6 us)
Async XLA Ops:
  60.4 103.5 %copy-start.2 = (s32[512]{0:T(512)S(1)}, s32[512]{0:T(512)}, u32[]{:S(2)}) copy-start(s32[512]{0:T(512)} %constant.62.clone) | copy-start | bytes 6148
  96.4 99.6 %copy-start = (bf16[512,128]{1,0:T(8,128)(2,1)S(1)}, bf16[512,128]{1,0:T(8,128)(2,1)}, u32[]{:S(2)}) copy-start(bf16[512,128]{1,0:T(8,128)(2,1)} %param.9) | copy-start | bytes 393220
  96.4 99.7 %copy-start.1 = (f32[128]{0:T(128)S(1)}, f32[128]{0:T(128)}, u32[]{:S(2)}) copy-start(f32[128]{0:T(128)} %param.11) | copy-start | bytes 1540

commit v4 on v2

--- a/solution.py
+++ b/solution.py
@@ -10,6 +10,7 @@
 
 CHANNELS = 512
 ROW_GROUP = 4
+HIGH_DIGIT = 8
 
 
 PRECISE = lax.Precision.HIGHEST
@@ -34,7 +35,7 @@
     return jnp.einsum(spec, left, right, precision=PRECISE, preferred_element_type=jnp.float32)
 
 
-def exchange_kernel(src_ref, dst_ref, send_sem, recv_sem, local_sem):
+def exchange_kernel(src_ref, dst_ref, send_sem, recv_sem, own_sem):
     count = src_ref.shape[0]
     me = lax.axis_index("seq")
     mesh_ids = pl.DeviceIdType.MESH
@@ -47,7 +48,7 @@
 
     lax.fori_loop(1, count, greet, 0)
     pl.semaphore_wait(barrier, count - 1)
-    own = pltpu.make_async_copy(src_ref.at[me], dst_ref.at[me], local_sem)
+    own = pltpu.make_async_copy(src_ref.at[me], dst_ref.at[me], own_sem)
     own.start()
 
     def remote(step):
@@ -79,11 +80,12 @@
 
 def exchange(blocks, tag):
     count = blocks.shape[0]
+    vmem = pl.BlockSpec(memory_space=pltpu.VMEM)
     return pl.pallas_call(
         exchange_kernel,
         out_shape=jax.ShapeDtypeStruct(blocks.shape, blocks.dtype),
-        in_specs=[pl.BlockSpec(memory_space=pl.ANY)],
-        out_specs=pl.BlockSpec(memory_space=pl.ANY),
+        in_specs=[vmem],
+        out_specs=vmem,
         scratch_shapes=[
             pltpu.SemaphoreType.DMA((count,)),
             pltpu.SemaphoreType.DMA((count,)),
@@ -102,21 +104,23 @@
     first_len = stride * ROW_GROUP
     second_len = all_bins // first_len
     half_first = first_len // 2
+    lanes = 128
+    tok_tiles = tok_rows // lanes
 
-    spec_rows = spectrum.reshape(2, 2, second_len, ROW_GROUP, seq_count, group)
-    spec_rows = jnp.transpose(spec_rows, (4, 5, 0, 1, 3, 2)).reshape(seq_count, -1, 128)
-    spec_chan = exchange(spec_rows, 0).reshape(seq_count, group, 2, 2, ROW_GROUP, second_len)
-    spec_chan = jnp.transpose(spec_chan, (1, 2, 0, 3, 4, 5)).reshape(group, 2, first_len, second_len)
+    spec_rows = spectrum.reshape(2, 2, second_len, ROW_GROUP, chan_width)
+    spec_rows = jnp.transpose(spec_rows, (4, 0, 1, 3, 2))
+    spec_chan = lax.all_to_all(spec_rows, "seq", 0, 2, tiled=True)
+    spec_chan = spec_chan.reshape(group, 2, first_len, second_len)
 
     widened = features.astype(jnp.float32)
     squares = lax.psum(jnp.sum(widened * widened, axis=1), "chan")
     scaled = widened * lax.rsqrt(squares / CHANNELS + 1e-06)[:, None] * norm_gain
     signal = (scaled * pre_gate.astype(jnp.float32)).astype(jnp.bfloat16)
 
-    sig_rows = signal.astype(jnp.float32).reshape(tok_rows, seq_count, group)
-    sig_rows = jnp.transpose(sig_rows, (1, 2, 0)).reshape(seq_count, -1, 128)
-    sig_chan = exchange(sig_rows, 1).reshape(seq_count, group, tok_rows)
-    sig_chan = jnp.transpose(sig_chan, (1, 0, 2)).reshape(group, half_first, second_len)
+    sig_rows = signal.astype(jnp.float32).reshape(tok_tiles, lanes, seq_count, group)
+    sig_rows = jnp.transpose(sig_rows, (2, 3, 0, 1)).reshape(seq_count, -1, lanes)
+    sig_chan = exchange(sig_rows, 1).reshape(seq_count, group, tok_tiles, lanes)
+    sig_chan = jnp.transpose(sig_chan, (1, 0, 2, 3)).reshape(group, half_first, second_len)
 
     digit_order = reversed_digits(seq_count)
     slots = np.arange(stride)
@@ -147,10 +151,10 @@
     untwist_re = back_re * cos_twist - back_im * sin_twist
     untwist_im = back_im * cos_twist + back_re * sin_twist
     conv = mm("rn,crm->cnm", cos_first, untwist_re) - mm("rn,crm->cnm", sin_first, untwist_im)
-    conv = (conv * (1.0 / all_bins)).reshape(group, seq_count, tok_rows)
-    conv = jnp.transpose(conv, (1, 0, 2)).reshape(seq_count, -1, 128)
-    result = exchange(conv, 2).reshape(seq_count, group, tok_rows)
-    result = jnp.transpose(result, (2, 0, 1)).reshape(tok_rows, chan_width)
+    conv = (conv * (1.0 / all_bins)).reshape(group, seq_count, tok_tiles, lanes)
+    conv = jnp.transpose(conv, (1, 0, 2, 3)).reshape(seq_count, -1, lanes)
+    result = exchange(conv, 2).reshape(seq_count, group, tok_tiles, lanes)
+    result = jnp.transpose(result, (2, 3, 0, 1)).reshape(tok_rows, chan_width)
     gated = post_gate.astype(jnp.float32) * (result + skip_weight * signal.astype(jnp.float32))
     return gated.astype(jnp.bfloat16)
 

time: 171 us -> 99.8 us (0.58)
  local copies, waits for them, and re-layouts: 65 us -> 10.2 us
  Pallas kernels: 71.5 us -> 42.9 us
  starting transfers between devices: 0 us -> 13.3 us
    reshape x10 -> x2, local copies, waits for them, and re-layouts: 40.4 us -> 1.81 us  [the longest x1 1.03 us: local(): sig_chan = exchange(sig_rows, 1).reshape(seq_count, group, tok_tiles, lanes)]
    pallas_call x3 -> x2, Pallas kernels: 71.5 us -> 42.9 us  [exchange(): pl.pallas_call(exchange_kernel, out_shape=jax.ShapeDtypeStruct(blocks.sha...]
    transpose x3 -> x2, local copies, waits for them, and re-layouts: 20 us -> 3.04 us  [the longest x1 2.29 us: local(): spec_rows = jnp.transpose(spec_rows, (4, 0, 1, 3, 2))]
    all_to_all x0 -> x1, starting transfers between devices: none -> 13.3 us  [local(): spec_chan = lax.all_to_all(spec_rows, 'seq', 0, 2, tiled=True)]
    unnamed x10 -> x17, local copies, waits for them, and re-layouts: 3.69 us -> 3.41 us
  transfers between devices with their start and end apart: 0 -> 1, of which waited for: 0 -> 0; matrix products, arithmetic and copies ran while one was open for 0% -> 15% of each run, Pallas kernels for 0% -> 26%
where the time goes in v4:
time: 99.8 us; the launch traced here: 99.4 us
  Pallas kernels  42.9 us (43%)
  matrix products  21.5 us (22%)
  starting transfers between devices  13.3 us (13%)
  local copies, waits for them, and re-layouts  10.2 us (10%)
  blocking collectives  9.06 us (9%)
  other arithmetic  2.23 us (2%)
    pallas_call x2, Pallas kernels, exchange(): pl.pallas_call(exchange_kernel, out_shape=jax.ShapeDtypeStruct(blocks.sha...  42.9 us
    dot_general x12, matrix products, mm(): jnp.einsum(spec, left, right, precision=PRECISE, preferred_element_type=j...  21.5 us
    all_to_all x1, starting transfers between devices, local(): spec_chan = lax.all_to_all(spec_rows, 'seq', 0, 2, tiled=True)  13.3 us
    psum x1, blocking collectives, local(): squares = lax.psum(jnp.sum(widened * widened, axis=1), 'chan')  9.06 us
    unnamed x17, local copies, waits for them, and re-layouts  3.41 us
    transpose x1, local copies, waits for them, and re-layouts, local(): spec_rows = jnp.transpose(spec_rows, (4, 0, 1, 3, 2))  2.29 us
  transfers between devices with their start and end apart: 1, of which 0 were waited for; matrix products, arithmetic and copies ran while one was open for 15% of the time, Pallas kernels for 26%

profile of v4, /device:TPU:1, one launch (start us, length us, event | category | flops | bytes accessed | tf_op | source)
XLA Modules:
  0.0 99.4 jit_solution(15079020173427018003)
XLA Ops:
  0.0 2.3 %copy.85 = f32[128,2,2,4,128]{4,3,2,1,0:T(4,128)} copy(f32[128,2,2,4,128]{0,3,4,2,1:T(4,128)} %bitcast.89) | data formatting | bytes 2097152 | tf_op jit(solution)/shard_map/transpose | solution.py:111
  2.3 13.3 %all-to-all-start = ((f32[128,2,2,4,128]{4,3,2,1,0:T(4,128)}), f32[128,2,2,4,128]{4,3,2,1,0:T(4,128)S(1)}, u32[]{:S(2)}, u32[]{:S(2)}) async-start(f32[128,2,2,4,128]{4,3,2,1,0:T(4,128)} %copy.85), calls=%async_computation | async-start | bytes 2097152 | tf_op jit(solution)/shard_map/all_to_all | solution.py:112
  15.8 0.8 copy-done.2
  16.7 9.1 %psum.7 = f32[512]{0:T(512)S(1)} all-reduce(f32[512]{0:T(512)S(1)} %fusion.20), channel_id=1, replica_groups=mesh['seq'=64,'chan'=4] {'chan'}, use_global_device_ids=true, to_apply=%region_1.0 | all-reduce | flops 512 | bytes 4096 | tf_op jit(solution)/shard_map/psum | solution.py:116
  26.6 0.8 reshape.80
  27.3 25.9 %shard_map.73 = f32[64,8,128]{2,1,0:T(8,128)} custom-call(f32[64,8,128]{2,1,0:T(8,128)} %bitcast.93), custom_call_target="tpu_custom_call" | custom-call | tf_op jit(solution)/shard_map/pallas_call | solution.py:84
  53.3 1.0 %copy.80 = f32[64,2,4,128]{3,2,0,1:T(4,128)S(1)} copy(f32[64,2,4,128]{3,2,1,0:T(4,128)} %bitcast.90) | data formatting | bytes 524288 | tf_op jit(solution)/shard_map/reshape | solution.py:122
  55.0 1.0 %fusion.44 = (f32[512,128]{0,1:T(8,128)S(1)}, f32[512,128]{0,1:T(8,128)S(1)}) fusion(s32[512]{0:T(512)S(1)} %copy-done.4), kind=kLoop, calls=%fused_computation.62 | loop fusion | flops 917504 | bytes 526336 | tf_op jit(solution)/shard_map/cos | solution.py:31
  56.0 3.3 %fusion = f32[2,512,128]{1,2,0:T(8,128)S(1)} fusion(f32[2,256,128]{2,1,0:T(8,128)S(1)} %bitcast.95, s32[512]{0:T(512)S(1)} %copy-done.4), kind=kOutput, calls=%fused_computation.1 | convolution fusion | flops 404619264 | bytes 788480 | tf_op jit(solution)/shard_map/rn,cnm->crm/dot_general | solution.py:35
  59.4 3.5 %convolution_bitcast_fusion = f32[2,512,128]{1,2,0:T(8,128)S(1)} fusion(f32[2,256,128]{2,1,0:T(8,128)S(1)} %bitcast.96, s32[512]{0:T(512)S(1)} %copy-done.4), kind=kOutput, calls=%fused_computation.2 | convolution fusion | flops 404488192 | bytes 788480 | tf_op jit(solution)/shard_map/rn,cnm->crm/dot_general | solution.py:35
  62.9 1.2 %fusion.58 = f32[2,512,128]{2,1,0:T(8,128)S(1)} fusion(f32[2,512,128]{1,2,0:T(8,128)S(1)} %fusion, f32[2,512,128]{1,2,0:T(8,128)S(1)} %convolution_bitcast_fusion, f32[512,128]{0,1:T(8,128)S(1)} %get-tuple-element.8, f32[512,128]{0,1:T(8,128)S(1)} %get-tuple-element.7), kind=kOutput, calls=%fused_computation.79 | convolution fusion | flops 201949184 | bytes 2097152 | tf_op jit(solution)/shard_map/crn,nk->crk/dot_general | solution.py:35
  64.1 2.0 %fusion.56 = f32[2,512,128]{2,1,0:T(8,128)} fusion(f32[2,512,128]{1,2,0:T(8,128)S(1)} %convolution_bitcast_fusion, f32[2,512,128]{1,2,0:T(8,128)S(1)} %fusion, f32[512,128]{0,1:T(8,128)S(1)} %get-tuple-element.8, f32[512,128]{0,1:T(8,128)S(1)} %get-tuple-element.7), kind=kOutput, calls=%fused_computation.77 | convolution fusion | flops 201949184 | bytes 2097152 | tf_op jit(solution)/shard_map/crn,nk->crk/dot_general | solution.py:35
  66.2 1.2 %convolution_add_fusion.1 = f32[2,512,128]{2,1,0:T(8,128)S(1)} fusion(f32[2,512,128]{2,1,0:T(8,128)S(1)} %fusion.58, f32[2,512,128]{1,2,0:T(8,128)S(1)} %convolution_bitcast_fusion, f32[2,512,128]{1,2,0:T(8,128)S(1)} %fusion, f32[512,128]{0,1:T(8,128)S(1)} %get-tuple-element.8, f32[512,128]{0,1:T(8,128)S(1)} %get-tuple-element.7), kind=kOutput, calls=%fused_computation.6 | convolution fusion | flops 202080256 | bytes 2621440 | tf_op jit(solution)/shard_map/crn,nk->crk/dot_general | solution.py:35
  68.8 1.2 %multiply_subtract_fusion = (f32[2,512,128]{2,1,0:T(8,128)S(1)}, f32[2,512,128]{2,1,0:T(8,128)S(1)}) fusion(f32[2,512,128]{2,1,0:T(8,128)S(1)} %convolution_add_fusion.1, f32[2,2,512,128]{3,2,0,1:T(8,128)S(1)} %bitcast.88, f32[2,512,128]{2,1,0:T(8,128)S(1)} %copy-done, f32[2,512,128]{1,2,0:T(8,128)S(1)} %fusion, ...), kind=kOutput, calls=%fused_computation.30 | convolution fusion | flops 202866688 | bytes 4718592 | tf_op jit(solution)/shard_map/crn,nk->crk/dot_general | solution.py:35
  70.1 0.9 fusion.52
  71.0 0.9 fusion.54
  71.8 0.9 convolution_add_fusion
  72.7 0.9 convolution_subtract_fusion
  73.6 2.8 %fusion.8 = f32[2,128,256]{2,1,0:T(8,128)S(1)} fusion(f32[2,512,128]{1,2,0:T(8,128)S(1)} %convolution_add_fusion, f32[2,512,128]{1,2,0:T(8,128)S(1)} %convolution_subtract_fusion, f32[512,128]{0,1:T(8,128)S(1)} %get-tuple-element.8, f32[512,128]{0,1:T(8,128)S(1)} %get-tuple-element.7, s32[512]{0:T(512)S(1)} %copy-done.4), kind=kOutput, calls=%fused_computation.20 | convolution fusion | flops 404881408 | bytes 1837056 | tf_op jit(solution)/shard_map/rn,crm->cnm/dot_general | solution.py:35
  76.4 2.6 %fusion.2 = f32[2,256,128]{1,2,0:T(8,128)S(1)} fusion(f32[2,128,256]{2,1,0:T(8,128)S(1)} %fusion.8, f32[2,512,128]{1,2,0:T(8,128)S(1)} %convolution_subtract_fusion, f32[2,512,128]{1,2,0:T(8,128)S(1)} %convolution_add_fusion, f32[512,128]{0,1:T(8,128)S(1)} %get-tuple-element.8, f32[512,128]{0,1:T(8,128)S(1)} %get-tuple-element.7, s32[512]{0:T(512)S(1)} %copy-done.4), kind=kOutput, calls=%fused_computation.9 | convolution fusion | flops 405012480 | bytes 2099200 | tf_op jit(solution)/shard_map/rn,crm->cnm/dot_general | solution.py:35
  79.2 0.8 copy.95
  79.9 17.0 %shard_map.74 = f32[64,8,128]{2,1,0:T(8,128)} custom-call(f32[64,8,128]{2,1,0:T(8,128)} %bitcast.92), custom_call_target="tpu_custom_call" | custom-call | tf_op jit(solution)/shard_map/pallas_call | solution.py:84
  97.6 1.1 %fusion.28 = bf16[512,128]{0,1:T(8,128)(2,1)S(1)} fusion(f32[16,8,4,128]{3,2,1,0:T(4,128)} %bitcast.94, f32[512,128]{0,1:T(8,128)S(1)} %fusion.42, bf16[512,128]{0,1:T(8,128)(2,1)S(1)} %copy.77, f32[128]{0:T(128)S(1)} %copy-done.6), kind=kLoop, calls=%fused_computation.50 | loop fusion | flops 327680 | bytes 786944 | tf_op jit(solution)/shard_map/convert_element_type | solution.py:159
  98.6 0.8 copy.96
  (23 shorter events, 3.9 us)
Async XLA Ops:
  2.3 13.3 %copy-start.1 = (bf16[512,128]{1,0:T(8,128)(2,1)S(1)}, bf16[512,128]{1,0:T(8,128)(2,1)}, u32[]{:S(2)}) copy-start(bf16[512,128]{1,0:T(8,128)(2,1)} %param.7) | copy-start | bytes 393220
  2.3 65.1 %all-to-all-start = ((f32[128,2,2,4,128]{4,3,2,1,0:T(4,128)}), f32[128,2,2,4,128]{4,3,2,1,0:T(4,128)S(1)}, u32[]{:S(2)}, u32[]{:S(2)}) async-start(f32[128,2,2,4,128]{4,3,2,1,0:T(4,128)} %copy.85), calls=%async_computation | async-start | bytes 2097152 | tf_op jit(solution)/shard_map/all_to_all | solution.py:112
  15.7 0.9 copy-start.2
  25.8 0.7 copy-start.5
  53.2 1.0 %copy-start.3 = (bf16[512,128]{1,0:T(8,128)(2,1)S(1)}, bf16[512,128]{1,0:T(8,128)(2,1)}, u32[]{:S(2)}) copy-start(bf16[512,128]{1,0:T(8,128)(2,1)} %param.9) | copy-start | bytes 393220
  54.3 0.7 copy-start.4
  67.8 1.0 %copy-start = (f32[2,512,128]{2,1,0:T(8,128)S(1)}, f32[2,512,128]{2,1,0:T(8,128)}, u32[]{:S(2)}) copy-start(f32[2,512,128]{2,1,0:T(8,128)} %fusion.56) | copy-start | bytes 1572868
  96.9 0.7 copy-start.6

commit v5 on v4

--- a/solution.py
+++ b/solution.py
@@ -13,7 +13,7 @@
 HIGH_DIGIT = 8
 
 
-PRECISE = lax.Precision.HIGHEST
+PRECISE = lax.Precision.HIGH
 FULL_TURN = 2.0 * math.pi
 
 

time: 99.8 us -> 96.1 us (0.963)
  matrix products: 21.5 us -> 17.8 us
    dot_general x12, matrix products: 21.5 us -> 17.8 us  [mm(): jnp.einsum(spec, left, right, precision=PRECISE, preferred_element_type=j...]
  transfers between devices with their start and end apart: 1 -> 1, of which waited for: 0 -> 0; matrix products, arithmetic and copies ran while one was open for 15% -> 14% of each run, Pallas kernels for 26% -> 27%
where the time goes in v5:
time: 96.1 us; the launch traced here: 95.7 us
  Pallas kernels  42.9 us (45%)
  matrix products  17.8 us (19%)
  starting transfers between devices  13.3 us (14%)
  local copies, waits for them, and re-layouts  10.2 us (11%)
  blocking collectives  9.06 us (9%)
  other arithmetic  2.23 us (2%)
    pallas_call x2, Pallas kernels, exchange(): pl.pallas_call(exchange_kernel, out_shape=jax.ShapeDtypeStruct(blocks.sha...  42.9 us
    dot_general x12, matrix products, mm(): jnp.einsum(spec, left, right, precision=PRECISE, preferred_element_type=j...  17.8 us
    all_to_all x1, starting transfers between devices, local(): spec_chan = lax.all_to_all(spec_rows, 'seq', 0, 2, tiled=True)  13.3 us
    psum x1, blocking collectives, local(): squares = lax.psum(jnp.sum(widened * widened, axis=1), 'chan')  9.06 us
    unnamed x17, local copies, waits for them, and re-layouts  3.41 us
    transpose x1, local copies, waits for them, and re-layouts, local(): spec_rows = jnp.transpose(spec_rows, (4, 0, 1, 3, 2))  2.29 us
  transfers between devices with their start and end apart: 1, of which 0 were waited for; matrix products, arithmetic and copies ran while one was open for 14% of the time, Pallas kernels for 27%

profile of v5, /device:TPU:1, one launch (start us, length us, event | category | flops | bytes accessed | tf_op | source)
XLA Modules:
  0.0 95.7 jit_solution(2755285280329172572)
XLA Ops:
  0.0 2.3 %copy.85 = f32[128,2,2,4,128]{4,3,2,1,0:T(4,128)} copy(f32[128,2,2,4,128]{0,3,4,2,1:T(4,128)} %bitcast.89) | data formatting | bytes 2097152 | tf_op jit(solution)/shard_map/transpose | solution.py:111
  2.3 13.3 %all-to-all-start = ((f32[128,2,2,4,128]{4,3,2,1,0:T(4,128)}), f32[128,2,2,4,128]{4,3,2,1,0:T(4,128)S(1)}, u32[]{:S(2)}, u32[]{:S(2)}) async-start(f32[128,2,2,4,128]{4,3,2,1,0:T(4,128)} %copy.85), calls=%async_computation | async-start | bytes 2097152 | tf_op jit(solution)/shard_map/all_to_all | solution.py:112
  15.8 0.8 copy-done.2
  16.7 9.1 %psum.7 = f32[512]{0:T(512)S(1)} all-reduce(f32[512]{0:T(512)S(1)} %fusion.20), channel_id=1, replica_groups=mesh['seq'=64,'chan'=4] {'chan'}, use_global_device_ids=true, to_apply=%region_1.0 | all-reduce | flops 512 | bytes 4096 | tf_op jit(solution)/shard_map/psum | solution.py:116
  26.6 0.8 reshape.80
  27.3 25.9 %shard_map.73 = f32[64,8,128]{2,1,0:T(8,128)} custom-call(f32[64,8,128]{2,1,0:T(8,128)} %bitcast.93), custom_call_target="tpu_custom_call" | custom-call | tf_op jit(solution)/shard_map/pallas_call | solution.py:84
  53.3 1.0 %copy.80 = f32[64,2,4,128]{3,2,0,1:T(4,128)S(1)} copy(f32[64,2,4,128]{3,2,1,0:T(4,128)} %bitcast.90) | data formatting | bytes 524288 | tf_op jit(solution)/shard_map/reshape | solution.py:122
  55.0 1.0 %fusion.44 = (f32[512,128]{0,1:T(8,128)S(1)}, f32[512,128]{0,1:T(8,128)S(1)}) fusion(s32[512]{0:T(512)S(1)} %copy-done.4), kind=kLoop, calls=%fused_computation.62 | loop fusion | flops 917504 | bytes 526336 | tf_op jit(solution)/shard_map/cos | solution.py:31
  56.0 3.2 %fusion = f32[2,512,128]{1,2,0:T(8,128)S(1)} fusion(f32[2,256,128]{2,1,0:T(8,128)S(1)} %bitcast.95, s32[512]{0:T(512)S(1)} %copy-done.4), kind=kOutput, calls=%fused_computation.1 | convolution fusion | flops 203292672 | bytes 788480 | tf_op jit(solution)/shard_map/rn,cnm->crm/dot_general | solution.py:35
  59.2 3.2 %convolution_bitcast_fusion = f32[2,512,128]{1,2,0:T(8,128)S(1)} fusion(f32[2,256,128]{2,1,0:T(8,128)S(1)} %bitcast.96, s32[512]{0:T(512)S(1)} %copy-done.4), kind=kOutput, calls=%fused_computation.2 | convolution fusion | flops 203161600 | bytes 788480 | tf_op jit(solution)/shard_map/rn,cnm->crm/dot_general | solution.py:35
  62.4 0.8 fusion.58
  63.2 1.6 %fusion.56 = f32[2,512,128]{2,1,0:T(8,128)} fusion(f32[2,512,128]{1,2,0:T(8,128)S(1)} %convolution_bitcast_fusion, f32[2,512,128]{1,2,0:T(8,128)S(1)} %fusion, f32[512,128]{0,1:T(8,128)S(1)} %get-tuple-element.8, f32[512,128]{0,1:T(8,128)S(1)} %get-tuple-element.7), kind=kOutput, calls=%fused_computation.77 | convolution fusion | flops 101285888 | bytes 2097152 | tf_op jit(solution)/shard_map/crn,nk->crk/dot_general | solution.py:35
  64.8 0.8 convolution_add_fusion.1
  66.0 0.7 copy.87
  67.1 0.8 multiply_subtract_fusion
  67.9 0.6 fusion.52
  69.2 0.7 convolution_add_fusion
  69.9 0.7 convolution_subtract_fusion
  70.6 2.4 %fusion.8 = f32[2,128,256]{2,1,0:T(8,128)S(1)} fusion(f32[2,512,128]{1,2,0:T(8,128)S(1)} %convolution_add_fusion, f32[2,512,128]{1,2,0:T(8,128)S(1)} %convolution_subtract_fusion, f32[512,128]{0,1:T(8,128)S(1)} %get-tuple-element.8, f32[512,128]{0,1:T(8,128)S(1)} %get-tuple-element.7, s32[512]{0:T(512)S(1)} %copy-done.4), kind=kOutput, calls=%fused_computation.20 | convolution fusion | flops 203554816 | bytes 1837056 | tf_op jit(solution)/shard_map/rn,crm->cnm/dot_general | solution.py:35
  72.9 2.4 %fusion.2 = f32[2,256,128]{1,2,0:T(8,128)S(1)} fusion(f32[2,128,256]{2,1,0:T(8,128)S(1)} %fusion.8, f32[2,512,128]{1,2,0:T(8,128)S(1)} %convolution_subtract_fusion, f32[2,512,128]{1,2,0:T(8,128)S(1)} %convolution_add_fusion, f32[512,128]{0,1:T(8,128)S(1)} %get-tuple-element.8, f32[512,128]{0,1:T(8,128)S(1)} %get-tuple-element.7, s32[512]{0:T(512)S(1)} %copy-done.4), kind=kOutput, calls=%fused_computation.9 | convolution fusion | flops 203685888 | bytes 2099200 | tf_op jit(solution)/shard_map/rn,crm->cnm/dot_general | solution.py:35
  75.5 0.8 copy.95
  76.2 17.0 %shard_map.74 = f32[64,8,128]{2,1,0:T(8,128)} custom-call(f32[64,8,128]{2,1,0:T(8,128)} %bitcast.92), custom_call_target="tpu_custom_call" | custom-call | tf_op jit(solution)/shard_map/pallas_call | solution.py:84
  93.9 1.1 %fusion.28 = bf16[512,128]{0,1:T(8,128)(2,1)S(1)} fusion(f32[16,8,4,128]{3,2,1,0:T(4,128)} %bitcast.94, f32[512,128]{0,1:T(8,128)S(1)} %fusion.42, bf16[512,128]{0,1:T(8,128)(2,1)S(1)} %copy.77, f32[128]{0:T(128)S(1)} %copy-done.6), kind=kLoop, calls=%fused_computation.50 | loop fusion | flops 327680 | bytes 786944 | tf_op jit(solution)/shard_map/convert_element_type | solution.py:159
  94.9 0.8 copy.96
  (23 shorter events, 3.8 us)
Async XLA Ops:
  2.3 13.3 %copy-start.1 = (bf16[512,128]{1,0:T(8,128)(2,1)S(1)}, bf16[512,128]{1,0:T(8,128)(2,1)}, u32[]{:S(2)}) copy-start(bf16[512,128]{1,0:T(8,128)(2,1)} %param.7) | copy-start | bytes 393220
  2.3 63.4 %all-to-all-start = ((f32[128,2,2,4,128]{4,3,2,1,0:T(4,128)}), f32[128,2,2,4,128]{4,3,2,1,0:T(4,128)S(1)}, u32[]{:S(2)}, u32[]{:S(2)}) async-start(f32[128,2,2,4,128]{4,3,2,1,0:T(4,128)} %copy.85), calls=%async_computation | async-start | bytes 2097152 | tf_op jit(solution)/shard_map/all_to_all | solution.py:112
  15.7 0.9 copy-start.2
  25.8 0.7 copy-start.5
  53.2 1.0 %copy-start.3 = (bf16[512,128]{1,0:T(8,128)(2,1)S(1)}, bf16[512,128]{1,0:T(8,128)(2,1)}, u32[]{:S(2)}) copy-start(bf16[512,128]{1,0:T(8,128)(2,1)} %param.9) | copy-start | bytes 393220
  54.3 0.7 copy-start.4
  66.0 1.0 %copy-start = (f32[2,512,128]{2,1,0:T(8,128)S(1)}, f32[2,512,128]{2,1,0:T(8,128)}, u32[]{:S(2)}) copy-start(f32[2,512,128]{2,1,0:T(8,128)} %fusion.56) | copy-start | bytes 1572868
  93.2 0.7 copy-start.6

commit v6 on v5

--- a/solution.py
+++ b/solution.py
@@ -95,9 +95,152 @@
     )(blocks)
 
 
+def front_kernel(
+    feat_ref, gate_ref, gain_ref, spec_ref,
+    sig_out, sig_recv, spec_recv,
+    sq_mine, sq_recv, sig_send, spec_sems, sig_sems, chan_sems, own_sems,
+):
+    count = spec_ref.shape[0]
+    chans = sq_recv.shape[0]
+    me = lax.axis_index("seq")
+    mine = lax.axis_index("chan")
+    mesh_ids = pl.DeviceIdType.MESH
+    barrier = pltpu.get_barrier_semaphore()
+
+    def greet(step, carry):
+        peer = lax.rem(me + step, count)
+        pl.semaphore_signal(barrier, inc=1, device_id={"seq": peer}, device_id_type=mesh_ids)
+        return carry
+
+    lax.fori_loop(1, count, greet, 0)
+    for step in range(1, chans):
+        peer = lax.rem(mine + step, chans)
+        pl.semaphore_signal(barrier, inc=1, device_id={"chan": peer}, device_id_type=mesh_ids)
+    pl.semaphore_wait(barrier, count + chans - 2)
+
+    def spec_copy(step):
+        peer = lax.rem(me + step, count)
+        return pltpu.make_async_remote_copy(
+            spec_ref.at[peer],
+            spec_recv.at[me],
+            spec_sems.at[0, step],
+            spec_sems.at[1, step],
+            device_id={"seq": peer},
+            device_id_type=mesh_ids,
+        )
+
+    spec_own = pltpu.make_async_copy(spec_ref.at[me], spec_recv.at[me], own_sems.at[0])
+    spec_own.start()
+
+    def spec_send(step, carry):
+        spec_copy(step).start()
+        return carry
+
+    lax.fori_loop(1, count, spec_send, 0)
+
+    feat = feat_ref[...].astype(jnp.float32)
+    part = jnp.sum(feat * feat, axis=0, keepdims=True)
+    sq_mine[...] = jnp.broadcast_to(part, sq_mine.shape)
+
+    def chan_copy(step):
+        peer = lax.rem(mine + step, chans)
+        return pltpu.make_async_remote_copy(
+            sq_mine,
+            sq_recv.at[mine],
+            chan_sems.at[0, step],
+            chan_sems.at[1, step],
+            device_id={"chan": peer},
+            device_id_type=mesh_ids,
+        )
+
+    for step in range(1, chans):
+        chan_copy(step).start()
+    for step in range(1, chans):
+        copy = chan_copy(step)
+        copy.wait_send()
+        copy.wait_recv()
+    total = part
+    for step in range(1, chans):
+        other = lax.rem(mine + step, chans)
+        total = total + sq_recv[other][0:1, :]
+    scale = lax.rsqrt(total / CHANNELS + 1e-06)
+    signal = (feat * scale * gain_ref[...] * gate_ref[...].astype(jnp.float32)).astype(jnp.bfloat16)
+    sig_out[...] = signal
+    wide = signal.astype(jnp.float32)
+    pair = sig_send.shape[1]
+    for peer in range(count):
+        sig_send[peer] = wide[pair * peer:pair * peer + pair, :]
+
+    def sig_copy(step):
+        peer = lax.rem(me + step, count)
+        return pltpu.make_async_remote_copy(
+            sig_send.at[peer],
+            sig_recv.at[me],
+            sig_sems.at[0, step],
+            sig_sems.at[1, step],
+            device_id={"seq": peer},
+            device_id_type=mesh_ids,
+        )
+
+    sig_own = pltpu.make_async_copy(sig_send.at[me], sig_recv.at[me], own_sems.at[1])
+    sig_own.start()
+
+    def sig_start(step, carry):
+        sig_copy(step).start()
+        return carry
+
+    lax.fori_loop(1, count, sig_start, 0)
+
+    def sig_finish(step, carry):
+        copy = sig_copy(step)
+        copy.wait_send()
+        copy.wait_recv()
+        return carry
+
+    lax.fori_loop(1, count, sig_finish, 0)
+    sig_own.wait()
+
+    def spec_finish(step, carry):
+        copy = spec_copy(step)
+        copy.wait_send()
+        copy.wait_recv()
+        return carry
+
+    lax.fori_loop(1, count, spec_finish, 0)
+    spec_own.wait()
+
+
+def front(feat_t, gate_t, gain_col, spec_rows, chans):
+    count = spec_rows.shape[0]
+    width, length = feat_t.shape
+    pair = width // count
+    vmem = pl.BlockSpec(memory_space=pltpu.VMEM)
+    return pl.pallas_call(
+        front_kernel,
+        out_shape=(
+            jax.ShapeDtypeStruct((width, length), jnp.bfloat16),
+            jax.ShapeDtypeStruct((count, pair, length), jnp.float32),
+            jax.ShapeDtypeStruct(spec_rows.shape, spec_rows.dtype),
+        ),
+        in_specs=[vmem] * 4,
+        out_specs=(vmem, vmem, vmem),
+        scratch_shapes=[
+            pltpu.VMEM((8, length), jnp.float32),
+            pltpu.VMEM((chans, 8, length), jnp.float32),
+            pltpu.VMEM((count, pair, length), jnp.float32),
+            pltpu.SemaphoreType.DMA((2, count)),
+            pltpu.SemaphoreType.DMA((2, count)),
+            pltpu.SemaphoreType.DMA((2, chans)),
+            pltpu.SemaphoreType.DMA((2,)),
+        ],
+        compiler_params=pltpu.CompilerParams(collective_id=0, has_side_effects=True),
+    )(feat_t, gate_t, gain_col, spec_rows)
+
+
 def local(features, pre_gate, post_gate, norm_gain, skip_weight, spectrum):
     tok_rows, chan_width = features.shape
     seq_count = lax.axis_size("seq")
+    chans = lax.axis_size("chan")
     stride = 2 * seq_count
     all_bins = stride * tok_rows
     group = chan_width // seq_count
@@ -108,19 +251,14 @@
     tok_tiles = tok_rows // lanes
 
     spec_rows = spectrum.reshape(2, 2, second_len, ROW_GROUP, chan_width)
-    spec_rows = jnp.transpose(spec_rows, (4, 0, 1, 3, 2))
-    spec_chan = lax.all_to_all(spec_rows, "seq", 0, 2, tiled=True)
-    spec_chan = spec_chan.reshape(group, 2, first_len, second_len)
-
-    widened = features.astype(jnp.float32)
-    squares = lax.psum(jnp.sum(widened * widened, axis=1), "chan")
-    scaled = widened * lax.rsqrt(squares / CHANNELS + 1e-06)[:, None] * norm_gain
-    signal = (scaled * pre_gate.astype(jnp.float32)).astype(jnp.bfloat16)
-
-    sig_rows = signal.astype(jnp.float32).reshape(tok_tiles, lanes, seq_count, group)
-    sig_rows = jnp.transpose(sig_rows, (2, 3, 0, 1)).reshape(seq_count, -1, lanes)
-    sig_chan = exchange(sig_rows, 1).reshape(seq_count, group, tok_tiles, lanes)
-    sig_chan = jnp.transpose(sig_chan, (1, 0, 2, 3)).reshape(group, half_first, second_len)
+    spec_rows = jnp.transpose(spec_rows, (4, 0, 1, 3, 2)).reshape(seq_count, -1, ROW_GROUP * second_len)
+    signal_t, sig_chan, spec_chan = front(
+        features.T, pre_gate.T, norm_gain.reshape(chan_width, 1), spec_rows, chans
+    )
+    spec_chan = spec_chan.reshape(seq_count, group, 2, 2, ROW_GROUP * second_len)
+    spec_chan = jnp.transpose(spec_chan, (1, 2, 0, 3, 4)).reshape(group, 2, first_len, second_len)
+    sig_chan = jnp.transpose(sig_chan, (1, 0, 2)).reshape(group, half_first, second_len)
+    signal = signal_t.T
 
     digit_order = reversed_digits(seq_count)
     slots = np.arange(stride)

time: 96.1 us -> 99.8 us (1.039)
  Pallas kernels: 42.9 us -> 64.6 us
  starting transfers between devices: 13.3 us -> 0 us
  blocking collectives: 9.06 us -> 0 us
  local copies, waits for them, and re-layouts: 10.2 us -> 16.3 us
  other arithmetic: 2.23 us -> 1.15 us
    pallas_call x0 -> x1, Pallas kernels: none -> 47.1 us  [front(): pl.pallas_call(front_kernel, out_shape=(jax.ShapeDtypeStruct((width, leng...]
    pallas_call x2 -> x1, Pallas kernels: 42.9 us -> 17.5 us  [exchange(): pl.pallas_call(exchange_kernel, out_shape=jax.ShapeDtypeStruct(blocks.sha...]
    all_to_all x1 -> x0, starting transfers between devices: 13.3 us -> none  [local(): spec_chan = lax.all_to_all(spec_rows, 'seq', 0, 2, tiled=True)]
    psum x1 -> x0, blocking collectives: 9.06 us -> none  [local(): squares = lax.psum(jnp.sum(widened * widened, axis=1), 'chan')]
    reshape x2 -> x6, local copies, waits for them, and re-layouts: 1.81 us -> 7.64 us  [the longest x1 2.06 us: local(): jnp.transpose(spec_chan, (1, 2, 0, 3, 4))]
    unnamed x17, local copies, waits for them, and re-layouts: 3.41 us -> 4.68 us
    all_to_all x2 -> x0, local copies, waits for them, and re-layouts: 1.02 us -> none  [local(): spec_chan = lax.all_to_all(spec_rows, 'seq', 0, 2, tiled=True)]
    transpose x1 -> x2, local copies, waits for them, and re-layouts: 2.29 us -> 2.33 us  [the longest x1 1.32 us: local(): jnp.transpose(spec_chan, (1, 2, 0, 3, 4))]
  transfers between devices with their start and end apart: 1 -> 0, of which waited for: 0 -> 0; matrix products, arithmetic and copies ran while one was open for 14% -> 0% of each run, Pallas kernels for 27% -> 0%
where the time goes in v6:
time: 99.8 us; the launch traced here: 99.5 us
  Pallas kernels  64.6 us (65%)
  matrix products  17.3 us (17%)
  local copies, waits for them, and re-layouts  16.3 us (16%)
  other arithmetic  1.15 us (1%)
    pallas_call x1, Pallas kernels, front(): pl.pallas_call(front_kernel, out_shape=(jax.ShapeDtypeStruct((width, leng...  47.1 us
    pallas_call x1, Pallas kernels, exchange(): pl.pallas_call(exchange_kernel, out_shape=jax.ShapeDtypeStruct(blocks.sha...  17.5 us
    dot_general x12, matrix products, mm(): jnp.einsum(spec, left, right, precision=PRECISE, preferred_element_type=j...  17.3 us
    unnamed x17, local copies, waits for them, and re-layouts  4.68 us
    reshape x1, local copies, waits for them, and re-layouts, local(): jnp.transpose(spec_chan, (1, 2, 0, 3, 4))  2.06 us

profile of v6, /device:TPU:1, one launch (start us, length us, event | category | flops | bytes accessed | tf_op | source)
XLA Modules:
  0.0 99.5 jit_solution(4576548017170138117)
XLA Ops:
  0.0 1.7 %copy.25 = bf16[512,128]{0,1:T(8,128)(2,1)} copy(bf16[512,128]{1,0:T(8,128)(2,1)} %param.7) | data formatting | bytes 262144 | tf_op args[0]
  1.7 0.8 copy.26
  3.1 0.7 copy.28.gain_ref
  3.9 1.6 %copy.27 = f32[2,2,128,4,128]{2,3,1,0,4:T(4,128)S(1)} copy(f32[2,2,128,4,128]{4,3,2,1,0:T(4,128)} %bitcast.84) | data formatting | bytes 2097152 | tf_op jit(solution)/shard_map/reshape | solution.py:253
  5.5 1.4 %reshape.79.spec_ref = f32[64,8,512]{2,1,0:T(8,128)} reshape(f32[128,2,2,4,128]{4,3,2,1,0:T(4,128)S(1)} %bitcast.83) | data formatting | bytes 2097152 | tf_op jit(solution)/shard_map/reshape | solution.py:254
  6.8 47.1 %shard_map.73 = (bf16[128,512]{1,0:T(8,128)(2,1)}, f32[64,2,512]{2,1,0:T(2,128)}, f32[64,8,512]{2,1,0:T(8,128)}) custom-call(bf16[128,512]{1,0:T(8,128)(2,1)} %bitcast.88, bf16[128,512]{1,0:T(8,128)(2,1)} %bitcast.89, f32[128,1]{1,0:T(8,128)} %copy.28.gain_ref, f32[64,8,512]{2,1,0:T(8,128)} %reshape.79.spec_ref), custom_call_target="tpu_custom_call" | custom-call | tf_op jit(solution)/shard_map/pallas_call | solution.py:218
  54.0 1.0 %copy.29 = f32[2,64,512]{2,1,0:T(8,128)S(1)} copy(f32[2,64,512]{2,0,1:T(2,128)} %bitcast.90) | data formatting | bytes 524288 | tf_op jit(solution)/shard_map/transpose | solution.py:260
  55.7 3.1 %fusion = f32[2,512,128]{1,2,0:T(8,128)S(1)} fusion(f32[2,256,128]{2,1,0:T(8,128)S(1)} %reshape.80, s32[512]{0:T(512)S(1)} %copy-done.4), kind=kOutput, calls=%fused_computation.1 | convolution fusion | flops 203292672 | bytes 788480 | tf_op jit(solution)/shard_map/rn,cnm->crm/dot_general | solution.py:35
  58.8 3.2 %convolution_bitcast_fusion = f32[2,512,128]{1,2,0:T(8,128)S(1)} fusion(f32[2,256,128]{2,1,0:T(8,128)S(1)} %reshape.80, s32[512]{0:T(512)S(1)} %copy-done.4), kind=kOutput, calls=%fused_computation.2 | convolution fusion | flops 203161600 | bytes 788480 | tf_op jit(solution)/shard_map/rn,cnm->crm/dot_general | solution.py:35
  62.0 1.0 %fusion.39 = (f32[512,128]{0,1:T(8,128)S(1)}, f32[512,128]{0,1:T(8,128)S(1)}) fusion(s32[512]{0:T(512)S(1)} %copy-done.4), kind=kLoop, calls=%fused_computation.55 | loop fusion | flops 917504 | bytes 526336 | tf_op jit(solution)/shard_map/cos | solution.py:31
  63.0 0.8 fusion.53
  63.9 0.8 convolution_add_fusion.1
  64.7 1.8 %reshape.81 = f32[64,2,2,2,512]{4,3,2,1,0:T(2,128)S(1)} reshape(f32[64,8,512]{2,1,0:T(8,128)} %get-tuple-element.9) | data formatting | bytes 2097152 | tf_op jit(solution)/shard_map/reshape | solution.py:258
  66.6 1.3 %copy.34 = f32[2,2,64,2,512]{4,3,2,0,1:T(2,128)} copy(f32[2,2,64,2,512]{4,3,1,0,2:T(2,128)S(1)} %bitcast.82) | data formatting | bytes 2097152 | tf_op jit(solution)/shard_map/transpose | solution.py:259
  67.9 2.1 %reshape.82 = f32[2,2,512,128]{3,2,0,1:T(8,128)S(1)} reshape(f32[2,2,64,2,512]{4,3,2,0,1:T(2,128)} %copy.34) | data formatting | bytes 2097152 | tf_op jit(solution)/shard_map/reshape | solution.py:259
  70.0 0.8 fusion.51
  70.8 0.8 multiply_subtract_fusion
  73.6 0.7 convolution_subtract_fusion
  74.3 2.4 %fusion.8 = f32[2,128,256]{2,1,0:T(8,128)S(1)} fusion(f32[2,512,128]{1,2,0:T(8,128)S(1)} %convolution_add_fusion, f32[2,512,128]{1,2,0:T(8,128)S(1)} %convolution_subtract_fusion, f32[512,128]{0,1:T(8,128)S(1)} %get-tuple-element.14, f32[512,128]{0,1:T(8,128)S(1)} %get-tuple-element.13, s32[512]{0:T(512)S(1)} %copy-done.4), kind=kOutput, calls=%fused_computation.20 | convolution fusion | flops 203554816 | bytes 1837056 | tf_op jit(solution)/shard_map/rn,crm->cnm/dot_general | solution.py:35
  76.7 2.6 %fusion.2 = f32[2,256,128]{1,2,0:T(8,128)S(1)} fusion(f32[2,128,256]{2,1,0:T(8,128)S(1)} %fusion.8, f32[2,512,128]{1,2,0:T(8,128)S(1)} %convolution_subtract_fusion, f32[2,512,128]{1,2,0:T(8,128)S(1)} %convolution_add_fusion, f32[512,128]{0,1:T(8,128)S(1)} %get-tuple-element.14, f32[512,128]{0,1:T(8,128)S(1)} %get-tuple-element.13, s32[512]{0:T(512)S(1)} %copy-done.4), kind=kOutput, calls=%fused_computation.9 | convolution fusion | flops 203685888 | bytes 2099200 | tf_op jit(solution)/shard_map/rn,crm->cnm/dot_general | solution.py:35
  79.4 0.8 copy.42
  80.2 17.5 %shard_map.74 = f32[64,8,128]{2,1,0:T(8,128)} custom-call(f32[64,8,128]{2,1,0:T(8,128)} %bitcast.87), custom_call_target="tpu_custom_call" | custom-call | tf_op jit(solution)/shard_map/pallas_call | solution.py:84
  97.8 0.8 copy-done
  98.7 0.8 copy.43
  (20 shorter events, 3.7 us)
Async XLA Ops:
  0.0 1.7 %copy-start.1 = (bf16[512,128]{1,0:T(8,128)(2,1)S(1)}, bf16[512,128]{1,0:T(8,128)(2,1)}, u32[]{:S(2)}) copy-start(bf16[512,128]{1,0:T(8,128)(2,1)} %param.8) | copy-start | bytes 393220
  2.5 0.7 copy-start.5
  55.0 0.7 copy-start.4
  80.2 17.5 %copy-start.2 = (bf16[512,128]{1,0:T(8,128)(2,1)S(1)}, bf16[512,128]{1,0:T(8,128)(2,1)}, u32[]{:S(2)}) copy-start(bf16[512,128]{1,0:T(8,128)(2,1)} %param.9) | copy-start | bytes 393220
  80.2 17.6 %copy-start.3 = (bf16[128,512]{1,0:T(8,128)(2,1)S(1)}, bf16[128,512]{1,0:T(8,128)(2,1)}, u32[]{:S(2)}) copy-start(bf16[128,512]{1,0:T(8,128)(2,1)} %get-tuple-element.10) | copy-start | bytes 393220
  97.7 1.0 copy-start
  97.7 0.9 copy-start.6

commit v7 on v6

--- a/solution.py
+++ b/solution.py
@@ -250,13 +250,16 @@
     lanes = 128
     tok_tiles = tok_rows // lanes
 
-    spec_rows = spectrum.reshape(2, 2, second_len, ROW_GROUP, chan_width)
-    spec_rows = jnp.transpose(spec_rows, (4, 0, 1, 3, 2)).reshape(seq_count, -1, ROW_GROUP * second_len)
+    half_group = ROW_GROUP // 2
+    spec_rows = spectrum.reshape(2, 2, second_len, half_group, 2, chan_width)
+    spec_rows = jnp.transpose(spec_rows, (5, 0, 1, 3, 4, 2)).astype(jnp.bfloat16)
+    spec_rows = spec_rows.reshape(seq_count, -1, 2 * second_len)
     signal_t, sig_chan, spec_chan = front(
         features.T, pre_gate.T, norm_gain.reshape(chan_width, 1), spec_rows, chans
     )
-    spec_chan = spec_chan.reshape(seq_count, group, 2, 2, ROW_GROUP * second_len)
-    spec_chan = jnp.transpose(spec_chan, (1, 2, 0, 3, 4)).reshape(group, 2, first_len, second_len)
+    spec_chan = spec_chan.reshape(seq_count, group, 2, -1, 2 * second_len)
+    spec_chan = jnp.transpose(spec_chan, (1, 2, 0, 3, 4)).astype(jnp.float32)
+    spec_chan = spec_chan.reshape(group, 2, first_len, second_len)
     sig_chan = jnp.transpose(sig_chan, (1, 0, 2)).reshape(group, half_first, second_len)
     signal = signal_t.T
 

time: 99.8 us -> 87 us (0.87)
  Pallas kernels: 64.6 us -> 53 us
  local copies, waits for them, and re-layouts: 16.3 us -> 14 us
  other arithmetic: 1.15 us -> 2.44 us
    pallas_call x1, Pallas kernels: 47.1 us -> 35.5 us  [front(): pl.pallas_call(front_kernel, out_shape=(jax.ShapeDtypeStruct((width, leng...]
    reshape x4, local copies, waits for them, and re-layouts: 6.89 us -> 5.21 us  [the longest x3 4.08 us: local(): spec_chan = spec_chan.reshape(group, 2, first_len, second_len)]
    transpose x1 -> x0, local copies, waits for them, and re-layouts: 1.32 us -> none  [local(): jnp.transpose(spec_chan, (1, 2, 0, 3, 4))]
    convert_element_type x0 -> x1, other arithmetic: none -> 1.29 us  [local(): jnp.transpose(spec_rows, (5, 0, 1, 3, 4, 2)).astype(jnp.bfloat16)]
where the time goes in v7:
time: 87 us; the launch traced here: 86.7 us
  Pallas kernels  53 us (61%)
  matrix products  17 us (20%)
  local copies, waits for them, and re-layouts  14 us (16%)
  other arithmetic  2.44 us (3%)
    pallas_call x1, Pallas kernels, front(): pl.pallas_call(front_kernel, out_shape=(jax.ShapeDtypeStruct((width, leng...  35.5 us
    pallas_call x1, Pallas kernels, exchange(): pl.pallas_call(exchange_kernel, out_shape=jax.ShapeDtypeStruct(blocks.sha...  17.5 us
    dot_general x12, matrix products, mm(): jnp.einsum(spec, left, right, precision=PRECISE, preferred_element_type=j...  17 us
    unnamed x17, local copies, waits for them, and re-layouts  4.69 us
    reshape x3, local copies, waits for them, and re-layouts, local(): spec_chan = spec_chan.reshape(group, 2, first_len, second_len)  4.08 us

profile of v7, /device:TPU:1, one launch (start us, length us, event | category | flops | bytes accessed | tf_op | source)
XLA Modules:
  0.0 86.7 jit_solution(14486353778813678422)
XLA Ops:
  0.0 1.7 %copy.25 = bf16[512,128]{0,1:T(8,128)(2,1)} copy(bf16[512,128]{1,0:T(8,128)(2,1)} %param.7) | data formatting | bytes 262144 | tf_op args[0]
  1.7 0.8 copy.26
  3.1 0.7 copy.28.gain_ref
  3.9 1.3 %convert_element_type.57 = bf16[2,2,512,128]{3,2,1,0:T(8,128)(2,1)S(1)} convert(f32[2,2,512,128]{3,2,1,0:T(8,128)} %param.12) | non-fusion elementwise | flops 262144 | bytes 1572864 | tf_op jit(solution)/shard_map/convert_element_type | solution.py:255
  5.2 0.7 copy.27
  5.9 1.1 %reshape.80.spec_ref = bf16[64,16,256]{2,1,0:T(8,128)(2,1)} reshape(bf16[128,2,2,2,2,128]{5,4,3,2,1,0:T(2,128)(2,1)S(1)} %bitcast.84) | data formatting | bytes 1048576 | tf_op jit(solution)/shard_map/reshape | solution.py:256
  7.0 35.5 %shard_map.73 = (bf16[128,512]{1,0:T(8,128)(2,1)}, f32[64,2,512]{2,1,0:T(2,128)}, bf16[64,16,256]{2,1,0:T(8,128)(2,1)}) custom-call(bf16[128,512]{1,0:T(8,128)(2,1)} %bitcast.88, bf16[128,512]{1,0:T(8,128)(2,1)} %bitcast.89, f32[128,1]{1,0:T(8,128)} %copy.28.gain_ref, bf16[64,16,256]{2,1,0:T(8,128)(2,1)} %reshape.80.spec_ref), custom_call_target="tpu_custom_call" | custom-call | tf_op jit(solution)/shard_map/pallas_call | solution.py:218
  42.5 1.0 %copy.29 = f32[2,64,512]{2,1,0:T(8,128)S(1)} copy(f32[2,64,512]{2,0,1:T(2,128)} %bitcast.90) | data formatting | bytes 524288 | tf_op jit(solution)/shard_map/transpose | solution.py:263
  44.2 3.1 %fusion = f32[2,512,128]{1,2,0:T(8,128)S(1)} fusion(f32[2,256,128]{2,1,0:T(8,128)S(1)} %reshape.81, s32[512]{0:T(512)S(1)} %copy-done.4), kind=kOutput, calls=%fused_computation.1 | convolution fusion | flops 203292672 | bytes 788480 | tf_op jit(solution)/shard_map/rn,cnm->crm/dot_general | solution.py:35
  47.3 3.2 %convolution_bitcast_fusion = f32[2,512,128]{1,2,0:T(8,128)S(1)} fusion(f32[2,256,128]{2,1,0:T(8,128)S(1)} %reshape.81, s32[512]{0:T(512)S(1)} %copy-done.4), kind=kOutput, calls=%fused_computation.2 | convolution fusion | flops 203161600 | bytes 788480 | tf_op jit(solution)/shard_map/rn,cnm->crm/dot_general | solution.py:35
  50.5 1.0 %fusion.39 = (f32[512,128]{0,1:T(8,128)S(1)}, f32[512,128]{0,1:T(8,128)S(1)}) fusion(s32[512]{0:T(512)S(1)} %copy-done.4), kind=kLoop, calls=%fused_computation.55 | loop fusion | flops 917504 | bytes 526336 | tf_op jit(solution)/shard_map/cos | solution.py:31
  51.6 0.8 fusion.53
  52.4 0.8 convolution_add_fusion.1
  53.2 1.3 %reshape.92 = f32[64,2,2,4,256]{4,3,2,1,0:T(4,128)S(1)} reshape(bf16[64,16,256]{2,1,0:T(8,128)(2,1)} %get-tuple-element.9) | data formatting | bytes 1572864 | tf_op jit(solution)/shard_map/reshape | solution.py:262
  54.5 1.1 %copy.34 = f32[2,2,64,4,256]{4,3,2,0,1:T(4,128)} copy(f32[2,2,64,4,256]{4,3,1,0,2:T(4,128)S(1)} %bitcast.82) | data formatting | bytes 2097152 | tf_op jit(solution)/shard_map/reshape | solution.py:262
  55.7 1.6 %reshape.89 = f32[2,2,512,128]{3,2,0,1:T(8,128)S(1)} reshape(f32[2,2,64,4,256]{4,3,2,0,1:T(4,128)} %copy.34) | data formatting | bytes 2097152 | tf_op jit(solution)/shard_map/reshape | solution.py:262
  57.3 0.8 fusion.51
  58.2 0.8 multiply_subtract_fusion
  61.7 2.4 %fusion.8 = f32[2,128,256]{2,1,0:T(8,128)S(1)} fusion(f32[2,512,128]{1,2,0:T(8,128)S(1)} %convolution_add_fusion, f32[2,512,128]{1,2,0:T(8,128)S(1)} %convolution_subtract_fusion, f32[512,128]{0,1:T(8,128)S(1)} %get-tuple-element.14, f32[512,128]{0,1:T(8,128)S(1)} %get-tuple-element.13, s32[512]{0:T(512)S(1)} %copy-done.4), kind=kOutput, calls=%fused_computation.20 | convolution fusion | flops 203554816 | bytes 1837056 | tf_op jit(solution)/shard_map/rn,crm->cnm/dot_general | solution.py:35
  64.1 2.4 %fusion.2 = f32[2,256,128]{1,2,0:T(8,128)S(1)} fusion(f32[2,128,256]{2,1,0:T(8,128)S(1)} %fusion.8, f32[2,512,128]{1,2,0:T(8,128)S(1)} %convolution_subtract_fusion, f32[2,512,128]{1,2,0:T(8,128)S(1)} %convolution_add_fusion, f32[512,128]{0,1:T(8,128)S(1)} %get-tuple-element.14, f32[512,128]{0,1:T(8,128)S(1)} %get-tuple-element.13, s32[512]{0:T(512)S(1)} %copy-done.4), kind=kOutput, calls=%fused_computation.9 | convolution fusion | flops 203685888 | bytes 2099200 | tf_op jit(solution)/shard_map/rn,crm->cnm/dot_general | solution.py:35
  66.6 0.8 copy.42
  67.3 17.5 %shard_map.74 = f32[64,8,128]{2,1,0:T(8,128)} custom-call(f32[64,8,128]{2,1,0:T(8,128)} %bitcast.87), custom_call_target="tpu_custom_call" | custom-call | tf_op jit(solution)/shard_map/pallas_call | solution.py:84
  85.0 0.8 copy-done
  85.9 0.8 copy.43
  (21 shorter events, 4.3 us)
Async XLA Ops:
  0.0 1.7 %copy-start.1 = (bf16[512,128]{1,0:T(8,128)(2,1)S(1)}, bf16[512,128]{1,0:T(8,128)(2,1)}, u32[]{:S(2)}) copy-start(bf16[512,128]{1,0:T(8,128)(2,1)} %param.8) | copy-start | bytes 393220
  2.5 0.7 copy-start.5
  43.5 0.7 copy-start.4
  67.3 17.5 %copy-start.2 = (bf16[512,128]{1,0:T(8,128)(2,1)S(1)}, bf16[512,128]{1,0:T(8,128)(2,1)}, u32[]{:S(2)}) copy-start(bf16[512,128]{1,0:T(8,128)(2,1)} %param.9) | copy-start | bytes 393220
  67.3 17.7 %copy-start.3 = (bf16[128,512]{1,0:T(8,128)(2,1)S(1)}, bf16[128,512]{1,0:T(8,128)(2,1)}, u32[]{:S(2)}) copy-start(bf16[128,512]{1,0:T(8,128)(2,1)} %get-tuple-element.10) | copy-start | bytes 393220
  84.8 1.0 %copy-start = (f32[64,8,128]{2,1,0:T(8,128)S(1)}, f32[64,8,128]{2,1,0:T(8,128)}, u32[]{:S(2)}) copy-start(f32[64,8,128]{2,1,0:T(8,128)} %shard_map.74) | copy-start | bytes 786436
  84.9 0.9 %copy-start.6 = (f32[128]{0:T(128)S(1)}, f32[128]{0:T(128)}, u32[]{:S(2)}) copy-start(f32[128]{0:T(128)} %param.11) | copy-start | bytes 1540

commit v8 on v7

--- a/solution.py
+++ b/solution.py
@@ -237,6 +237,55 @@
     )(feat_t, gate_t, gain_col, spec_rows)
 
 
+def bin_rows(seq_count):
+    digit_order = reversed_digits(seq_count)
+    stride = 2 * seq_count
+    slots = np.arange(stride)
+    low_bins = 2 * digit_order[slots // 2] + slots % 2
+    return (low_bins[:, None] + stride * np.arange(ROW_GROUP)[None, :]).reshape(-1).astype(np.int32)
+
+
+def convolve(sig_cols, spec_chan, seq_count, tok_rows):
+    group = spec_chan.shape[0]
+    first_len, second_len = spec_chan.shape[2], spec_chan.shape[3]
+    half_first = first_len // 2
+    all_bins = first_len * second_len
+    row_bins = jnp.asarray(bin_rows(seq_count))
+    first_in = jnp.arange(half_first, dtype=jnp.int32)
+    cos_first, sin_first = rotation(row_bins[:, None] * first_in[None, :], first_len)
+    second_in = jnp.arange(second_len, dtype=jnp.int32)
+    cos_twist, sin_twist = rotation(row_bins[:, None] * second_in[None, :], all_bins)
+    cos_second, sin_second = rotation(second_in[:, None] * second_in[None, :], second_len)
+    fwd_second = jnp.concatenate(
+        [jnp.concatenate([cos_second, -sin_second], 1), jnp.concatenate([sin_second, cos_second], 1)], 0
+    )
+    inv_second = jnp.concatenate(
+        [jnp.concatenate([cos_second, sin_second], 1), jnp.concatenate([-sin_second, cos_second], 1)], 0
+    )
+    stacked = jnp.concatenate([cos_first, sin_first], 0)
+    last = jnp.concatenate([cos_first.T, -sin_first.T], 1) * (1.0 / all_bins)
+
+    both = mm("rn,nm->rm", stacked, sig_cols)
+    along_cos, along_sin = both[:first_len], both[first_len:]
+    outs_re, outs_im = [], []
+    for chan in range(group):
+        lanes_of = slice(chan * second_len, (chan + 1) * second_len)
+        p_cos, p_sin = along_cos[:, lanes_of], along_sin[:, lanes_of]
+        twist_re = p_cos * cos_twist - p_sin * sin_twist
+        twist_im = -p_sin * cos_twist - p_cos * sin_twist
+        freq = mm("rn,nk->rk", jnp.concatenate([twist_re, twist_im], 1), fwd_second)
+        freq_re, freq_im = freq[:, :second_len], freq[:, second_len:]
+        filt_re, filt_im = spec_chan[chan, 0], spec_chan[chan, 1]
+        prod_re = freq_re * filt_re - freq_im * filt_im
+        prod_im = freq_re * filt_im + freq_im * filt_re
+        back = mm("rk,kn->rn", jnp.concatenate([prod_re, prod_im], 1), inv_second)
+        back_re, back_im = back[:, :second_len], back[:, second_len:]
+        outs_re.append(back_re * cos_twist - back_im * sin_twist)
+        outs_im.append(back_im * cos_twist + back_re * sin_twist)
+    untwisted = jnp.concatenate([jnp.concatenate(outs_re, 1), jnp.concatenate(outs_im, 1)], 0)
+    return mm("nr,rm->nm", last, untwisted)
+
+
 def local(features, pre_gate, post_gate, norm_gain, skip_weight, spectrum):
     tok_rows, chan_width = features.shape
     seq_count = lax.axis_size("seq")
@@ -260,40 +309,12 @@
     spec_chan = spec_chan.reshape(seq_count, group, 2, -1, 2 * second_len)
     spec_chan = jnp.transpose(spec_chan, (1, 2, 0, 3, 4)).astype(jnp.float32)
     spec_chan = spec_chan.reshape(group, 2, first_len, second_len)
-    sig_chan = jnp.transpose(sig_chan, (1, 0, 2)).reshape(group, half_first, second_len)
+    sig_cols = sig_chan.reshape(seq_count, group, tok_tiles, lanes)
+    sig_cols = jnp.transpose(sig_cols, (0, 2, 1, 3)).reshape(half_first, group * second_len)
     signal = signal_t.T
-
-    digit_order = reversed_digits(seq_count)
-    slots = np.arange(stride)
-    low_bins = 2 * digit_order[slots // 2] + slots % 2
-    row_bins = (low_bins[:, None] + stride * np.arange(ROW_GROUP)[None, :]).reshape(-1)
-    row_bins = jnp.asarray(row_bins.astype(np.int32))
-
-    first_in = jnp.arange(half_first, dtype=jnp.int32)
-    cos_first, sin_first = rotation(row_bins[:, None] * first_in[None, :], first_len)
-    second_in = jnp.arange(second_len, dtype=jnp.int32)
-    cos_twist, sin_twist = rotation(row_bins[:, None] * second_in[None, :], all_bins)
-    cos_second, sin_second = rotation(second_in[:, None] * second_in[None, :], second_len)
-
-    part_re = mm("rn,cnm->crm", cos_first, sig_chan)
-    part_im = -mm("rn,cnm->crm", sin_first, sig_chan)
-    twist_re = part_re * cos_twist + part_im * sin_twist
-    twist_im = part_im * cos_twist - part_re * sin_twist
-    freq_re = mm("crn,nk->crk", twist_re, cos_second) + mm("crn,nk->crk", twist_im, sin_second)
-    freq_im = mm("crn,nk->crk", twist_im, cos_second) - mm("crn,nk->crk", twist_re, sin_second)
-
-    filt_re = spec_chan[:, 0]
-    filt_im = spec_chan[:, 1]
-    prod_re = freq_re * filt_re - freq_im * filt_im
-    prod_im = freq_re * filt_im + freq_im * filt_re
-
-    back_re = mm("crk,kn->crn", prod_re, cos_second) - mm("crk,kn->crn", prod_im, sin_second)
-    back_im = mm("crk,kn->crn", prod_im, cos_second) + mm("crk,kn->crn", prod_re, sin_second)
-    untwist_re = back_re * cos_twist - back_im * sin_twist
-    untwist_im = back_im * cos_twist + back_re * sin_twist
-    conv = mm("rn,crm->cnm", cos_first, untwist_re) - mm("rn,crm->cnm", sin_first, untwist_im)
-    conv = (conv * (1.0 / all_bins)).reshape(group, seq_count, tok_tiles, lanes)
-    conv = jnp.transpose(conv, (1, 0, 2, 3)).reshape(seq_count, -1, lanes)
+    conv = convolve(sig_cols, spec_chan, seq_count, tok_rows)
+    conv = jnp.transpose(conv.reshape(seq_count, tok_tiles, group, lanes), (0, 2, 1, 3))
+    conv = conv.reshape(seq_count, -1, lanes)
     result = exchange(conv, 2).reshape(seq_count, group, tok_tiles, lanes)
     result = jnp.transpose(result, (2, 3, 0, 1)).reshape(tok_rows, chan_width)
     gated = post_gate.astype(jnp.float32) * (result + skip_weight * signal.astype(jnp.float32))

time: 87 us -> 75.6 us (0.87)
  matrix products: 17 us -> 2.88 us
  other arithmetic: 2.44 us -> 8.95 us
  local copies, waits for them, and re-layouts: 14 us -> 10.3 us
    dot_general x12 -> x6, matrix products: 17 us -> 2.88 us  [mm(): jnp.einsum(spec, left, right, precision=PRECISE, preferred_element_type=j...]
    reshape x3, local copies, waits for them, and re-layouts: 4.08 us -> 0.85 us  [local(): spec_chan = spec_chan.reshape(group, 2, first_len, second_len)]
    cos x1 -> x2, other arithmetic: 1.03 us -> 4.19 us  [rotation(): return (jnp.cos(angle), jnp.sin(angle))]
    sub x0 -> x4, other arithmetic: none -> 2.81 us  [the longest x1 1.39 us: convolve(): outs_re.append(back_re * cos_twist - back_im * sin_twist)]
    transpose x2 -> x0, local copies, waits for them, and re-layouts: 1.76 us -> none  [the longest x1 1 us: local(): jnp.transpose(sig_chan, (1, 0, 2)).reshape(group, half_first, second_len)]
    reshape x1 -> x2, local copies, waits for them, and re-layouts: 0.02 us -> 0.9 us  [local(): conv.reshape(seq_count, tok_tiles, group, lanes)]
    unnamed x17 -> x27, local copies, waits for them, and re-layouts: 4.69 us -> 5.06 us
where the time goes in v8:
time: 75.6 us; the launch traced here: 75.3 us
  Pallas kernels  53 us (70%)
  local copies, waits for them, and re-layouts  10.3 us (14%)
  other arithmetic  8.95 us (12%)
  matrix products  2.88 us (4%)
    pallas_call x1, Pallas kernels, front(): pl.pallas_call(front_kernel, out_shape=(jax.ShapeDtypeStruct((width, leng...  35.5 us
    pallas_call x1, Pallas kernels, exchange(): pl.pallas_call(exchange_kernel, out_shape=jax.ShapeDtypeStruct(blocks.sha...  17.5 us
    unnamed x27, local copies, waits for them, and re-layouts  5.06 us
    cos x2, other arithmetic, rotation(): return (jnp.cos(angle), jnp.sin(angle))  4.19 us
    dot_general x6, matrix products, mm(): jnp.einsum(spec, left, right, precision=PRECISE, preferred_element_type=j...  2.88 us

profile of v8, /device:TPU:1, one launch (start us, length us, event | category | flops | bytes accessed | tf_op | source)
XLA Modules:
  0.0 75.3 jit_solution(5109291498672309367)
XLA Ops:
  0.0 1.3 %convert_element_type.56 = bf16[2,2,512,128]{3,2,1,0:T(8,128)(2,1)S(1)} convert(f32[2,2,512,128]{3,2,1,0:T(8,128)} %param.12) | non-fusion elementwise | flops 262144 | bytes 1572864 | tf_op jit(solution)/shard_map/convert_element_type | solution.py:304
  1.3 0.7 copy.18
  2.1 1.1 %reshape.38.spec_ref = bf16[64,16,256]{2,1,0:T(8,128)(2,1)} reshape(bf16[128,2,2,2,2,128]{5,4,3,2,1,0:T(2,128)(2,1)S(1)} %bitcast.64) | data formatting | bytes 1048576 | tf_op jit(solution)/shard_map/reshape | solution.py:305
  3.2 0.8 %copy.16 = bf16[512,128]{0,1:T(8,128)(2,1)} copy(bf16[512,128]{1,0:T(8,128)(2,1)S(1)} %copy-done.3) | data formatting | bytes 262144 | tf_op args[0]
  4.1 0.8 %copy.17 = bf16[512,128]{0,1:T(8,128)(2,1)} copy(bf16[512,128]{1,0:T(8,128)(2,1)S(1)} %copy-done.4) | data formatting | bytes 262144 | tf_op args[1]
  4.9 0.7 copy-done.8
  5.5 0.7 copy.19.gain_ref
  6.3 35.5 %shard_map.73 = (bf16[128,512]{1,0:T(8,128)(2,1)}, f32[64,2,512]{2,1,0:T(2,128)}, bf16[64,16,256]{2,1,0:T(8,128)(2,1)}) custom-call(bf16[128,512]{1,0:T(8,128)(2,1)} %bitcast.67, bf16[128,512]{1,0:T(8,128)(2,1)} %bitcast.68, f32[128,1]{1,0:T(8,128)} %copy.19.gain_ref, bf16[64,16,256]{2,1,0:T(8,128)(2,1)} %reshape.38.spec_ref), custom_call_target="tpu_custom_call" | custom-call | tf_op jit(solution)/shard_map/pallas_call | solution.py:218
  41.7 0.7 copy-done.7
  42.4 2.1 %fusion.59 = (f32[512,256]{1,0:T(8,128)S(1)}, f32[512,256]{1,0:T(8,128)S(1)}) fusion(s32[512]{0:T(512)S(1)} %copy-done.7), kind=kLoop, calls=%fused_computation.92 | loop fusion | flops 1835008 | bytes 1050624 | tf_op jit(solution)/shard_map/cos | solution.py:31
  44.6 0.6 fusion.3
  45.2 1.2 %multiply_subtract_fusion.5 = (f32[512,128]{0,1:T(8,128)S(1)}, f32[512,128]{0,1:T(8,128)S(1)}, f32[512,128]{0,1:T(8,128)S(1)}, f32[512,128]{0,1:T(8,128)S(1)}) fusion(f32[1024,256]{0,1:T(8,128)S(1)} %fusion.3, s32[512]{0:T(512)S(1)} %copy-done.7), kind=kLoop, calls=%fused_computation.88 | loop fusion | flops 1835008 | bytes 2099200 | tf_op jit(solution)/shard_map/sub | solution.py:274
  47.0 0.4 fusion.28
  47.4 0.6 copy-done.1
  48.4 0.4 reshape.48
  49.3 0.4 fusion.32
  50.5 0.4 fusion.24
  51.0 1.4 %multiply_subtract_fusion.3 = (f32[512,128]{0,1:T(8,128)S(1)}, f32[512,128]{0,1:T(8,128)S(1)}, f32[512,128]{0,1:T(8,128)S(1)}, f32[512,128]{0,1:T(8,128)S(1)}) fusion(f32[512,256]{0,1:T(8,128)S(1)} %fusion.24, s32[512]{0:T(512)S(1)} %copy-done.7, f32[512,256]{0,1:T(8,128)S(1)} %fusion.32), kind=kLoop, calls=%fused_computation.86 | loop fusion | flops 1703936 | bytes 2099200 | tf_op jit(solution)/shard_map/sub | solution.py:283
  52.4 2.1 %fusion.60 = (f32[256,512]{1,0:T(8,128)S(1)}, f32[256,512]{1,0:T(8,128)S(1)}) fusion(s32[512]{0:T(512)S(1)} %copy-done.7), kind=kLoop, calls=%fused_computation.93 | loop fusion | flops 1966080 | bytes 1050624 | tf_op jit(solution)/shard_map/cos | solution.py:31
  54.4 0.6 fusion
  55.2 0.8 %copy.26 = f32[64,4,2,128]{3,1,2,0:T(4,128)} copy(f32[64,4,2,128]{3,2,1,0:T(2,128)S(1)} %reshape.43) | data formatting | bytes 524288 | tf_op jit(solution)/shard_map/reshape | solution.py:316
  56.0 17.5 %shard_map.74 = f32[64,8,128]{2,1,0:T(8,128)} custom-call(f32[64,8,128]{2,1,0:T(8,128)} %bitcast.66), custom_call_target="tpu_custom_call" | custom-call | tf_op jit(solution)/shard_map/pallas_call | solution.py:84
  73.6 0.8 %copy-done = f32[64,8,128]{2,1,0:T(8,128)S(1)} copy-done((f32[64,8,128]{2,1,0:T(8,128)S(1)}, f32[64,8,128]{2,1,0:T(8,128)}, u32[]{:S(2)}) %copy-start) | copy-done | bytes 262168
  74.6 0.8 %copy.27 = bf16[512,128]{1,0:T(8,128)(2,1)} copy(bf16[512,128]{0,1:T(8,128)(2,1)S(1)} %fusion.49) | data formatting | bytes 262144 | tf_op jit(solution)/shard_map/convert_element_type | solution.py:321
  (31 shorter events, 2.7 us)
Async XLA Ops:
  2.1 1.2 %copy-start.3 = (bf16[512,128]{1,0:T(8,128)(2,1)S(1)}, bf16[512,128]{1,0:T(8,128)(2,1)}, u32[]{:S(2)}) copy-start(bf16[512,128]{1,0:T(8,128)(2,1)} %param.7) | copy-start | bytes 393220
  3.2 0.9 %copy-start.4 = (bf16[512,128]{1,0:T(8,128)(2,1)S(1)}, bf16[512,128]{1,0:T(8,128)(2,1)}, u32[]{:S(2)}) copy-start(bf16[512,128]{1,0:T(8,128)(2,1)} %param.8) | copy-start | bytes 393220
  4.9 0.7 copy-start.8
  41.7 0.7 copy-start.7
  42.4 2.1 %copy-start.2 = (f32[64,2,512]{2,1,0:T(2,128)S(1)}, f32[64,2,512]{2,1,0:T(2,128)}, u32[]{:S(2)}) copy-start(f32[64,2,512]{2,1,0:T(2,128)} %get-tuple-element.8) | copy-start | bytes 786436
  47.0 1.0 %copy-start.1 = (bf16[64,16,256]{2,1,0:T(8,128)(2,1)S(1)}, bf16[64,16,256]{2,1,0:T(8,128)(2,1)}, u32[]{:S(2)}) copy-start(bf16[64,16,256]{2,1,0:T(8,128)(2,1)} %get-tuple-element.9) | copy-start | bytes 1572868
  56.0 17.5 %copy-start.5 = (bf16[512,128]{1,0:T(8,128)(2,1)S(1)}, bf16[512,128]{1,0:T(8,128)(2,1)}, u32[]{:S(2)}) copy-start(bf16[512,128]{1,0:T(8,128)(2,1)} %param.9) | copy-start | bytes 393220
  56.0 17.7 %copy-start.6 = (bf16[128,512]{1,0:T(8,128)(2,1)S(1)}, bf16[128,512]{1,0:T(8,128)(2,1)}, u32[]{:S(2)}) copy-start(bf16[128,512]{1,0:T(8,128)(2,1)} %get-tuple-element.10) | copy-start | bytes 393220
  73.5 1.0 %copy-start = (f32[64,8,128]{2,1,0:T(8,128)S(1)}, f32[64,8,128]{2,1,0:T(8,128)}, u32[]{:S(2)}) copy-start(f32[64,8,128]{2,1,0:T(8,128)} %shard_map.74) | copy-start | bytes 786436
  73.5 0.9 %copy-start.9 = (f32[128]{0:T(128)S(1)}, f32[128]{0:T(128)}, u32[]{:S(2)}) copy-start(f32[128]{0:T(128)} %param.11) | copy-start | bytes 1540

commit v9 on v8

--- a/solution.py
+++ b/solution.py
@@ -46,7 +46,7 @@
         pl.semaphore_signal(barrier, inc=1, device_id={"seq": peer}, device_id_type=mesh_ids)
         return carry
 
-    lax.fori_loop(1, count, greet, 0)
+    lax.fori_loop(1, count, greet, 0, unroll=True)
     pl.semaphore_wait(barrier, count - 1)
     own = pltpu.make_async_copy(src_ref.at[me], dst_ref.at[me], own_sem)
     own.start()
@@ -66,7 +66,7 @@
         remote(step).start()
         return carry
 
-    lax.fori_loop(1, count, send, 0)
+    lax.fori_loop(1, count, send, 0, unroll=True)
 
     def finish(step, carry):
         copy = remote(step)
@@ -74,7 +74,7 @@
         copy.wait_recv()
         return carry
 
-    lax.fori_loop(1, count, finish, 0)
+    lax.fori_loop(1, count, finish, 0, unroll=True)
     own.wait()
 
 
@@ -112,7 +112,7 @@
         pl.semaphore_signal(barrier, inc=1, device_id={"seq": peer}, device_id_type=mesh_ids)
         return carry
 
-    lax.fori_loop(1, count, greet, 0)
+    lax.fori_loop(1, count, greet, 0, unroll=True)
     for step in range(1, chans):
         peer = lax.rem(mine + step, chans)
         pl.semaphore_signal(barrier, inc=1, device_id={"chan": peer}, device_id_type=mesh_ids)
@@ -136,7 +136,7 @@
         spec_copy(step).start()
         return carry
 
-    lax.fori_loop(1, count, spec_send, 0)
+    lax.fori_loop(1, count, spec_send, 0, unroll=True)
 
     feat = feat_ref[...].astype(jnp.float32)
     part = jnp.sum(feat * feat, axis=0, keepdims=True)
@@ -189,7 +189,7 @@
         sig_copy(step).start()
         return carry
 
-    lax.fori_loop(1, count, sig_start, 0)
+    lax.fori_loop(1, count, sig_start, 0, unroll=True)
 
     def sig_finish(step, carry):
         copy = sig_copy(step)
@@ -197,7 +197,7 @@
         copy.wait_recv()
         return carry
 
-    lax.fori_loop(1, count, sig_finish, 0)
+    lax.fori_loop(1, count, sig_finish, 0, unroll=True)
     sig_own.wait()
 
     def spec_finish(step, carry):
@@ -206,7 +206,7 @@
         copy.wait_recv()
         return carry
 
-    lax.fori_loop(1, count, spec_finish, 0)
+    lax.fori_loop(1, count, spec_finish, 0, unroll=True)
     spec_own.wait()
 
 

time: 75.6 us -> 75.3 us (level)
  no operation moved by 1% of the time
where the time goes in v9:
time: 75.3 us; the launch traced here: 75.1 us
  Pallas kernels  52.7 us (70%)
  local copies, waits for them, and re-layouts  10.3 us (14%)
  other arithmetic  8.95 us (12%)
  matrix products  2.88 us (4%)
    pallas_call x1, Pallas kernels, front(): pl.pallas_call(front_kernel, out_shape=(jax.ShapeDtypeStruct((width, leng...  35 us
    pallas_call x1, Pallas kernels, exchange(): pl.pallas_call(exchange_kernel, out_shape=jax.ShapeDtypeStruct(blocks.sha...  17.7 us
    unnamed x27, local copies, waits for them, and re-layouts  5.06 us
    cos x2, other arithmetic, rotation(): return (jnp.cos(angle), jnp.sin(angle))  4.19 us
    dot_general x6, matrix products, mm(): jnp.einsum(spec, left, right, precision=PRECISE, preferred_element_type=j...  2.88 us

profile of v9, /device:TPU:1, one launch (start us, length us, event | category | flops | bytes accessed | tf_op | source)
XLA Modules:
  0.0 75.1 jit_solution(13840822006259735866)
XLA Ops:
  0.0 1.3 %convert_element_type.56 = bf16[2,2,512,128]{3,2,1,0:T(8,128)(2,1)S(1)} convert(f32[2,2,512,128]{3,2,1,0:T(8,128)} %param.12) | non-fusion elementwise | flops 262144 | bytes 1572864 | tf_op jit(solution)/shard_map/convert_element_type | solution.py:304
  1.3 0.7 copy.18
  2.1 1.1 %reshape.38.spec_ref = bf16[64,16,256]{2,1,0:T(8,128)(2,1)} reshape(bf16[128,2,2,2,2,128]{5,4,3,2,1,0:T(2,128)(2,1)S(1)} %bitcast.64) | data formatting | bytes 1048576 | tf_op jit(solution)/shard_map/reshape | solution.py:305
  3.2 0.8 %copy.16 = bf16[512,128]{0,1:T(8,128)(2,1)} copy(bf16[512,128]{1,0:T(8,128)(2,1)S(1)} %copy-done.3) | data formatting | bytes 262144 | tf_op args[0]
  4.1 0.8 %copy.17 = bf16[512,128]{0,1:T(8,128)(2,1)} copy(bf16[512,128]{1,0:T(8,128)(2,1)S(1)} %copy-done.4) | data formatting | bytes 262144 | tf_op args[1]
  4.9 0.7 copy-done.8
  5.5 0.7 copy.19.gain_ref
  6.3 35.0 %shard_map.73 = (bf16[128,512]{1,0:T(8,128)(2,1)}, f32[64,2,512]{2,1,0:T(2,128)}, bf16[64,16,256]{2,1,0:T(8,128)(2,1)}) custom-call(bf16[128,512]{1,0:T(8,128)(2,1)} %bitcast.67, bf16[128,512]{1,0:T(8,128)(2,1)} %bitcast.68, f32[128,1]{1,0:T(8,128)} %copy.19.gain_ref, bf16[64,16,256]{2,1,0:T(8,128)(2,1)} %reshape.38.spec_ref), custom_call_target="tpu_custom_call" | custom-call | tf_op jit(solution)/shard_map/pallas_call | solution.py:218
  41.3 0.7 copy-done.7
  42.0 2.1 %fusion.59 = (f32[512,256]{1,0:T(8,128)S(1)}, f32[512,256]{1,0:T(8,128)S(1)}) fusion(s32[512]{0:T(512)S(1)} %copy-done.7), kind=kLoop, calls=%fused_computation.92 | loop fusion | flops 1835008 | bytes 1050624 | tf_op jit(solution)/shard_map/cos | solution.py:31
  44.1 0.6 fusion.3
  44.7 1.2 %multiply_subtract_fusion.5 = (f32[512,128]{0,1:T(8,128)S(1)}, f32[512,128]{0,1:T(8,128)S(1)}, f32[512,128]{0,1:T(8,128)S(1)}, f32[512,128]{0,1:T(8,128)S(1)}) fusion(f32[1024,256]{0,1:T(8,128)S(1)} %fusion.3, s32[512]{0:T(512)S(1)} %copy-done.7), kind=kLoop, calls=%fused_computation.88 | loop fusion | flops 1835008 | bytes 2099200 | tf_op jit(solution)/shard_map/sub | solution.py:274
  46.5 0.4 fusion.28
  46.9 0.6 copy-done.1
  48.0 0.4 reshape.48
  48.9 0.4 fusion.32
  49.3 0.4 fusion.20
  50.5 1.4 %multiply_subtract_fusion.3 = (f32[512,128]{0,1:T(8,128)S(1)}, f32[512,128]{0,1:T(8,128)S(1)}, f32[512,128]{0,1:T(8,128)S(1)}, f32[512,128]{0,1:T(8,128)S(1)}) fusion(f32[512,256]{0,1:T(8,128)S(1)} %fusion.24, s32[512]{0:T(512)S(1)} %copy-done.7, f32[512,256]{0,1:T(8,128)S(1)} %fusion.32), kind=kLoop, calls=%fused_computation.86 | loop fusion | flops 1703936 | bytes 2099200 | tf_op jit(solution)/shard_map/sub | solution.py:283
  51.9 2.1 %fusion.60 = (f32[256,512]{1,0:T(8,128)S(1)}, f32[256,512]{1,0:T(8,128)S(1)}) fusion(s32[512]{0:T(512)S(1)} %copy-done.7), kind=kLoop, calls=%fused_computation.93 | loop fusion | flops 1966080 | bytes 1050624 | tf_op jit(solution)/shard_map/cos | solution.py:31
  54.0 0.6 fusion
  54.7 0.8 %copy.26 = f32[64,4,2,128]{3,1,2,0:T(4,128)} copy(f32[64,4,2,128]{3,2,1,0:T(2,128)S(1)} %reshape.43) | data formatting | bytes 524288 | tf_op jit(solution)/shard_map/reshape | solution.py:316
  55.5 17.7 %shard_map.74 = f32[64,8,128]{2,1,0:T(8,128)} custom-call(f32[64,8,128]{2,1,0:T(8,128)} %bitcast.66), custom_call_target="tpu_custom_call" | custom-call | tf_op jit(solution)/shard_map/pallas_call | solution.py:84
  73.4 0.8 %copy-done = f32[64,8,128]{2,1,0:T(8,128)S(1)} copy-done((f32[64,8,128]{2,1,0:T(8,128)S(1)}, f32[64,8,128]{2,1,0:T(8,128)}, u32[]{:S(2)}) %copy-start) | copy-done | bytes 262168
  74.3 0.8 %copy.27 = bf16[512,128]{1,0:T(8,128)(2,1)} copy(bf16[512,128]{0,1:T(8,128)(2,1)S(1)} %fusion.49) | data formatting | bytes 262144 | tf_op jit(solution)/shard_map/convert_element_type | solution.py:321
  (31 shorter events, 2.7 us)
Async XLA Ops:
  2.1 1.2 %copy-start.3 = (bf16[512,128]{1,0:T(8,128)(2,1)S(1)}, bf16[512,128]{1,0:T(8,128)(2,1)}, u32[]{:S(2)}) copy-start(bf16[512,128]{1,0:T(8,128)(2,1)} %param.7) | copy-start | bytes 393220
  3.2 0.9 %copy-start.4 = (bf16[512,128]{1,0:T(8,128)(2,1)S(1)}, bf16[512,128]{1,0:T(8,128)(2,1)}, u32[]{:S(2)}) copy-start(bf16[512,128]{1,0:T(8,128)(2,1)} %param.8) | copy-start | bytes 393220
  4.9 0.7 copy-start.8
  41.3 0.7 copy-start.7
  42.0 2.1 %copy-start.2 = (f32[64,2,512]{2,1,0:T(2,128)S(1)}, f32[64,2,512]{2,1,0:T(2,128)}, u32[]{:S(2)}) copy-start(f32[64,2,512]{2,1,0:T(2,128)} %get-tuple-element.8) | copy-start | bytes 786436
  46.5 1.0 %copy-start.1 = (bf16[64,16,256]{2,1,0:T(8,128)(2,1)S(1)}, bf16[64,16,256]{2,1,0:T(8,128)(2,1)}, u32[]{:S(2)}) copy-start(bf16[64,16,256]{2,1,0:T(8,128)(2,1)} %get-tuple-element.9) | copy-start | bytes 1572868
  55.5 17.7 %copy-start.5 = (bf16[512,128]{1,0:T(8,128)(2,1)S(1)}, bf16[512,128]{1,0:T(8,128)(2,1)}, u32[]{:S(2)}) copy-start(bf16[512,128]{1,0:T(8,128)(2,1)} %param.9) | copy-start | bytes 393220
  55.5 17.9 %copy-start.6 = (bf16[128,512]{1,0:T(8,128)(2,1)S(1)}, bf16[128,512]{1,0:T(8,128)(2,1)}, u32[]{:S(2)}) copy-start(bf16[128,512]{1,0:T(8,128)(2,1)} %get-tuple-element.10) | copy-start | bytes 393220
  73.2 1.0 %copy-start = (f32[64,8,128]{2,1,0:T(8,128)S(1)}, f32[64,8,128]{2,1,0:T(8,128)}, u32[]{:S(2)}) copy-start(f32[64,8,128]{2,1,0:T(8,128)} %shard_map.74) | copy-start | bytes 786436
  73.2 0.9 %copy-start.9 = (f32[128]{0:T(128)S(1)}, f32[128]{0:T(128)}, u32[]{:S(2)}) copy-start(f32[128]{0:T(128)} %param.11) | copy-start | bytes 1540

commit v10 on v9

--- a/solution.py
+++ b/solution.py
@@ -250,11 +250,16 @@
     first_len, second_len = spec_chan.shape[2], spec_chan.shape[3]
     half_first = first_len // 2
     all_bins = first_len * second_len
-    row_bins = jnp.asarray(bin_rows(seq_count))
-    first_in = jnp.arange(half_first, dtype=jnp.int32)
-    cos_first, sin_first = rotation(row_bins[:, None] * first_in[None, :], first_len)
+    row_bins = bin_rows(seq_count).astype(np.int64)
+    first_in = np.arange(half_first)
+    first_turn = (row_bins[:, None] * first_in[None, :]) % first_len * (2.0 * np.pi / first_len)
+    stacked_np = np.concatenate([np.cos(first_turn), np.sin(first_turn)], 0)
+    stacked = jnp.asarray(stacked_np.astype(np.float32))
+    signs = np.concatenate([np.ones(first_len), -np.ones(first_len)]) / all_bins
+    twist_turn = (row_bins[:, None] * np.arange(second_len)[None, :]) % all_bins * (2.0 * np.pi / all_bins)
+    cos_twist = jnp.asarray(np.cos(twist_turn).astype(np.float32))
+    sin_twist = jnp.asarray(np.sin(twist_turn).astype(np.float32))
     second_in = jnp.arange(second_len, dtype=jnp.int32)
-    cos_twist, sin_twist = rotation(row_bins[:, None] * second_in[None, :], all_bins)
     cos_second, sin_second = rotation(second_in[:, None] * second_in[None, :], second_len)
     fwd_second = jnp.concatenate(
         [jnp.concatenate([cos_second, -sin_second], 1), jnp.concatenate([sin_second, cos_second], 1)], 0
@@ -262,8 +267,7 @@
     inv_second = jnp.concatenate(
         [jnp.concatenate([cos_second, sin_second], 1), jnp.concatenate([-sin_second, cos_second], 1)], 0
     )
-    stacked = jnp.concatenate([cos_first, sin_first], 0)
-    last = jnp.concatenate([cos_first.T, -sin_first.T], 1) * (1.0 / all_bins)
+    last = stacked * jnp.asarray(signs.astype(np.float32))[:, None]
 
     both = mm("rn,nm->rm", stacked, sig_cols)
     along_cos, along_sin = both[:first_len], both[first_len:]
@@ -283,7 +287,7 @@
         outs_re.append(back_re * cos_twist - back_im * sin_twist)
         outs_im.append(back_im * cos_twist + back_re * sin_twist)
     untwisted = jnp.concatenate([jnp.concatenate(outs_re, 1), jnp.concatenate(outs_im, 1)], 0)
-    return mm("nr,rm->nm", last, untwisted)
+    return mm("rn,rm->nm", last, untwisted)
 
 
 def local(features, pre_gate, post_gate, norm_gain, skip_weight, spectrum):

time: 75.3 us -> 73.3 us (0.973)
  other arithmetic: 8.95 us -> 2.52 us
  local copies, waits for them, and re-layouts: 10.3 us -> 13 us
  matrix products: 2.88 us -> 4.45 us
    cos x2 -> x0, other arithmetic: 4.19 us -> none  [rotation(): return (jnp.cos(angle), jnp.sin(angle))]
    unnamed x27 -> x29, local copies, waits for them, and re-layouts: 5.06 us -> 6.8 us
    dot_general x6 -> x7, matrix products: 2.88 us -> 4.45 us  [mm(): jnp.einsum(spec, left, right, precision=PRECISE, preferred_element_type=j...]
    sub x1 -> x0, other arithmetic: 1.39 us -> none  [convolve(): outs_re.append(back_re * cos_twist - back_im * sin_twist)]
    reshape x3, local copies, waits for them, and re-layouts: 0.85 us -> 1.89 us  [local(): spec_chan = spec_chan.reshape(group, 2, first_len, second_len)]
    sub x1, other arithmetic: 1.22 us -> 0.19 us  [convolve(): twist_re = p_cos * cos_twist - p_sin * sin_twist]
where the time goes in v10:
time: 73.3 us; the launch traced here: 72.9 us
  Pallas kernels  52.7 us (72%)
  local copies, waits for them, and re-layouts  13 us (18%)
  matrix products  4.45 us (6%)
  other arithmetic  2.52 us (3%)
    pallas_call x1, Pallas kernels, front(): pl.pallas_call(front_kernel, out_shape=(jax.ShapeDtypeStruct((width, leng...  35 us
    pallas_call x1, Pallas kernels, exchange(): pl.pallas_call(exchange_kernel, out_shape=jax.ShapeDtypeStruct(blocks.sha...  17.7 us
    unnamed x29, local copies, waits for them, and re-layouts  6.8 us
    dot_general x7, matrix products, mm(): jnp.einsum(spec, left, right, precision=PRECISE, preferred_element_type=j...  4.45 us
    reshape x3, local copies, waits for them, and re-layouts, local(): spec_chan = spec_chan.reshape(group, 2, first_len, second_len)  1.89 us

profile of v10, /device:TPU:1, one launch (start us, length us, event | category | flops | bytes accessed | tf_op | source)
XLA Modules:
  0.0 72.9 jit_solution(12809001559493138199)
XLA Ops:
  0.0 1.7 %copy.19 = bf16[512,128]{0,1:T(8,128)(2,1)} copy(bf16[512,128]{1,0:T(8,128)(2,1)} %param.10) | data formatting | bytes 262144 | tf_op args[0]
  1.7 0.8 %copy.20 = bf16[512,128]{0,1:T(8,128)(2,1)} copy(bf16[512,128]{1,0:T(8,128)(2,1)S(1)} %copy-done.6) | data formatting | bytes 262144 | tf_op args[1]
  2.5 0.7 copy-done.9
  3.1 0.7 copy.22.gain_ref
  3.9 1.3 %convert_element_type.44 = bf16[2,2,512,128]{3,2,1,0:T(8,128)(2,1)S(1)} convert(f32[2,2,512,128]{3,2,1,0:T(8,128)} %param.15) | non-fusion elementwise | flops 262144 | bytes 1572864 | tf_op jit(solution)/shard_map/convert_element_type | solution.py:308
  5.2 0.7 %copy.21 = bf16[2,2,128,2,2,128]{2,4,3,1,0,5:T(2,128)(2,1)S(1)} copy(bf16[2,2,128,2,2,128]{5,4,3,2,1,0:T(2,128)(2,1)S(1)} %bitcast.66) | data formatting | bytes 1048576 | tf_op jit(solution)/shard_map/convert_element_type | solution.py:308
  5.9 1.1 %reshape.38.spec_ref = bf16[64,16,256]{2,1,0:T(8,128)(2,1)} reshape(bf16[128,2,2,2,2,128]{5,4,3,2,1,0:T(2,128)(2,1)S(1)} %bitcast.67) | data formatting | bytes 1048576 | tf_op jit(solution)/shard_map/reshape | solution.py:309
  7.0 35.0 %shard_map.100 = (bf16[128,512]{1,0:T(8,128)(2,1)}, f32[64,2,512]{2,1,0:T(2,128)}, bf16[64,16,256]{2,1,0:T(8,128)(2,1)}) custom-call(bf16[128,512]{1,0:T(8,128)(2,1)} %bitcast.70, bf16[128,512]{1,0:T(8,128)(2,1)} %bitcast.71, f32[128,1]{1,0:T(8,128)} %copy.22.gain_ref, bf16[64,16,256]{2,1,0:T(8,128)(2,1)} %reshape.38.spec_ref), custom_call_target="tpu_custom_call" | custom-call | tf_op jit(solution)/shard_map/pallas_call | solution.py:218
  42.0 1.3 %reshape.51 = f32[64,2,2,4,256]{4,3,2,1,0:T(4,128)S(1)} reshape(bf16[64,16,256]{2,1,0:T(8,128)(2,1)} %get-tuple-element.9) | data formatting | bytes 1572864 | tf_op jit(solution)/shard_map/reshape | solution.py:315
  43.5 0.4 reshape.48
  44.3 0.9 %copy-done.2 = f32[1024,256]{1,0:T(8,128)S(1)} copy-done((f32[1024,256]{1,0:T(8,128)S(1)}, f32[1024,256]{1,0:T(8,128)}, u32[]{:S(2)}) %copy-start.2) | copy-done | bytes 1048600
  45.3 1.6 %fusion.27 = f32[1024,256]{0,1:T(8,128)S(1)} fusion(f32[1024,256]{1,0:T(8,128)S(1)} %copy-done.2, f32[32,8,2,128]{3,2,1,0:T(2,128)} %bitcast.72), kind=kOutput, calls=%fused_computation.34 | convolution fusion | flops 402653184 | bytes 2359296 | tf_op jit(solution)/shard_map/rn,nm->rm/dot_general | solution.py:35
  47.7 0.4 fusion
  48.2 0.4 fusion.4
  48.9 0.4 fusion.8
  49.4 0.4 fusion.12
  50.0 0.8 %copy-done.5 = f32[512,256]{1,0:T(8,128)S(1)} copy-done((f32[512,256]{1,0:T(8,128)S(1)}, f32[512,256]{1,0:T(8,128)}, u32[]{:S(2)}) %copy-start.5) | copy-done | bytes 524312
  50.9 0.6 fusion.16
  51.5 0.4 copy-done.4
  51.9 0.6 convolution_add_fusion
  52.7 0.8 %copy.29 = f32[64,4,2,128]{3,1,2,0:T(4,128)} copy(f32[64,4,2,128]{3,2,1,0:T(2,128)S(1)} %reshape.43) | data formatting | bytes 524288 | tf_op jit(solution)/shard_map/reshape | solution.py:320
  53.4 17.7 %shard_map.101 = f32[64,8,128]{2,1,0:T(8,128)} custom-call(f32[64,8,128]{2,1,0:T(8,128)} %bitcast.69), custom_call_target="tpu_custom_call" | custom-call | tf_op jit(solution)/shard_map/pallas_call | solution.py:84
  71.3 0.8 %copy-done.3 = f32[64,8,128]{2,1,0:T(8,128)S(1)} copy-done((f32[64,8,128]{2,1,0:T(8,128)S(1)}, f32[64,8,128]{2,1,0:T(8,128)}, u32[]{:S(2)}) %copy-start.3) | copy-done | bytes 262168
  72.2 0.8 %copy.30 = bf16[512,128]{1,0:T(8,128)(2,1)} copy(bf16[512,128]{0,1:T(8,128)(2,1)S(1)} %fusion.26) | data formatting | bytes 262144 | tf_op jit(solution)/shard_map/convert_element_type | solution.py:325
  (32 shorter events, 2.3 us)
Async XLA Ops:
  0.0 1.7 %copy-start.6 = (bf16[512,128]{1,0:T(8,128)(2,1)S(1)}, bf16[512,128]{1,0:T(8,128)(2,1)}, u32[]{:S(2)}) copy-start(bf16[512,128]{1,0:T(8,128)(2,1)} %param.11) | copy-start | bytes 393220
  2.5 0.7 copy-start.9
  44.0 1.2 %copy-start.2 = (f32[1024,256]{1,0:T(8,128)S(1)}, f32[1024,256]{1,0:T(8,128)}, u32[]{:S(2)}) copy-start(f32[1024,256]{1,0:T(8,128)} %constant.25.clone) | copy-start | bytes 3145732
  45.3 1.6 %copy-start = (f32[512,128]{0,1:T(8,128)S(1)}, f32[512,128]{0,1:T(8,128)}, u32[]{:S(2)}) copy-start(f32[512,128]{0,1:T(8,128)} %constant.27.clone) | copy-start | bytes 786436
  45.3 1.6 %copy-start.1 = (f32[512,128]{0,1:T(8,128)S(1)}, f32[512,128]{0,1:T(8,128)}, u32[]{:S(2)}) copy-start(f32[512,128]{0,1:T(8,128)} %constant.26.clone) | copy-start | bytes 786436
  49.8 1.0 %copy-start.5 = (f32[512,256]{1,0:T(8,128)S(1)}, f32[512,256]{1,0:T(8,128)}, u32[]{:S(2)}) copy-start(f32[512,256]{1,0:T(8,128)} %constant.31) | copy-start | bytes 1572868
  50.9 1.0 %copy-start.4 = (f32[512,256]{1,0:T(8,128)S(1)}, f32[512,256]{1,0:T(8,128)}, u32[]{:S(2)}) copy-start(f32[512,256]{1,0:T(8,128)} %constant.32) | copy-start | bytes 1572868
  53.4 17.7 %copy-start.7 = (bf16[512,128]{1,0:T(8,128)(2,1)S(1)}, bf16[512,128]{1,0:T(8,128)(2,1)}, u32[]{:S(2)}) copy-start(bf16[512,128]{1,0:T(8,128)(2,1)} %param.12) | copy-start | bytes 393220
  53.4 17.8 %copy-start.8 = (bf16[128,512]{1,0:T(8,128)(2,1)S(1)}, bf16[128,512]{1,0:T(8,128)(2,1)}, u32[]{:S(2)}) copy-start(bf16[128,512]{1,0:T(8,128)(2,1)} %get-tuple-element.10) | copy-start | bytes 393220
  71.1 1.0 %copy-start.3 = (f32[64,8,128]{2,1,0:T(8,128)S(1)}, f32[64,8,128]{2,1,0:T(8,128)}, u32[]{:S(2)}) copy-start(f32[64,8,128]{2,1,0:T(8,128)} %shard_map.101) | copy-start | bytes 786436
  71.1 0.9 %copy-start.10 = (f32[128]{0:T(128)S(1)}, f32[128]{0:T(128)}, u32[]{:S(2)}) copy-start(f32[128]{0:T(128)} %param.14) | copy-start | bytes 1540

commit v11 on v10

--- a/solution.py
+++ b/solution.py
@@ -139,7 +139,7 @@
     lax.fori_loop(1, count, spec_send, 0, unroll=True)
 
     feat = feat_ref[...].astype(jnp.float32)
-    part = jnp.sum(feat * feat, axis=0, keepdims=True)
+    part = jnp.sum(jnp.transpose(feat * feat), axis=0, keepdims=True)
     sq_mine[...] = jnp.broadcast_to(part, sq_mine.shape)
 
     def chan_copy(step):
@@ -164,9 +164,10 @@
         other = lax.rem(mine + step, chans)
         total = total + sq_recv[other][0:1, :]
     scale = lax.rsqrt(total / CHANNELS + 1e-06)
+    scale = jnp.transpose(jnp.broadcast_to(scale, (8, scale.shape[1])))[:, 0:1]
     signal = (feat * scale * gain_ref[...] * gate_ref[...].astype(jnp.float32)).astype(jnp.bfloat16)
     sig_out[...] = signal
-    wide = signal.astype(jnp.float32)
+    wide = jnp.transpose(signal.astype(jnp.float32))
     pair = sig_send.shape[1]
     for peer in range(count):
         sig_send[peer] = wide[pair * peer:pair * peer + pair, :]
@@ -210,15 +211,15 @@
     spec_own.wait()
 
 
-def front(feat_t, gate_t, gain_col, spec_rows, chans):
+def front(feat, gate, gain_row, spec_rows, chans):
     count = spec_rows.shape[0]
-    width, length = feat_t.shape
+    length, width = feat.shape
     pair = width // count
     vmem = pl.BlockSpec(memory_space=pltpu.VMEM)
     return pl.pallas_call(
         front_kernel,
         out_shape=(
-            jax.ShapeDtypeStruct((width, length), jnp.bfloat16),
+            jax.ShapeDtypeStruct((length, width), jnp.bfloat16),
             jax.ShapeDtypeStruct((count, pair, length), jnp.float32),
             jax.ShapeDtypeStruct(spec_rows.shape, spec_rows.dtype),
         ),
@@ -234,7 +235,7 @@
             pltpu.SemaphoreType.DMA((2,)),
         ],
         compiler_params=pltpu.CompilerParams(collective_id=0, has_side_effects=True),
-    )(feat_t, gate_t, gain_col, spec_rows)
+    )(feat, gate, gain_row, spec_rows)
 
 
 def bin_rows(seq_count):
@@ -307,15 +308,14 @@
     spec_rows = spectrum.reshape(2, 2, second_len, half_group, 2, chan_width)
     spec_rows = jnp.transpose(spec_rows, (5, 0, 1, 3, 4, 2)).astype(jnp.bfloat16)
     spec_rows = spec_rows.reshape(seq_count, -1, 2 * second_len)
-    signal_t, sig_chan, spec_chan = front(
-        features.T, pre_gate.T, norm_gain.reshape(chan_width, 1), spec_rows, chans
+    signal, sig_chan, spec_chan = front(
+        features, pre_gate, norm_gain.reshape(1, chan_width), spec_rows, chans
     )
     spec_chan = spec_chan.reshape(seq_count, group, 2, -1, 2 * second_len)
     spec_chan = jnp.transpose(spec_chan, (1, 2, 0, 3, 4)).astype(jnp.float32)
     spec_chan = spec_chan.reshape(group, 2, first_len, second_len)
     sig_cols = sig_chan.reshape(seq_count, group, tok_tiles, lanes)
     sig_cols = jnp.transpose(sig_cols, (0, 2, 1, 3)).reshape(half_first, group * second_len)
-    signal = signal_t.T
     conv = convolve(sig_cols, spec_chan, seq_count, tok_rows)
     conv = jnp.transpose(conv.reshape(seq_count, tok_tiles, group, lanes), (0, 2, 1, 3))
     conv = conv.reshape(seq_count, -1, lanes)

time: 73.3 us -> 70.3 us (0.959)
  local copies, waits for them, and re-layouts: 13 us -> 9.41 us
    unnamed x29 -> x21, local copies, waits for them, and re-layouts: 6.8 us -> 4.55 us
    convert_element_type x1 -> x0, local copies, waits for them, and re-layouts: 0.76 us -> none  [local(): return gated.astype(jnp.bfloat16)]
where the time goes in v11:
time: 70.3 us; the launch traced here: 69.9 us
  Pallas kernels  52.6 us (75%)
  local copies, waits for them, and re-layouts  9.41 us (13%)
  matrix products  4.45 us (6%)
  other arithmetic  3.12 us (4%)
    pallas_call x1, Pallas kernels, front(): pl.pallas_call(front_kernel, out_shape=(jax.ShapeDtypeStruct((length, wid...  35 us
    pallas_call x1, Pallas kernels, exchange(): pl.pallas_call(exchange_kernel, out_shape=jax.ShapeDtypeStruct(blocks.sha...  17.7 us
    unnamed x21, local copies, waits for them, and re-layouts  4.55 us
    dot_general x7, matrix products, mm(): jnp.einsum(spec, left, right, precision=PRECISE, preferred_element_type=j...  4.45 us
    reshape x3, local copies, waits for them, and re-layouts, local(): spec_chan = spec_chan.reshape(group, 2, first_len, second_len)  1.89 us

profile of v11, /device:TPU:1, one launch (start us, length us, event | category | flops | bytes accessed | tf_op | source)
XLA Modules:
  0.0 69.9 jit_solution(15549724175509469163)
XLA Ops:
  0.0 1.3 %convert_element_type.43 = bf16[2,2,512,128]{3,2,1,0:T(8,128)(2,1)S(1)} convert(f32[2,2,512,128]{3,2,1,0:T(8,128)} %param.15) | non-fusion elementwise | flops 262144 | bytes 1572864 | tf_op jit(solution)/shard_map/convert_element_type | solution.py:309
  1.3 0.7 %copy.14 = bf16[2,2,128,2,2,128]{2,4,3,1,0,5:T(2,128)(2,1)S(1)} copy(bf16[2,2,128,2,2,128]{5,4,3,2,1,0:T(2,128)(2,1)S(1)} %bitcast.59) | data formatting | bytes 1048576 | tf_op jit(solution)/shard_map/convert_element_type | solution.py:309
  2.1 1.1 %reshape.38.spec_ref = bf16[64,16,256]{2,1,0:T(8,128)(2,1)} reshape(bf16[128,2,2,2,2,128]{5,4,3,2,1,0:T(2,128)(2,1)S(1)} %bitcast.60) | data formatting | bytes 1048576 | tf_op jit(solution)/shard_map/reshape | solution.py:310
  3.2 35.0 %shard_map.100 = (bf16[512,128]{1,0:T(8,128)(2,1)}, f32[64,2,512]{2,1,0:T(2,128)}, bf16[64,16,256]{2,1,0:T(8,128)(2,1)}) custom-call(bf16[512,128]{1,0:T(8,128)(2,1)} %feat_ref.1, bf16[512,128]{1,0:T(8,128)(2,1)} %gate_ref.1, f32[1,128]{1,0:T(1,128)} %bitcast.65, bf16[64,16,256]{2,1,0:T(8,128)(2,1)} %reshape.38.spec_ref), custom_call_target="tpu_custom_call" | custom-call | tf_op jit(solution)/shard_map/pallas_call | solution.py:219
  38.1 1.3 %reshape.51 = f32[64,2,2,4,256]{4,3,2,1,0:T(4,128)S(1)} reshape(bf16[64,16,256]{2,1,0:T(8,128)(2,1)} %get-tuple-element.9) | data formatting | bytes 1572864 | tf_op jit(solution)/shard_map/reshape | solution.py:316
  39.6 0.4 reshape.48
  40.4 0.9 %copy-done.2 = f32[1024,256]{1,0:T(8,128)S(1)} copy-done((f32[1024,256]{1,0:T(8,128)S(1)}, f32[1024,256]{1,0:T(8,128)}, u32[]{:S(2)}) %copy-start.2) | copy-done | bytes 1048600
  41.4 1.6 %fusion.25 = f32[1024,256]{0,1:T(8,128)S(1)} fusion(f32[1024,256]{1,0:T(8,128)S(1)} %copy-done.2, f32[32,8,2,128]{3,2,1,0:T(2,128)} %bitcast.64), kind=kOutput, calls=%fused_computation.32 | convolution fusion | flops 402653184 | bytes 2359296 | tf_op jit(solution)/shard_map/rn,nm->rm/dot_general | solution.py:35
  43.0 0.2 multiply_subtract_fusion.5
  43.2 0.3 fusion.42
  43.5 0.3 fusion.44
  43.8 0.4 fusion
  44.3 0.4 fusion.4
  45.0 0.4 fusion.8
  45.5 0.4 fusion.12
  46.1 0.8 %copy-done.4 = f32[512,256]{1,0:T(8,128)S(1)} copy-done((f32[512,256]{1,0:T(8,128)S(1)}, f32[512,256]{1,0:T(8,128)}, u32[]{:S(2)}) %copy-start.4) | copy-done | bytes 524312
  47.0 0.6 fusion.16
  47.6 0.4 copy-done.3
  48.0 0.6 convolution_add_fusion
  48.8 0.8 %copy.21 = f32[64,4,2,128]{3,1,2,0:T(4,128)} copy(f32[64,4,2,128]{3,2,1,0:T(2,128)S(1)} %reshape.43) | data formatting | bytes 524288 | tf_op jit(solution)/shard_map/reshape | solution.py:320
  49.5 17.7 %shard_map.101 = f32[64,8,128]{2,1,0:T(8,128)} custom-call(f32[64,8,128]{2,1,0:T(8,128)} %bitcast.61), custom_call_target="tpu_custom_call" | custom-call | tf_op jit(solution)/shard_map/pallas_call | solution.py:84
  67.2 1.0 %copy.36 = f32[16,8,4,128]{3,1,2,0:T(8,128)S(1)} copy(f32[16,8,4,128]{3,2,1,0:T(4,128)} %bitcast.62) | data formatting | bytes 524288
  68.4 0.7 %copy-done.5 = bf16[512,128]{1,0:T(8,128)(2,1)S(1)} copy-done((bf16[512,128]{1,0:T(8,128)(2,1)S(1)}, bf16[512,128]{1,0:T(8,128)(2,1)}, u32[]{:S(2)}) %copy-start.5) | copy-done | bytes 131096
  69.2 0.7 %multiply_convert_fusion = bf16[512,128]{1,0:T(8,128)(2,1)} fusion(f32[512,128]{1,0:T(8,128)S(1)} %copy.22, bf16[512,128]{1,0:T(8,128)(2,1)S(1)} %copy-done.6, bf16[512,128]{1,0:T(8,128)(2,1)S(1)} %copy-done.5, f32[128]{0:T(128)S(1)} %copy-done.7), kind=kLoop, calls=%fused_computation.47 | loop fusion | flops 393216 | bytes 655872 | tf_op jit(solution)/shard_map/convert_element_type | solution.py:325
  (23 shorter events, 1.5 us)
Async XLA Ops:
  40.1 1.2 %copy-start.2 = (f32[1024,256]{1,0:T(8,128)S(1)}, f32[1024,256]{1,0:T(8,128)}, u32[]{:S(2)}) copy-start(f32[1024,256]{1,0:T(8,128)} %constant.25.clone) | copy-start | bytes 3145732
  41.4 1.6 %copy-start = (f32[512,128]{0,1:T(8,128)S(1)}, f32[512,128]{0,1:T(8,128)}, u32[]{:S(2)}) copy-start(f32[512,128]{0,1:T(8,128)} %constant.27.clone) | copy-start | bytes 786436
  41.4 1.6 %copy-start.1 = (f32[512,128]{0,1:T(8,128)S(1)}, f32[512,128]{0,1:T(8,128)}, u32[]{:S(2)}) copy-start(f32[512,128]{0,1:T(8,128)} %constant.26.clone) | copy-start | bytes 786436
  45.9 1.0 %copy-start.4 = (f32[512,256]{1,0:T(8,128)S(1)}, f32[512,256]{1,0:T(8,128)}, u32[]{:S(2)}) copy-start(f32[512,256]{1,0:T(8,128)} %constant.31) | copy-start | bytes 1572868
  47.0 1.0 %copy-start.3 = (f32[512,256]{1,0:T(8,128)S(1)}, f32[512,256]{1,0:T(8,128)}, u32[]{:S(2)}) copy-start(f32[512,256]{1,0:T(8,128)} %constant.32) | copy-start | bytes 1572868
  68.2 0.9 %copy-start.5 = (bf16[512,128]{1,0:T(8,128)(2,1)S(1)}, bf16[512,128]{1,0:T(8,128)(2,1)}, u32[]{:S(2)}) copy-start(bf16[512,128]{1,0:T(8,128)(2,1)} %param.12) | copy-start | bytes 393220
  68.2 1.0 %copy-start.6 = (bf16[512,128]{1,0:T(8,128)(2,1)S(1)}, bf16[512,128]{1,0:T(8,128)(2,1)}, u32[]{:S(2)}) copy-start(bf16[512,128]{1,0:T(8,128)(2,1)} %get-tuple-element.10) | copy-start | bytes 393220
  68.3 0.8 %copy-start.7 = (f32[128]{0:T(128)S(1)}, f32[128]{0:T(128)}, u32[]{:S(2)}) copy-start(f32[128]{0:T(128)} %param.14) | copy-start | bytes 1540

commit v12 on v11

--- a/solution.py
+++ b/solution.py
@@ -98,7 +98,7 @@
 def front_kernel(
     feat_ref, gate_ref, gain_ref, spec_ref,
     sig_out, sig_recv, spec_recv,
-    sq_mine, sq_recv, sig_send, spec_sems, sig_sems, chan_sems, own_sems,
+    sq_mine, sq_recv, sig_turn, sig_send, spec_sems, sig_sems, chan_sems, own_sems,
 ):
     count = spec_ref.shape[0]
     chans = sq_recv.shape[0]
@@ -167,15 +167,24 @@
     scale = jnp.transpose(jnp.broadcast_to(scale, (8, scale.shape[1])))[:, 0:1]
     signal = (feat * scale * gain_ref[...] * gate_ref[...].astype(jnp.float32)).astype(jnp.bfloat16)
     sig_out[...] = signal
-    wide = jnp.transpose(signal.astype(jnp.float32))
-    pair = sig_send.shape[1]
-    for peer in range(count):
-        sig_send[peer] = wide[pair * peer:pair * peer + pair, :]
+    wide = signal.astype(jnp.float32)
+    lanes = wide.shape[1]
+    pair = lanes // count
+    tiles = wide.shape[0] // lanes
+    chunk = pair * tiles
+    for tile in range(tiles):
+        sig_turn[...] = jnp.transpose(wide[lanes * tile:lanes * (tile + 1), :])
+        for chan in range(pair):
+            rows = sig_turn[pl.ds(chan, count, stride=pair), :]
+            sig_send[pl.ds(tiles * chan + tile, count, stride=chunk), :] = rows
+
+    def sig_rows(peer):
+        return sig_send.at[pl.ds(pl.multiple_of(peer * chunk, chunk), chunk)]
 
     def sig_copy(step):
         peer = lax.rem(me + step, count)
         return pltpu.make_async_remote_copy(
-            sig_send.at[peer],
+            sig_rows(peer),
             sig_recv.at[me],
             sig_sems.at[0, step],
             sig_sems.at[1, step],
@@ -183,7 +192,7 @@
             device_id_type=mesh_ids,
         )
 
-    sig_own = pltpu.make_async_copy(sig_send.at[me], sig_recv.at[me], own_sems.at[1])
+    sig_own = pltpu.make_async_copy(sig_rows(me), sig_recv.at[me], own_sems.at[1])
     sig_own.start()
 
     def sig_start(step, carry):
@@ -220,7 +229,7 @@
         front_kernel,
         out_shape=(
             jax.ShapeDtypeStruct((length, width), jnp.bfloat16),
-            jax.ShapeDtypeStruct((count, pair, length), jnp.float32),
+            jax.ShapeDtypeStruct((count, pair * length // 128, 128), jnp.float32),
             jax.ShapeDtypeStruct(spec_rows.shape, spec_rows.dtype),
         ),
         in_specs=[vmem] * 4,
@@ -228,7 +237,8 @@
         scratch_shapes=[
             pltpu.VMEM((8, length), jnp.float32),
             pltpu.VMEM((chans, 8, length), jnp.float32),
-            pltpu.VMEM((count, pair, length), jnp.float32),
+            pltpu.VMEM((128, 128), jnp.float32),
+            pltpu.VMEM((count * pair * length // 128, 128), jnp.float32),
             pltpu.SemaphoreType.DMA((2, count)),
             pltpu.SemaphoreType.DMA((2, count)),
             pltpu.SemaphoreType.DMA((2, chans)),

time: 70.3 us -> 69.8 us (level)
  matrix products: 4.45 us -> 3.45 us
    reshape x0 -> x1, local copies, waits for them, and re-layouts: none -> 1.12 us  [local(): sig_cols = sig_chan.reshape(seq_count, group, tok_tiles, lanes)]
    dot_general x7, matrix products: 4.45 us -> 3.45 us  [mm(): jnp.einsum(spec, left, right, precision=PRECISE, preferred_element_type=j...]
where the time goes in v12:
time: 69.8 us; the launch traced here: 69.4 us
  Pallas kernels  52.6 us (75%)
  local copies, waits for them, and re-layouts  9.97 us (14%)
  matrix products  3.45 us (5%)
  other arithmetic  3.11 us (4%)
    pallas_call x1, Pallas kernels, front(): pl.pallas_call(front_kernel, out_shape=(jax.ShapeDtypeStruct((length, wid...  35 us
    pallas_call x1, Pallas kernels, exchange(): pl.pallas_call(exchange_kernel, out_shape=jax.ShapeDtypeStruct(blocks.sha...  17.7 us
    unnamed x21, local copies, waits for them, and re-layouts  3.98 us
    dot_general x7, matrix products, mm(): jnp.einsum(spec, left, right, precision=PRECISE, preferred_element_type=j...  3.45 us
    reshape x3, local copies, waits for them, and re-layouts, local(): spec_chan = spec_chan.reshape(group, 2, first_len, second_len)  1.89 us

profile of v12, /device:TPU:1, one launch (start us, length us, event | category | flops | bytes accessed | tf_op | source)
XLA Modules:
  0.0 69.4 jit_solution(7407654577791210697)
XLA Ops:
  0.0 1.3 %convert_element_type.43 = bf16[2,2,512,128]{3,2,1,0:T(8,128)(2,1)S(1)} convert(f32[2,2,512,128]{3,2,1,0:T(8,128)} %param.15) | non-fusion elementwise | flops 262144 | bytes 1572864 | tf_op jit(solution)/shard_map/convert_element_type | solution.py:319
  1.3 0.7 %copy.14 = bf16[2,2,128,2,2,128]{2,4,3,1,0,5:T(2,128)(2,1)S(1)} copy(bf16[2,2,128,2,2,128]{5,4,3,2,1,0:T(2,128)(2,1)S(1)} %bitcast.58) | data formatting | bytes 1048576 | tf_op jit(solution)/shard_map/convert_element_type | solution.py:319
  2.1 1.1 %reshape.38.spec_ref = bf16[64,16,256]{2,1,0:T(8,128)(2,1)} reshape(bf16[128,2,2,2,2,128]{5,4,3,2,1,0:T(2,128)(2,1)S(1)} %bitcast.59) | data formatting | bytes 1048576 | tf_op jit(solution)/shard_map/reshape | solution.py:320
  3.2 35.0 %shard_map.100 = (bf16[512,128]{1,0:T(8,128)(2,1)}, f32[64,8,128]{2,1,0:T(8,128)}, bf16[64,16,256]{2,1,0:T(8,128)(2,1)}) custom-call(bf16[512,128]{1,0:T(8,128)(2,1)} %feat_ref.1, bf16[512,128]{1,0:T(8,128)(2,1)} %gate_ref.1, f32[1,128]{1,0:T(1,128)} %bitcast.65, bf16[64,16,256]{2,1,0:T(8,128)(2,1)} %reshape.38.spec_ref), custom_call_target="tpu_custom_call" | custom-call | tf_op jit(solution)/shard_map/pallas_call | solution.py:228
  38.1 1.3 %reshape.51 = f32[64,2,2,4,256]{4,3,2,1,0:T(4,128)S(1)} reshape(bf16[64,16,256]{2,1,0:T(8,128)(2,1)} %get-tuple-element.9) | data formatting | bytes 1572864 | tf_op jit(solution)/shard_map/reshape | solution.py:326
  39.6 0.4 reshape.48
  40.4 1.1 %copy.15 = f32[64,2,4,128]{3,1,2,0:T(2,128)S(1)} copy(f32[64,2,4,128]{3,2,1,0:T(4,128)} %bitcast.64) | data formatting | bytes 524288 | tf_op jit(solution)/shard_map/reshape | solution.py:327
  41.6 0.6 fusion.25
  42.2 0.3 copy-done
  42.8 0.3 fusion.42
  43.1 0.3 fusion.44
  43.3 0.4 fusion
  43.9 0.4 fusion.4
  44.5 0.4 fusion.8
  45.1 0.4 fusion.12
  45.7 0.8 %copy-done.4 = f32[512,256]{1,0:T(8,128)S(1)} copy-done((f32[512,256]{1,0:T(8,128)S(1)}, f32[512,256]{1,0:T(8,128)}, u32[]{:S(2)}) %copy-start.4) | copy-done | bytes 524312
  46.5 0.6 fusion.16
  47.1 0.4 copy-done.3
  47.6 0.6 convolution_add_fusion
  48.3 0.8 %copy.21 = f32[64,4,2,128]{3,1,2,0:T(4,128)} copy(f32[64,4,2,128]{3,2,1,0:T(2,128)S(1)} %reshape.43) | data formatting | bytes 524288 | tf_op jit(solution)/shard_map/reshape | solution.py:330
  49.1 17.7 %shard_map.101 = f32[64,8,128]{2,1,0:T(8,128)} custom-call(f32[64,8,128]{2,1,0:T(8,128)} %bitcast.61), custom_call_target="tpu_custom_call" | custom-call | tf_op jit(solution)/shard_map/pallas_call | solution.py:84
  66.8 1.0 %copy.36 = f32[16,8,4,128]{3,1,2,0:T(8,128)S(1)} copy(f32[16,8,4,128]{3,2,1,0:T(4,128)} %bitcast.62) | data formatting | bytes 524288
  67.9 0.7 %copy-done.5 = bf16[512,128]{1,0:T(8,128)(2,1)S(1)} copy-done((bf16[512,128]{1,0:T(8,128)(2,1)S(1)}, bf16[512,128]{1,0:T(8,128)(2,1)}, u32[]{:S(2)}) %copy-start.5) | copy-done | bytes 131096
  68.7 0.7 %multiply_convert_fusion = bf16[512,128]{1,0:T(8,128)(2,1)} fusion(f32[512,128]{1,0:T(8,128)S(1)} %copy.22, bf16[512,128]{1,0:T(8,128)(2,1)S(1)} %copy-done.6, bf16[512,128]{1,0:T(8,128)(2,1)S(1)} %copy-done.5, f32[128]{0:T(128)S(1)} %copy-done.7), kind=kLoop, calls=%fused_computation.47 | loop fusion | flops 393216 | bytes 655872 | tf_op jit(solution)/shard_map/convert_element_type | solution.py:335
  (24 shorter events, 1.8 us)
Async XLA Ops:
  40.1 1.4 %copy-start.2 = (f32[1024,256]{1,0:T(8,128)S(1)}, f32[1024,256]{1,0:T(8,128)}, u32[]{:S(2)}) copy-start(f32[1024,256]{1,0:T(8,128)} %constant.25.clone) | copy-start | bytes 3145732
  41.6 1.0 %copy-start = (f32[512,128]{0,1:T(8,128)S(1)}, f32[512,128]{0,1:T(8,128)}, u32[]{:S(2)}) copy-start(f32[512,128]{0,1:T(8,128)} %constant.27.clone) | copy-start | bytes 786436
  41.6 1.0 %copy-start.1 = (f32[512,128]{0,1:T(8,128)S(1)}, f32[512,128]{0,1:T(8,128)}, u32[]{:S(2)}) copy-start(f32[512,128]{0,1:T(8,128)} %constant.26.clone) | copy-start | bytes 786436
  45.5 1.0 %copy-start.4 = (f32[512,256]{1,0:T(8,128)S(1)}, f32[512,256]{1,0:T(8,128)}, u32[]{:S(2)}) copy-start(f32[512,256]{1,0:T(8,128)} %constant.31) | copy-start | bytes 1572868
  46.5 1.0 %copy-start.3 = (f32[512,256]{1,0:T(8,128)S(1)}, f32[512,256]{1,0:T(8,128)}, u32[]{:S(2)}) copy-start(f32[512,256]{1,0:T(8,128)} %constant.32) | copy-start | bytes 1572868
  67.8 0.9 %copy-start.5 = (bf16[512,128]{1,0:T(8,128)(2,1)S(1)}, bf16[512,128]{1,0:T(8,128)(2,1)}, u32[]{:S(2)}) copy-start(bf16[512,128]{1,0:T(8,128)(2,1)} %param.12) | copy-start | bytes 393220
  67.8 1.0 %copy-start.6 = (bf16[512,128]{1,0:T(8,128)(2,1)S(1)}, bf16[512,128]{1,0:T(8,128)(2,1)}, u32[]{:S(2)}) copy-start(bf16[512,128]{1,0:T(8,128)(2,1)} %get-tuple-element.10) | copy-start | bytes 393220
  67.9 0.8 %copy-start.7 = (f32[128]{0:T(128)S(1)}, f32[128]{0:T(128)}, u32[]{:S(2)}) copy-start(f32[128]{0:T(128)} %param.14) | copy-start | bytes 1540

commit v13 on v12

--- a/solution.py
+++ b/solution.py
@@ -301,35 +301,249 @@
     return mm("rn,rm->nm", last, untwisted)
 
 
+def split(value):
+    high = value.astype(jnp.bfloat16)
+    return high, (value - high.astype(jnp.float32)).astype(jnp.bfloat16)
+
+
+def dot3(left, right):
+    l_hi, l_lo = left if isinstance(left, tuple) else split(left)
+    r_hi, r_lo = right if isinstance(right, tuple) else split(right)
+    out = jnp.dot(l_hi, r_hi, preferred_element_type=jnp.float32)
+    out = out + jnp.dot(l_hi, r_lo, preferred_element_type=jnp.float32)
+    return out + jnp.dot(l_lo, r_hi, preferred_element_type=jnp.float32)
+
+
+def whole_kernel(
+    feat_ref, gate_ref, gain_ref, spec_ref,
+    st_hi, st_lo, tc_ref, ts_ref, fa_hi, fa_lo, fb_hi, fb_lo, ia_hi, ia_lo, ib_hi, ib_lo,
+    lc_hi, lc_lo, ls_hi, ls_lo,
+    sig_out, res_recv,
+    sq_mine, sq_recv, sig_turn, sig_send, sig_recv, spec_recv, cols, conv_one, conv_send,
+    spec_sems, sig_sems, res_sems, chan_sems, own_sems,
+):
+    count = spec_ref.shape[0]
+    chans = sq_recv.shape[0]
+    me = lax.axis_index("seq")
+    mine = lax.axis_index("chan")
+    mesh_ids = pl.DeviceIdType.MESH
+    barrier = pltpu.get_barrier_semaphore()
+
+    def greet(step, carry):
+        peer = lax.rem(me + step, count)
+        pl.semaphore_signal(barrier, inc=1, device_id={"seq": peer}, device_id_type=mesh_ids)
+        return carry
+
+    lax.fori_loop(1, count, greet, 0)
+    for step in range(1, chans):
+        peer = lax.rem(mine + step, chans)
+        pl.semaphore_signal(barrier, inc=1, device_id={"chan": peer}, device_id_type=mesh_ids)
+    pl.semaphore_wait(barrier, count + chans - 2)
+
+    def seq_copy(source, target, sems, step):
+        peer = lax.rem(me + step, count)
+        return pltpu.make_async_remote_copy(
+            source(peer), target, sems.at[0, step], sems.at[1, step],
+            device_id={"seq": peer}, device_id_type=mesh_ids,
+        )
+
+    def start_all(source, target, sems):
+        def body(step, carry):
+            seq_copy(source, target, sems, step).start()
+            return carry
+        lax.fori_loop(1, count, body, 0)
+
+    def finish_all(source, target, sems):
+        def body(step, carry):
+            copy = seq_copy(source, target, sems, step)
+            copy.wait_send()
+            copy.wait_recv()
+            return carry
+        lax.fori_loop(1, count, body, 0)
+
+    spec_src = lambda peer: spec_ref.at[peer]
+    spec_own = pltpu.make_async_copy(spec_ref.at[me], spec_recv.at[me], own_sems.at[0])
+    spec_own.start()
+    start_all(spec_src, spec_recv.at[me], spec_sems)
+
+    feat = feat_ref[...].astype(jnp.float32)
+    part = jnp.sum(jnp.transpose(feat * feat), axis=0, keepdims=True)
+    sq_mine[...] = jnp.broadcast_to(part, sq_mine.shape)
+
+    def chan_copy(step):
+        peer = lax.rem(mine + step, chans)
+        return pltpu.make_async_remote_copy(
+            sq_mine, sq_recv.at[mine], chan_sems.at[0, step], chan_sems.at[1, step],
+            device_id={"chan": peer}, device_id_type=mesh_ids,
+        )
+
+    for step in range(1, chans):
+        chan_copy(step).start()
+    for step in range(1, chans):
+        copy = chan_copy(step)
+        copy.wait_send()
+        copy.wait_recv()
+    total = part
+    for step in range(1, chans):
+        other = lax.rem(mine + step, chans)
+        total = total + sq_recv[other][0:1, :]
+    scale = lax.rsqrt(total / CHANNELS + 1e-06)
+    scale = jnp.transpose(jnp.broadcast_to(scale, (8, scale.shape[1])))[:, 0:1]
+    signal = (feat * scale * gain_ref[...] * gate_ref[...].astype(jnp.float32)).astype(jnp.bfloat16)
+    sig_out[...] = signal
+    wide = signal.astype(jnp.float32)
+    lanes = wide.shape[1]
+    pair = lanes // count
+    tiles = wide.shape[0] // lanes
+    chunk = pair * tiles
+    for tile in range(tiles):
+        sig_turn[...] = jnp.transpose(wide[lanes * tile:lanes * (tile + 1), :])
+        for chan in range(pair):
+            rows = sig_turn[pl.ds(chan, count, stride=pair), :]
+            sig_send[pl.ds(tiles * chan + tile, count, stride=chunk), :] = rows
+
+    def rows_of(buffer):
+        return lambda peer: buffer.at[pl.ds(pl.multiple_of(peer * chunk, chunk), chunk)]
+
+    sig_own = pltpu.make_async_copy(rows_of(sig_send)(me), rows_of(sig_recv)(me), own_sems.at[1])
+    sig_own.start()
+    start_all(rows_of(sig_send), rows_of(sig_recv)(me), sig_sems)
+    finish_all(rows_of(sig_send), rows_of(sig_recv)(me), sig_sems)
+    sig_own.wait()
+
+    for chan in range(pair):
+        for tile in range(tiles):
+            rows = sig_recv[pl.ds(tiles * chan + tile, count, stride=chunk), :]
+            cols[chan, pl.ds(tile, count, stride=tiles), :] = rows
+
+    first_len = tc_ref.shape[0]
+    boths = []
+    for chan in range(pair):
+        signal_cols = cols[chan].astype(jnp.bfloat16)
+        both = jnp.dot(st_hi[...], signal_cols, preferred_element_type=jnp.float32)
+        boths.append(both + jnp.dot(st_lo[...], signal_cols, preferred_element_type=jnp.float32))
+
+    finish_all(spec_src, spec_recv.at[me], spec_sems)
+    spec_own.wait()
+
+    cos_twist, sin_twist = tc_ref[...], ts_ref[...]
+    own_rows = first_len // count
+    for chan in range(pair):
+        p_cos = boths[chan][:first_len]
+        p_sin = boths[chan][first_len:]
+        twist_re = p_cos * cos_twist - p_sin * sin_twist
+        twist_im = -p_sin * cos_twist - p_cos * sin_twist
+        freq = dot3(twist_re, (fa_hi[...], fa_lo[...])) + dot3(twist_im, (fb_hi[...], fb_lo[...]))
+        freq_re, freq_im = freq[:, :lanes], freq[:, lanes:]
+        filt = []
+        for part_of in range(2):
+            block = spec_recv[:, pl.ds((2 * chan + part_of) * own_rows, own_rows), :]
+            filt.append(block.astype(jnp.float32).reshape(first_len, lanes))
+        filt_re, filt_im = filt
+        prod_re = freq_re * filt_re - freq_im * filt_im
+        prod_im = freq_re * filt_im + freq_im * filt_re
+        back = dot3(prod_re, (ia_hi[...], ia_lo[...])) + dot3(prod_im, (ib_hi[...], ib_lo[...]))
+        back_re, back_im = back[:, :lanes], back[:, lanes:]
+        untwist_re = back_re * cos_twist - back_im * sin_twist
+        untwist_im = back_im * cos_twist + back_re * sin_twist
+        conv_one[...] = dot3((lc_hi[...], lc_lo[...]), untwist_re) + dot3((ls_hi[...], ls_lo[...]), untwist_im)
+        for tile in range(tiles):
+            rows = conv_one[pl.ds(tile, count, stride=tiles), :]
+            conv_send[pl.ds(tiles * chan + tile, count, stride=chunk), :] = rows
+
+    res_src = rows_of(conv_send)
+    res_own = pltpu.make_async_copy(res_src(me), res_recv.at[me], own_sems.at[2])
+    res_own.start()
+    start_all(res_src, res_recv.at[me], res_sems)
+    finish_all(res_src, res_recv.at[me], res_sems)
+    res_own.wait()
+
+
+def whole(features, pre_gate, gain_row, spec_rows, tables, chans):
+    count = spec_rows.shape[0]
+    length, width = features.shape
+    pair = width // count
+    lanes = 128
+    chunk = pair * length // lanes
+    vmem = pl.BlockSpec(memory_space=pltpu.VMEM)
+    operands = (features, pre_gate, gain_row, spec_rows) + tuple(tables)
+    return pl.pallas_call(
+        whole_kernel,
+        out_shape=(
+            jax.ShapeDtypeStruct((length, width), jnp.bfloat16),
+            jax.ShapeDtypeStruct((count, chunk, lanes), jnp.float32),
+        ),
+        in_specs=[vmem] * len(operands),
+        out_specs=(vmem, vmem),
+        scratch_shapes=[
+            pltpu.VMEM((8, length), jnp.float32),
+            pltpu.VMEM((chans, 8, length), jnp.float32),
+            pltpu.VMEM((lanes, lanes), jnp.float32),
+            pltpu.VMEM((count * chunk, lanes), jnp.float32),
+            pltpu.VMEM((count * chunk, lanes), jnp.float32),
+            pltpu.VMEM(spec_rows.shape, spec_rows.dtype),
+            pltpu.VMEM((pair, count * chunk // pair, lanes), jnp.float32),
+            pltpu.VMEM((count * chunk // pair, lanes), jnp.float32),
+            pltpu.VMEM((count * chunk, lanes), jnp.float32),
+            pltpu.SemaphoreType.DMA((2, count)),
+            pltpu.SemaphoreType.DMA((2, count)),
+            pltpu.SemaphoreType.DMA((2, count)),
+            pltpu.SemaphoreType.DMA((2, chans)),
+            pltpu.SemaphoreType.DMA((3,)),
+        ],
+        compiler_params=pltpu.CompilerParams(
+            collective_id=0, has_side_effects=True, vmem_limit_bytes=48 * 1024 * 1024
+        ),
+    )(*operands)
+
+
+def dft_tables(seq_count, tok_rows):
+    stride = 2 * seq_count
+    first_len = stride * ROW_GROUP
+    all_bins = stride * tok_rows
+    second_len = all_bins // first_len
+    half_first = first_len // 2
+    row_bins = bin_rows(seq_count).astype(np.int64)
+    first_turn = (row_bins[:, None] * np.arange(half_first)[None, :]) % first_len * (2.0 * np.pi / first_len)
+    cos_first, sin_first = np.cos(first_turn), np.sin(first_turn)
+    twist_turn = (row_bins[:, None] * np.arange(second_len)[None, :]) % all_bins * (2.0 * np.pi / all_bins)
+    second_in = np.arange(second_len)
+    second_turn = (second_in[:, None] * second_in[None, :]) % second_len * (2.0 * np.pi / second_len)
+    cos_second, sin_second = np.cos(second_turn), np.sin(second_turn)
+
+    def pair_of(array):
+        array = array.astype(np.float32)
+        high = array.astype(jnp.bfloat16)
+        return [jnp.asarray(high), jnp.asarray((array - high.astype(np.float32)).astype(jnp.bfloat16))]
+
+    tables = pair_of(np.concatenate([cos_first, sin_first], 0))
+    tables += [jnp.asarray(np.cos(twist_turn).astype(np.float32)), jnp.asarray(np.sin(twist_turn).astype(np.float32))]
+    tables += pair_of(np.concatenate([cos_second, -sin_second], 1))
+    tables += pair_of(np.concatenate([sin_second, cos_second], 1))
+    tables += pair_of(np.concatenate([cos_second, sin_second], 1))
+    tables += pair_of(np.concatenate([-sin_second, cos_second], 1))
+    tables += pair_of(cos_first.T / all_bins)
+    tables += pair_of(-sin_first.T / all_bins)
+    return tables
+
+
 def local(features, pre_gate, post_gate, norm_gain, skip_weight, spectrum):
     tok_rows, chan_width = features.shape
     seq_count = lax.axis_size("seq")
     chans = lax.axis_size("chan")
-    stride = 2 * seq_count
-    all_bins = stride * tok_rows
     group = chan_width // seq_count
-    first_len = stride * ROW_GROUP
-    second_len = all_bins // first_len
-    half_first = first_len // 2
+    second_len = tok_rows // ROW_GROUP
     lanes = 128
     tok_tiles = tok_rows // lanes
 
-    half_group = ROW_GROUP // 2
-    spec_rows = spectrum.reshape(2, 2, second_len, half_group, 2, chan_width)
-    spec_rows = jnp.transpose(spec_rows, (5, 0, 1, 3, 4, 2)).astype(jnp.bfloat16)
-    spec_rows = spec_rows.reshape(seq_count, -1, 2 * second_len)
-    signal, sig_chan, spec_chan = front(
-        features, pre_gate, norm_gain.reshape(1, chan_width), spec_rows, chans
+    spec_rows = spectrum.reshape(2, 2, second_len, ROW_GROUP, chan_width)
+    spec_rows = jnp.transpose(spec_rows, (4, 0, 1, 3, 2)).astype(jnp.bfloat16)
+    spec_rows = spec_rows.reshape(seq_count, -1, second_len)
+    signal, result = whole(
+        features, pre_gate, norm_gain.reshape(1, chan_width), spec_rows,
+        dft_tables(seq_count, tok_rows), chans,
     )
-    spec_chan = spec_chan.reshape(seq_count, group, 2, -1, 2 * second_len)
-    spec_chan = jnp.transpose(spec_chan, (1, 2, 0, 3, 4)).astype(jnp.float32)
-    spec_chan = spec_chan.reshape(group, 2, first_len, second_len)
-    sig_cols = sig_chan.reshape(seq_count, group, tok_tiles, lanes)
-    sig_cols = jnp.transpose(sig_cols, (0, 2, 1, 3)).reshape(half_first, group * second_len)
-    conv = convolve(sig_cols, spec_chan, seq_count, tok_rows)
-    conv = jnp.transpose(conv.reshape(seq_count, tok_tiles, group, lanes), (0, 2, 1, 3))
-    conv = conv.reshape(seq_count, -1, lanes)
-    result = exchange(conv, 2).reshape(seq_count, group, tok_tiles, lanes)
+    result = result.reshape(seq_count, group, tok_tiles, lanes)
     result = jnp.transpose(result, (2, 3, 0, 1)).reshape(tok_rows, chan_width)
     gated = post_gate.astype(jnp.float32) * (result + skip_weight * signal.astype(jnp.float32))
     return gated.astype(jnp.bfloat16)

time: 69.8 us -> 66.8 us (0.957)
  matrix products: 3.45 us -> 0 us
  local copies, waits for them, and re-layouts: 9.97 us -> 11.6 us
  Pallas kernels: 52.6 us -> 51.5 us
    unnamed x21 -> x43, local copies, waits for them, and re-layouts: 3.98 us -> 9.91 us
    reshape x7 -> x0, local copies, waits for them, and re-layouts: 5.05 us -> none  [the longest x3 1.89 us: local(): spec_chan = spec_chan.reshape(group, 2, first_len, second_len)]
    dot_general x7 -> x0, matrix products: 3.45 us -> none  [mm(): jnp.einsum(spec, left, right, precision=PRECISE, preferred_element_type=j...]
    pallas_call x2 -> x1, Pallas kernels: 52.6 us -> 51.5 us  [whole(): pl.pallas_call(whole_kernel, out_shape=(jax.ShapeDtypeStruct((length, wid...]
    convert_element_type x1, other arithmetic: 1.29 us -> 2.21 us  [local(): spec_rows = jnp.transpose(spec_rows, (4, 0, 1, 3, 2)).astype(jnp.bfloat16)]
    convert_element_type x1, local copies, waits for them, and re-layouts: 0.75 us -> 1.6 us  [local(): spec_rows = jnp.transpose(spec_rows, (4, 0, 1, 3, 2)).astype(jnp.bfloat16)]
where the time goes in v13:
time: 66.8 us; the launch traced here: 66.3 us
  Pallas kernels  51.5 us (77%)
  local copies, waits for them, and re-layouts  11.6 us (17%)
  other arithmetic  2.92 us (4%)
    pallas_call x1, Pallas kernels, whole(): pl.pallas_call(whole_kernel, out_shape=(jax.ShapeDtypeStruct((length, wid...  51.5 us
    unnamed x43, local copies, waits for them, and re-layouts  9.91 us
    convert_element_type x1, other arithmetic, local(): spec_rows = jnp.transpose(spec_rows, (4, 0, 1, 3, 2)).astype(jnp.bfloat16)  2.21 us
    convert_element_type x1, local copies, waits for them, and re-layouts, local(): spec_rows = jnp.transpose(spec_rows, (4, 0, 1, 3, 2)).astype(jnp.bfloat16)  1.6 us

profile of v13, /device:TPU:1, one launch (start us, length us, event | category | flops | bytes accessed | tf_op | source)
XLA Modules:
  0.0 66.3 jit_solution(9945139537059371267)
XLA Ops:
  0.0 0.0 copy-start.5
  0.0 0.0 copy-start.6
  0.0 0.0 copy-start.7
  0.0 2.2 %convert_element_type.19 = bf16[2,2,512,128]{3,2,1,0:T(8,128)(2,1)} convert(f32[2,2,512,128]{3,2,1,0:T(8,128)} %param.27) | non-fusion elementwise | flops 262144 | bytes 1572864 | tf_op jit(solution)/shard_map/convert_element_type | solution.py:540
  2.3 1.6 %copy.25 = bf16[2,2,128,4,128]{2,3,1,0,4:T(4,128)(2,1)S(1)} copy(bf16[2,2,128,4,128]{4,3,2,1,0:T(4,128)(2,1)} %bitcast.18) | data formatting | bytes 1048576 | tf_op jit(solution)/shard_map/convert_element_type | solution.py:540
  3.9 0.0 copy-start.18
  3.9 0.0 copy-done.2
  4.0 0.6 copy-done.18
  4.5 0.9 %copy-done.8 = bf16[512,128]{1,0:T(8,128)(2,1)S(1)} copy-done((bf16[512,128]{1,0:T(8,128)(2,1)S(1)}, bf16[512,128]{1,0:T(8,128)(2,1)}, u32[]{:S(2)}) %copy-start.8) | copy-done | bytes 131096
  5.4 0.9 %copy-done.9 = bf16[512,128]{1,0:T(8,128)(2,1)S(1)} copy-done((bf16[512,128]{1,0:T(8,128)(2,1)S(1)}, bf16[512,128]{1,0:T(8,128)(2,1)}, u32[]{:S(2)}) %copy-start.9) | copy-done | bytes 131096
  6.3 0.8 %copy-done.10 = bf16[128,256]{1,0:T(8,128)(2,1)S(1)} copy-done((bf16[128,256]{1,0:T(8,128)(2,1)S(1)}, bf16[128,256]{1,0:T(8,128)(2,1)}, u32[]{:S(2)}) %copy-start.10) | copy-done | bytes 65560
  7.2 0.8 %copy-done.11 = bf16[128,256]{1,0:T(8,128)(2,1)S(1)} copy-done((bf16[128,256]{1,0:T(8,128)(2,1)S(1)}, bf16[128,256]{1,0:T(8,128)(2,1)}, u32[]{:S(2)}) %copy-start.11) | copy-done | bytes 65560
  8.0 0.8 %copy-done.12 = bf16[128,256]{1,0:T(8,128)(2,1)S(1)} copy-done((bf16[128,256]{1,0:T(8,128)(2,1)S(1)}, bf16[128,256]{1,0:T(8,128)(2,1)}, u32[]{:S(2)}) %copy-start.12) | copy-done | bytes 65560
  8.9 0.8 %copy-done.13 = bf16[128,256]{1,0:T(8,128)(2,1)S(1)} copy-done((bf16[128,256]{1,0:T(8,128)(2,1)S(1)}, bf16[128,256]{1,0:T(8,128)(2,1)}, u32[]{:S(2)}) %copy-start.13) | copy-done | bytes 65560
  9.7 0.8 %copy-done.14 = bf16[128,256]{1,0:T(8,128)(2,1)S(1)} copy-done((bf16[128,256]{1,0:T(8,128)(2,1)S(1)}, bf16[128,256]{1,0:T(8,128)(2,1)}, u32[]{:S(2)}) %copy-start.14) | copy-done | bytes 65560
  10.5 0.8 %copy-done.15 = bf16[128,256]{1,0:T(8,128)(2,1)S(1)} copy-done((bf16[128,256]{1,0:T(8,128)(2,1)S(1)}, bf16[128,256]{1,0:T(8,128)(2,1)}, u32[]{:S(2)}) %copy-start.15) | copy-done | bytes 65560
  11.4 0.8 %copy-done.16 = bf16[128,256]{1,0:T(8,128)(2,1)S(1)} copy-done((bf16[128,256]{1,0:T(8,128)(2,1)S(1)}, bf16[128,256]{1,0:T(8,128)(2,1)}, u32[]{:S(2)}) %copy-start.16) | copy-done | bytes 65560
  12.2 0.8 %copy-done.17 = bf16[128,256]{1,0:T(8,128)(2,1)S(1)} copy-done((bf16[128,256]{1,0:T(8,128)(2,1)S(1)}, bf16[128,256]{1,0:T(8,128)(2,1)}, u32[]{:S(2)}) %copy-start.17) | copy-done | bytes 65560
  13.1 51.5 %shard_map.208 = (bf16[512,128]{1,0:T(8,128)(2,1)S(1)}, f32[64,8,128]{2,1,0:T(8,128)S(1)}) custom-call(bf16[512,128]{1,0:T(8,128)(2,1)S(1)} %copy-done.8, bf16[512,128]{1,0:T(8,128)(2,1)S(1)} %copy-done.9, f32[1,128]{1,0:T(1,128)S(1)} %bitcast.17, bf16[64,32,128]{2,1,0:T(8,128)(2,1)S(1)} %bitcast.15, bf16[1024,256]{1,0:T(8,128)(2,1)S(1)} %copy-done.1, ...), custom_call_target="tpu_custom_call" | custom-call | tf_op jit(solution)/shard_map/pallas_call | solution.py:470
  64.6 0.0 copy-start.19
  64.6 0.0 copy-start.20
  64.7 0.1 copy.26
  64.8 0.8 %copy-done.19 = bf16[512,128]{1,0:T(8,128)(2,1)S(1)} copy-done((bf16[512,128]{1,0:T(8,128)(2,1)S(1)}, bf16[512,128]{1,0:T(8,128)(2,1)}, u32[]{:S(2)}) %copy-start.19) | copy-done | bytes 131096
  65.5 0.7 %multiply_convert_fusion = bf16[512,128]{1,0:T(8,128)(2,1)} fusion(f32[512,128]{1,0:T(8,128)S(1)} %copy.26, bf16[512,128]{1,0:T(8,128)(2,1)S(1)} %get-tuple-element.8, bf16[512,128]{1,0:T(8,128)(2,1)S(1)} %copy-done.19, f32[128]{0:T(128)S(1)} %copy-done.20), kind=kLoop, calls=%fused_computation.1 | loop fusion | flops 393216 | bytes 655872 | tf_op jit(solution)/shard_map/convert_element_type | solution.py:549
  (24 shorter events, 0.1 us)
Async XLA Ops:
  0.0 3.9 %copy-start.2 = (bf16[256,512]{1,0:T(8,128)(2,1)S(1)}, bf16[256,512]{1,0:T(8,128)(2,1)}, u32[]{:S(2)}) copy-start(bf16[256,512]{1,0:T(8,128)(2,1)} %constant.47.clone.ls_lo) | copy-start | bytes 786436
  0.0 3.9 %copy-start.3 = (bf16[256,512]{1,0:T(8,128)(2,1)S(1)}, bf16[256,512]{1,0:T(8,128)(2,1)}, u32[]{:S(2)}) copy-start(bf16[256,512]{1,0:T(8,128)(2,1)} %constant.46.clone.ls_hi) | copy-start | bytes 786436
  0.0 3.9 %copy-start.4 = (bf16[256,512]{1,0:T(8,128)(2,1)S(1)}, bf16[256,512]{1,0:T(8,128)(2,1)}, u32[]{:S(2)}) copy-start(bf16[256,512]{1,0:T(8,128)(2,1)} %constant.45.clone.lc_lo) | copy-start | bytes 786436
  0.0 3.9 %copy-start.5 = (bf16[256,512]{1,0:T(8,128)(2,1)S(1)}, bf16[256,512]{1,0:T(8,128)(2,1)}, u32[]{:S(2)}) copy-start(bf16[256,512]{1,0:T(8,128)(2,1)} %constant.44.clone.lc_hi) | copy-start | bytes 786436
  0.0 3.9 %copy-start.6 = (f32[512,128]{1,0:T(8,128)S(1)}, f32[512,128]{1,0:T(8,128)}, u32[]{:S(2)}) copy-start(f32[512,128]{1,0:T(8,128)} %constant.35.clone.ts_ref) | copy-start | bytes 786436
  0.0 3.9 %copy-start.7 = (f32[512,128]{1,0:T(8,128)S(1)}, f32[512,128]{1,0:T(8,128)}, u32[]{:S(2)}) copy-start(f32[512,128]{1,0:T(8,128)} %constant.34.clone.tc_ref) | copy-start | bytes 786436
  2.3 1.7 %copy-start = (bf16[1024,256]{1,0:T(8,128)(2,1)S(1)}, bf16[1024,256]{1,0:T(8,128)(2,1)}, u32[]{:S(2)}) copy-start(bf16[1024,256]{1,0:T(8,128)(2,1)} %constant.33.clone.st_lo) | copy-start | bytes 1572868
  2.3 1.7 %copy-start.1 = (bf16[1024,256]{1,0:T(8,128)(2,1)S(1)}, bf16[1024,256]{1,0:T(8,128)(2,1)}, u32[]{:S(2)}) copy-start(bf16[1024,256]{1,0:T(8,128)(2,1)} %constant.32.clone.st_hi) | copy-start | bytes 1572868
  3.9 0.7 copy-start.18
  4.5 0.9 %copy-start.8 = (bf16[512,128]{1,0:T(8,128)(2,1)S(1)}, bf16[512,128]{1,0:T(8,128)(2,1)}, u32[]{:S(2)}) copy-start(bf16[512,128]{1,0:T(8,128)(2,1)} %feat_ref.1) | copy-start | bytes 393220
  5.4 0.9 %copy-start.9 = (bf16[512,128]{1,0:T(8,128)(2,1)S(1)}, bf16[512,128]{1,0:T(8,128)(2,1)}, u32[]{:S(2)}) copy-start(bf16[512,128]{1,0:T(8,128)(2,1)} %gate_ref.1) | copy-start | bytes 393220
  6.3 0.8 %copy-start.10 = (bf16[128,256]{1,0:T(8,128)(2,1)S(1)}, bf16[128,256]{1,0:T(8,128)(2,1)}, u32[]{:S(2)}) copy-start(bf16[128,256]{1,0:T(8,128)(2,1)} %constant.43.clone.ib_lo) | copy-start | bytes 196612
  7.2 0.8 %copy-start.11 = (bf16[128,256]{1,0:T(8,128)(2,1)S(1)}, bf16[128,256]{1,0:T(8,128)(2,1)}, u32[]{:S(2)}) copy-start(bf16[128,256]{1,0:T(8,128)(2,1)} %constant.42.clone.ib_hi) | copy-start | bytes 196612
  8.0 0.8 %copy-start.12 = (bf16[128,256]{1,0:T(8,128)(2,1)S(1)}, bf16[128,256]{1,0:T(8,128)(2,1)}, u32[]{:S(2)}) copy-start(bf16[128,256]{1,0:T(8,128)(2,1)} %constant.41.clone.ia_lo) | copy-start | bytes 196612
  8.9 0.8 %copy-start.13 = (bf16[128,256]{1,0:T(8,128)(2,1)S(1)}, bf16[128,256]{1,0:T(8,128)(2,1)}, u32[]{:S(2)}) copy-start(bf16[128,256]{1,0:T(8,128)(2,1)} %constant.40.clone.ia_hi) | copy-start | bytes 196612
  9.7 0.8 %copy-start.14 = (bf16[128,256]{1,0:T(8,128)(2,1)S(1)}, bf16[128,256]{1,0:T(8,128)(2,1)}, u32[]{:S(2)}) copy-start(bf16[128,256]{1,0:T(8,128)(2,1)} %constant.39.clone.fb_lo) | copy-start | bytes 196612
  10.5 0.8 %copy-start.15 = (bf16[128,256]{1,0:T(8,128)(2,1)S(1)}, bf16[128,256]{1,0:T(8,128)(2,1)}, u32[]{:S(2)}) copy-start(bf16[128,256]{1,0:T(8,128)(2,1)} %constant.38.clone.fb_hi) | copy-start | bytes 196612
  11.4 0.8 %copy-start.16 = (bf16[128,256]{1,0:T(8,128)(2,1)S(1)}, bf16[128,256]{1,0:T(8,128)(2,1)}, u32[]{:S(2)}) copy-start(bf16[128,256]{1,0:T(8,128)(2,1)} %constant.37.clone.fa_lo) | copy-start | bytes 196612
  12.2 0.8 %copy-start.17 = (bf16[128,256]{1,0:T(8,128)(2,1)S(1)}, bf16[128,256]{1,0:T(8,128)(2,1)}, u32[]{:S(2)}) copy-start(bf16[128,256]{1,0:T(8,128)(2,1)} %constant.36.clone.fa_hi) | copy-start | bytes 196612
  64.6 0.9 %copy-start.19 = (bf16[512,128]{1,0:T(8,128)(2,1)S(1)}, bf16[512,128]{1,0:T(8,128)(2,1)}, u32[]{:S(2)}) copy-start(bf16[512,128]{1,0:T(8,128)(2,1)} %param.24) | copy-start | bytes 393220
  64.6 0.9 %copy-start.20 = (f32[128]{0:T(128)S(1)}, f32[128]{0:T(128)}, u32[]{:S(2)}) copy-start(f32[128]{0:T(128)} %param.26) | copy-start | bytes 1540

commit v14 on v13

--- a/solution.py
+++ b/solution.py
@@ -10,6 +10,8 @@
 
 CHANNELS = 512
 ROW_GROUP = 4
+TABLE_NAMES = ("st_hi", "st_lo", "tc", "ts", "fa_hi", "fa_lo", "fb_hi", "fb_lo", "ia_hi", "ia_lo", "ib_hi", "ib_lo",
+               "lc_hi", "lc_lo", "ls_hi", "ls_lo")
 HIGH_DIGIT = 8
 
 
@@ -314,14 +316,18 @@
     return out + jnp.dot(l_lo, r_hi, preferred_element_type=jnp.float32)
 
 
-def whole_kernel(
-    feat_ref, gate_ref, gain_ref, spec_ref,
-    st_hi, st_lo, tc_ref, ts_ref, fa_hi, fa_lo, fb_hi, fb_lo, ia_hi, ia_lo, ib_hi, ib_lo,
-    lc_hi, lc_lo, ls_hi, ls_lo,
-    sig_out, res_recv,
-    sq_mine, sq_recv, sig_turn, sig_send, sig_recv, spec_recv, cols, conv_one, conv_send,
-    spec_sems, sig_sems, res_sems, chan_sems, own_sems,
-):
+def whole_kernel(feat_ref, gate_ref, gain_ref, spec_ref, *refs):
+    table_count = len(TABLE_NAMES)
+    held = refs[:table_count]
+    sig_out, res_recv = refs[table_count:table_count + 2]
+    (sq_mine, sq_recv, sig_turn, sig_send, sig_recv, spec_recv, cols, conv_one, conv_send,
+     spec_sems, sig_sems, res_sems, chan_sems, own_sems, table_sems) = refs[table_count + 2:table_count + 17]
+    tables = refs[table_count + 17:]
+    loads = [pltpu.make_async_copy(held[k], tables[k], table_sems.at[k]) for k in range(table_count)]
+    for load in loads:
+        load.start()
+    (st_hi, st_lo, tc_ref, ts_ref, fa_hi, fa_lo, fb_hi, fb_lo, ia_hi, ia_lo, ib_hi, ib_lo,
+     lc_hi, lc_lo, ls_hi, ls_lo) = tables
     count = spec_ref.shape[0]
     chans = sq_recv.shape[0]
     me = lax.axis_index("seq")
@@ -417,6 +423,8 @@
             cols[chan, pl.ds(tile, count, stride=tiles), :] = rows
 
     first_len = tc_ref.shape[0]
+    for load in loads:
+        load.wait()
     boths = []
     for chan in range(pair):
         signal_cols = cols[chan].astype(jnp.bfloat16)
@@ -467,13 +475,14 @@
     chunk = pair * length // lanes
     vmem = pl.BlockSpec(memory_space=pltpu.VMEM)
     operands = (features, pre_gate, gain_row, spec_rows) + tuple(tables)
+    hbm = pl.BlockSpec(memory_space=pl.ANY)
     return pl.pallas_call(
         whole_kernel,
         out_shape=(
             jax.ShapeDtypeStruct((length, width), jnp.bfloat16),
             jax.ShapeDtypeStruct((count, chunk, lanes), jnp.float32),
         ),
-        in_specs=[vmem] * len(operands),
+        in_specs=[vmem] * 4 + [hbm] * len(tables),
         out_specs=(vmem, vmem),
         scratch_shapes=[
             pltpu.VMEM((8, length), jnp.float32),
@@ -490,7 +499,9 @@
             pltpu.SemaphoreType.DMA((2, count)),
             pltpu.SemaphoreType.DMA((2, chans)),
             pltpu.SemaphoreType.DMA((3,)),
-        ],
+            pltpu.SemaphoreType.DMA((len(tables),)),
+        ]
+        + [pltpu.VMEM(table.shape, table.dtype) for table in tables],
         compiler_params=pltpu.CompilerParams(
             collective_id=0, has_side_effects=True, vmem_limit_bytes=48 * 1024 * 1024
         ),

time: 66.8 us -> 68.1 us (1.019)
  Pallas kernels: 51.5 us -> 52.8 us
    pallas_call x1, Pallas kernels: 51.5 us -> 52.8 us  [whole(): pl.pallas_call(whole_kernel, out_shape=(jax.ShapeDtypeStruct((length, wid...]
where the time goes in v14:
time: 68.1 us; the launch traced here: 67.5 us
  Pallas kernels  52.8 us (78%)
  local copies, waits for them, and re-layouts  11.6 us (17%)
  other arithmetic  2.92 us (4%)
    pallas_call x1, Pallas kernels, whole(): pl.pallas_call(whole_kernel, out_shape=(jax.ShapeDtypeStruct((length, wid...  52.8 us
    unnamed x43, local copies, waits for them, and re-layouts  9.91 us
    convert_element_type x1, other arithmetic, local(): spec_rows = jnp.transpose(spec_rows, (4, 0, 1, 3, 2)).astype(jnp.bfloat16)  2.21 us
    convert_element_type x1, local copies, waits for them, and re-layouts, local(): spec_rows = jnp.transpose(spec_rows, (4, 0, 1, 3, 2)).astype(jnp.bfloat16)  1.6 us

profile of v14, /device:TPU:1, one launch (start us, length us, event | category | flops | bytes accessed | tf_op | source)
XLA Modules:
  0.0 67.5 jit_solution(1535935364200237577)
XLA Ops:
  0.0 0.0 copy-start.5
  0.0 0.0 copy-start.6
  0.0 0.0 copy-start.7
  0.0 2.2 %convert_element_type.19 = bf16[2,2,512,128]{3,2,1,0:T(8,128)(2,1)} convert(f32[2,2,512,128]{3,2,1,0:T(8,128)} %param.27) | non-fusion elementwise | flops 262144 | bytes 1572864 | tf_op jit(solution)/shard_map/convert_element_type | solution.py:551
  2.3 1.6 %copy.25 = bf16[2,2,128,4,128]{2,3,1,0,4:T(4,128)(2,1)S(1)} copy(bf16[2,2,128,4,128]{4,3,2,1,0:T(4,128)(2,1)} %bitcast.18) | data formatting | bytes 1048576 | tf_op jit(solution)/shard_map/convert_element_type | solution.py:551
  3.9 0.0 copy-start.18
  3.9 0.0 copy-done.2
  4.0 0.6 copy-done.18
  4.5 0.9 %copy-done.8 = bf16[512,128]{1,0:T(8,128)(2,1)S(1)} copy-done((bf16[512,128]{1,0:T(8,128)(2,1)S(1)}, bf16[512,128]{1,0:T(8,128)(2,1)}, u32[]{:S(2)}) %copy-start.8) | copy-done | bytes 131096
  5.4 0.9 %copy-done.9 = bf16[512,128]{1,0:T(8,128)(2,1)S(1)} copy-done((bf16[512,128]{1,0:T(8,128)(2,1)S(1)}, bf16[512,128]{1,0:T(8,128)(2,1)}, u32[]{:S(2)}) %copy-start.9) | copy-done | bytes 131096
  6.3 0.8 %copy-done.10 = bf16[128,256]{1,0:T(8,128)(2,1)S(1)} copy-done((bf16[128,256]{1,0:T(8,128)(2,1)S(1)}, bf16[128,256]{1,0:T(8,128)(2,1)}, u32[]{:S(2)}) %copy-start.10) | copy-done | bytes 65560
  7.2 0.8 %copy-done.11 = bf16[128,256]{1,0:T(8,128)(2,1)S(1)} copy-done((bf16[128,256]{1,0:T(8,128)(2,1)S(1)}, bf16[128,256]{1,0:T(8,128)(2,1)}, u32[]{:S(2)}) %copy-start.11) | copy-done | bytes 65560
  8.0 0.8 %copy-done.12 = bf16[128,256]{1,0:T(8,128)(2,1)S(1)} copy-done((bf16[128,256]{1,0:T(8,128)(2,1)S(1)}, bf16[128,256]{1,0:T(8,128)(2,1)}, u32[]{:S(2)}) %copy-start.12) | copy-done | bytes 65560
  8.9 0.8 %copy-done.13 = bf16[128,256]{1,0:T(8,128)(2,1)S(1)} copy-done((bf16[128,256]{1,0:T(8,128)(2,1)S(1)}, bf16[128,256]{1,0:T(8,128)(2,1)}, u32[]{:S(2)}) %copy-start.13) | copy-done | bytes 65560
  9.7 0.8 %copy-done.14 = bf16[128,256]{1,0:T(8,128)(2,1)S(1)} copy-done((bf16[128,256]{1,0:T(8,128)(2,1)S(1)}, bf16[128,256]{1,0:T(8,128)(2,1)}, u32[]{:S(2)}) %copy-start.14) | copy-done | bytes 65560
  10.5 0.8 %copy-done.15 = bf16[128,256]{1,0:T(8,128)(2,1)S(1)} copy-done((bf16[128,256]{1,0:T(8,128)(2,1)S(1)}, bf16[128,256]{1,0:T(8,128)(2,1)}, u32[]{:S(2)}) %copy-start.15) | copy-done | bytes 65560
  11.4 0.8 %copy-done.16 = bf16[128,256]{1,0:T(8,128)(2,1)S(1)} copy-done((bf16[128,256]{1,0:T(8,128)(2,1)S(1)}, bf16[128,256]{1,0:T(8,128)(2,1)}, u32[]{:S(2)}) %copy-start.16) | copy-done | bytes 65560
  12.2 0.8 %copy-done.17 = bf16[128,256]{1,0:T(8,128)(2,1)S(1)} copy-done((bf16[128,256]{1,0:T(8,128)(2,1)S(1)}, bf16[128,256]{1,0:T(8,128)(2,1)}, u32[]{:S(2)}) %copy-start.17) | copy-done | bytes 65560
  13.1 52.8 %shard_map.208 = (bf16[512,128]{1,0:T(8,128)(2,1)S(1)}, f32[64,8,128]{2,1,0:T(8,128)S(1)}) custom-call(bf16[512,128]{1,0:T(8,128)(2,1)S(1)} %copy-done.8, bf16[512,128]{1,0:T(8,128)(2,1)S(1)} %copy-done.9, f32[1,128]{1,0:T(1,128)S(1)} %bitcast.17, bf16[64,32,128]{2,1,0:T(8,128)(2,1)S(1)} %bitcast.15, bf16[1024,256]{1,0:T(8,128)(2,1)S(1)} %copy-done.1, ...), custom_call_target="tpu_custom_call" | custom-call | tf_op jit(solution)/shard_map/pallas_call | solution.py:479
  65.9 0.0 copy-start.19
  65.9 0.0 copy-start.20
  65.9 0.1 copy.26
  66.0 0.8 %copy-done.19 = bf16[512,128]{1,0:T(8,128)(2,1)S(1)} copy-done((bf16[512,128]{1,0:T(8,128)(2,1)S(1)}, bf16[512,128]{1,0:T(8,128)(2,1)}, u32[]{:S(2)}) %copy-start.19) | copy-done | bytes 131096
  66.8 0.7 %multiply_convert_fusion = bf16[512,128]{1,0:T(8,128)(2,1)} fusion(f32[512,128]{1,0:T(8,128)S(1)} %copy.26, bf16[512,128]{1,0:T(8,128)(2,1)S(1)} %get-tuple-element.8, bf16[512,128]{1,0:T(8,128)(2,1)S(1)} %copy-done.19, f32[128]{0:T(128)S(1)} %copy-done.20), kind=kLoop, calls=%fused_computation.1 | loop fusion | flops 393216 | bytes 655872 | tf_op jit(solution)/shard_map/convert_element_type | solution.py:560
  (24 shorter events, 0.1 us)
Async XLA Ops:
  0.0 3.9 %copy-start.2 = (bf16[256,512]{1,0:T(8,128)(2,1)S(1)}, bf16[256,512]{1,0:T(8,128)(2,1)}, u32[]{:S(2)}) copy-start(bf16[256,512]{1,0:T(8,128)(2,1)} %constant.47.clone.refs_15_) | copy-start | bytes 786436
  0.0 3.9 %copy-start.3 = (bf16[256,512]{1,0:T(8,128)(2,1)S(1)}, bf16[256,512]{1,0:T(8,128)(2,1)}, u32[]{:S(2)}) copy-start(bf16[256,512]{1,0:T(8,128)(2,1)} %constant.46.clone.refs_14_) | copy-start | bytes 786436
  0.0 3.9 %copy-start.4 = (bf16[256,512]{1,0:T(8,128)(2,1)S(1)}, bf16[256,512]{1,0:T(8,128)(2,1)}, u32[]{:S(2)}) copy-start(bf16[256,512]{1,0:T(8,128)(2,1)} %constant.45.clone.refs_13_) | copy-start | bytes 786436
  0.0 3.9 %copy-start.5 = (bf16[256,512]{1,0:T(8,128)(2,1)S(1)}, bf16[256,512]{1,0:T(8,128)(2,1)}, u32[]{:S(2)}) copy-start(bf16[256,512]{1,0:T(8,128)(2,1)} %constant.44.clone.refs_12_) | copy-start | bytes 786436
  0.0 3.9 %copy-start.6 = (f32[512,128]{1,0:T(8,128)S(1)}, f32[512,128]{1,0:T(8,128)}, u32[]{:S(2)}) copy-start(f32[512,128]{1,0:T(8,128)} %constant.35.clone.refs_3_) | copy-start | bytes 786436
  0.0 3.9 %copy-start.7 = (f32[512,128]{1,0:T(8,128)S(1)}, f32[512,128]{1,0:T(8,128)}, u32[]{:S(2)}) copy-start(f32[512,128]{1,0:T(8,128)} %constant.34.clone.refs_2_) | copy-start | bytes 786436
  2.3 1.7 %copy-start = (bf16[1024,256]{1,0:T(8,128)(2,1)S(1)}, bf16[1024,256]{1,0:T(8,128)(2,1)}, u32[]{:S(2)}) copy-start(bf16[1024,256]{1,0:T(8,128)(2,1)} %constant.33.clone.refs_1_) | copy-start | bytes 1572868
  2.3 1.7 %copy-start.1 = (bf16[1024,256]{1,0:T(8,128)(2,1)S(1)}, bf16[1024,256]{1,0:T(8,128)(2,1)}, u32[]{:S(2)}) copy-start(bf16[1024,256]{1,0:T(8,128)(2,1)} %constant.32.clone.refs_0_) | copy-start | bytes 1572868
  3.9 0.7 copy-start.18
  4.5 0.9 %copy-start.8 = (bf16[512,128]{1,0:T(8,128)(2,1)S(1)}, bf16[512,128]{1,0:T(8,128)(2,1)}, u32[]{:S(2)}) copy-start(bf16[512,128]{1,0:T(8,128)(2,1)} %feat_ref.1) | copy-start | bytes 393220
  5.4 0.9 %copy-start.9 = (bf16[512,128]{1,0:T(8,128)(2,1)S(1)}, bf16[512,128]{1,0:T(8,128)(2,1)}, u32[]{:S(2)}) copy-start(bf16[512,128]{1,0:T(8,128)(2,1)} %gate_ref.1) | copy-start | bytes 393220
  6.3 0.8 %copy-start.10 = (bf16[128,256]{1,0:T(8,128)(2,1)S(1)}, bf16[128,256]{1,0:T(8,128)(2,1)}, u32[]{:S(2)}) copy-start(bf16[128,256]{1,0:T(8,128)(2,1)} %constant.43.clone.refs_11_) | copy-start | bytes 196612
  7.2 0.8 %copy-start.11 = (bf16[128,256]{1,0:T(8,128)(2,1)S(1)}, bf16[128,256]{1,0:T(8,128)(2,1)}, u32[]{:S(2)}) copy-start(bf16[128,256]{1,0:T(8,128)(2,1)} %constant.42.clone.refs_10_) | copy-start | bytes 196612
  8.0 0.8 %copy-start.12 = (bf16[128,256]{1,0:T(8,128)(2,1)S(1)}, bf16[128,256]{1,0:T(8,128)(2,1)}, u32[]{:S(2)}) copy-start(bf16[128,256]{1,0:T(8,128)(2,1)} %constant.41.clone.refs_9_) | copy-start | bytes 196612
  8.9 0.8 %copy-start.13 = (bf16[128,256]{1,0:T(8,128)(2,1)S(1)}, bf16[128,256]{1,0:T(8,128)(2,1)}, u32[]{:S(2)}) copy-start(bf16[128,256]{1,0:T(8,128)(2,1)} %constant.40.clone.refs_8_) | copy-start | bytes 196612
  9.7 0.8 %copy-start.14 = (bf16[128,256]{1,0:T(8,128)(2,1)S(1)}, bf16[128,256]{1,0:T(8,128)(2,1)}, u32[]{:S(2)}) copy-start(bf16[128,256]{1,0:T(8,128)(2,1)} %constant.39.clone.refs_7_) | copy-start | bytes 196612
  10.5 0.8 %copy-start.15 = (bf16[128,256]{1,0:T(8,128)(2,1)S(1)}, bf16[128,256]{1,0:T(8,128)(2,1)}, u32[]{:S(2)}) copy-start(bf16[128,256]{1,0:T(8,128)(2,1)} %constant.38.clone.refs_6_) | copy-start | bytes 196612
  11.4 0.8 %copy-start.16 = (bf16[128,256]{1,0:T(8,128)(2,1)S(1)}, bf16[128,256]{1,0:T(8,128)(2,1)}, u32[]{:S(2)}) copy-start(bf16[128,256]{1,0:T(8,128)(2,1)} %constant.37.clone.refs_5_) | copy-start | bytes 196612
  12.2 0.8 %copy-start.17 = (bf16[128,256]{1,0:T(8,128)(2,1)S(1)}, bf16[128,256]{1,0:T(8,128)(2,1)}, u32[]{:S(2)}) copy-start(bf16[128,256]{1,0:T(8,128)(2,1)} %constant.36.clone.refs_4_) | copy-start | bytes 196612
  65.9 0.9 %copy-start.19 = (bf16[512,128]{1,0:T(8,128)(2,1)S(1)}, bf16[512,128]{1,0:T(8,128)(2,1)}, u32[]{:S(2)}) copy-start(bf16[512,128]{1,0:T(8,128)(2,1)} %param.24) | copy-start | bytes 393220
  65.9 0.9 %copy-start.20 = (f32[128]{0:T(128)S(1)}, f32[128]{0:T(128)}, u32[]{:S(2)}) copy-start(f32[128]{0:T(128)} %param.26) | copy-start | bytes 1540

commit v15 on v14

--- a/solution.py
+++ b/solution.py
@@ -316,8 +316,8 @@
     return out + jnp.dot(l_lo, r_hi, preferred_element_type=jnp.float32)
 
 
-def whole_kernel(feat_ref, gate_ref, gain_ref, spec_ref, *refs):
-    table_count = len(TABLE_NAMES)
+def whole_kernel(*refs):
+    table_count = len(TABLE_NAMES) + 4
     held = refs[:table_count]
     sig_out, res_recv = refs[table_count:table_count + 2]
     (sq_mine, sq_recv, sig_turn, sig_send, sig_recv, spec_recv, cols, conv_one, conv_send,
@@ -326,6 +326,11 @@
     loads = [pltpu.make_async_copy(held[k], tables[k], table_sems.at[k]) for k in range(table_count)]
     for load in loads:
         load.start()
+    for load in loads[:4]:
+        load.wait()
+    loads = loads[4:]
+    feat_ref, gate_ref, gain_ref, spec_ref = tables[:4]
+    tables = tables[4:]
     (st_hi, st_lo, tc_ref, ts_ref, fa_hi, fa_lo, fb_hi, fb_lo, ia_hi, ia_lo, ib_hi, ib_lo,
      lc_hi, lc_lo, ls_hi, ls_lo) = tables
     count = spec_ref.shape[0]
@@ -482,7 +487,7 @@
             jax.ShapeDtypeStruct((length, width), jnp.bfloat16),
             jax.ShapeDtypeStruct((count, chunk, lanes), jnp.float32),
         ),
-        in_specs=[vmem] * 4 + [hbm] * len(tables),
+        in_specs=[hbm] * len(operands),
         out_specs=(vmem, vmem),
         scratch_shapes=[
             pltpu.VMEM((8, length), jnp.float32),
@@ -499,11 +504,11 @@
             pltpu.SemaphoreType.DMA((2, count)),
             pltpu.SemaphoreType.DMA((2, chans)),
             pltpu.SemaphoreType.DMA((3,)),
-            pltpu.SemaphoreType.DMA((len(tables),)),
+            pltpu.SemaphoreType.DMA((len(operands),)),
         ]
-        + [pltpu.VMEM(table.shape, table.dtype) for table in tables],
+        + [pltpu.VMEM(table.shape, table.dtype) for table in operands],
         compiler_params=pltpu.CompilerParams(
-            collective_id=0, has_side_effects=True, vmem_limit_bytes=48 * 1024 * 1024
+            collective_id=0, has_side_effects=True, vmem_limit_bytes=67043328
         ),
     )(*operands)
 

time: 68.1 us -> 58.8 us (0.86)
  local copies, waits for them, and re-layouts: 11.6 us -> 3.06 us
  other arithmetic: 2.92 us -> 2 us
  Pallas kernels: 52.8 us -> 53.5 us
    unnamed x43 -> x7, local copies, waits for them, and re-layouts: 9.91 us -> 1.79 us
    convert_element_type x1, other arithmetic: 2.21 us -> 1.29 us  [local(): spec_rows = jnp.transpose(spec_rows, (4, 0, 1, 3, 2)).astype(jnp.bfloat16)]
    pallas_call x1, Pallas kernels: 52.8 us -> 53.5 us  [whole(): pl.pallas_call(whole_kernel, out_shape=(jax.ShapeDtypeStruct((length, wid...]
where the time goes in v15:
time: 58.8 us; the launch traced here: 58.7 us
  Pallas kernels  53.5 us (91%)
  local copies, waits for them, and re-layouts  3.06 us (5%)
  other arithmetic  2 us (3%)
    pallas_call x1, Pallas kernels, whole(): pl.pallas_call(whole_kernel, out_shape=(jax.ShapeDtypeStruct((length, wid...  53.5 us
    unnamed x7, local copies, waits for them, and re-layouts  1.79 us
    convert_element_type x1, other arithmetic, local(): spec_rows = jnp.transpose(spec_rows, (4, 0, 1, 3, 2)).astype(jnp.bfloat16)  1.29 us

profile of v15, /device:TPU:1, one launch (start us, length us, event | category | flops | bytes accessed | tf_op | source)
XLA Modules:
  0.0 58.7 jit_solution(6887581621786774754)
XLA Ops:
  0.0 1.3 %convert_element_type.19 = bf16[2,2,512,128]{3,2,1,0:T(8,128)(2,1)S(1)} convert(f32[2,2,512,128]{3,2,1,0:T(8,128)} %param.27) | non-fusion elementwise | flops 262144 | bytes 1572864 | tf_op jit(solution)/shard_map/convert_element_type | solution.py:556
  1.3 1.2 %copy.25 = bf16[2,2,128,4,128]{2,3,1,0,4:T(4,128)(2,1)} copy(bf16[2,2,128,4,128]{4,3,2,1,0:T(4,128)(2,1)S(1)} %bitcast.16) | data formatting | bytes 1048576 | tf_op jit(solution)/shard_map/convert_element_type | solution.py:556
  2.5 53.5 %shard_map.208 = (bf16[512,128]{1,0:T(8,128)(2,1)}, f32[64,8,128]{2,1,0:T(8,128)}) custom-call(bf16[512,128]{1,0:T(8,128)(2,1)} %refs_0_.1, bf16[512,128]{1,0:T(8,128)(2,1)} %refs_1_.1, f32[1,128]{1,0:T(1,128)} %bitcast.19, bf16[64,32,128]{2,1,0:T(8,128)(2,1)} %bitcast.15, bf16[1024,256]{1,0:T(8,128)(2,1)} %constant.32.clone.refs_4_, ...), custom_call_target="tpu_custom_call" | custom-call | tf_op jit(solution)/shard_map/pallas_call | solution.py:484
  56.0 1.0 %copy.29 = f32[16,8,4,128]{3,1,2,0:T(8,128)S(1)} copy(f32[16,8,4,128]{3,2,1,0:T(4,128)} %bitcast.18) | data formatting | bytes 524288
  57.0 0.0 copy-start
  57.0 0.0 copy-start.1
  57.0 0.0 copy-start.2
  57.0 0.1 copy.26
  57.1 0.7 %copy-done = bf16[512,128]{1,0:T(8,128)(2,1)S(1)} copy-done((bf16[512,128]{1,0:T(8,128)(2,1)S(1)}, bf16[512,128]{1,0:T(8,128)(2,1)}, u32[]{:S(2)}) %copy-start) | copy-done | bytes 131096
  57.9 0.1 copy-done.1
  57.9 0.0 copy-done.2
  57.9 0.7 %multiply_convert_fusion = bf16[512,128]{1,0:T(8,128)(2,1)} fusion(f32[512,128]{1,0:T(8,128)S(1)} %copy.26, bf16[512,128]{1,0:T(8,128)(2,1)S(1)} %copy-done.1, bf16[512,128]{1,0:T(8,128)(2,1)S(1)} %copy-done, f32[128]{0:T(128)S(1)} %copy-done.2), kind=kLoop, calls=%fused_computation.1 | loop fusion | flops 393216 | bytes 655872 | tf_op jit(solution)/shard_map/convert_element_type | solution.py:565
Async XLA Ops:
  57.0 0.9 %copy-start = (bf16[512,128]{1,0:T(8,128)(2,1)S(1)}, bf16[512,128]{1,0:T(8,128)(2,1)}, u32[]{:S(2)}) copy-start(bf16[512,128]{1,0:T(8,128)(2,1)} %param.24) | copy-start | bytes 393220
  57.0 1.0 %copy-start.1 = (bf16[512,128]{1,0:T(8,128)(2,1)S(1)}, bf16[512,128]{1,0:T(8,128)(2,1)}, u32[]{:S(2)}) copy-start(bf16[512,128]{1,0:T(8,128)(2,1)} %get-tuple-element.8) | copy-start | bytes 393220
  57.0 1.0 %copy-start.2 = (f32[128]{0:T(128)S(1)}, f32[128]{0:T(128)}, u32[]{:S(2)}) copy-start(f32[128]{0:T(128)} %param.26) | copy-start | bytes 1540

commit v16 on v15

--- a/solution.py
+++ b/solution.py
@@ -436,17 +436,21 @@
         both = jnp.dot(st_hi[...], signal_cols, preferred_element_type=jnp.float32)
         boths.append(both + jnp.dot(st_lo[...], signal_cols, preferred_element_type=jnp.float32))
 
-    finish_all(spec_src, spec_recv.at[me], spec_sems)
-    spec_own.wait()
-
     cos_twist, sin_twist = tc_ref[...], ts_ref[...]
     own_rows = first_len // count
+    freqs = []
     for chan in range(pair):
         p_cos = boths[chan][:first_len]
         p_sin = boths[chan][first_len:]
         twist_re = p_cos * cos_twist - p_sin * sin_twist
         twist_im = -p_sin * cos_twist - p_cos * sin_twist
-        freq = dot3(twist_re, (fa_hi[...], fa_lo[...])) + dot3(twist_im, (fb_hi[...], fb_lo[...]))
+        freqs.append(dot3(twist_re, (fa_hi[...], fa_lo[...])) + dot3(twist_im, (fb_hi[...], fb_lo[...])))
+
+    finish_all(spec_src, spec_recv.at[me], spec_sems)
+    spec_own.wait()
+
+    for chan in range(pair):
+        freq = freqs[chan]
         freq_re, freq_im = freq[:, :lanes], freq[:, lanes:]
         filt = []
         for part_of in range(2):

time: 58.8 us -> 58 us (0.986)
  Pallas kernels: 53.5 us -> 52.7 us
    pallas_call x1, Pallas kernels: 53.5 us -> 52.7 us  [whole(): pl.pallas_call(whole_kernel, out_shape=(jax.ShapeDtypeStruct((length, wid...]
where the time goes in v16:
time: 58 us; the launch traced here: 57.9 us
  Pallas kernels  52.7 us (91%)
  local copies, waits for them, and re-layouts  3.06 us (5%)
  other arithmetic  2 us (3%)
    pallas_call x1, Pallas kernels, whole(): pl.pallas_call(whole_kernel, out_shape=(jax.ShapeDtypeStruct((length, wid...  52.7 us
    unnamed x7, local copies, waits for them, and re-layouts  1.79 us
    convert_element_type x1, other arithmetic, local(): spec_rows = jnp.transpose(spec_rows, (4, 0, 1, 3, 2)).astype(jnp.bfloat16)  1.29 us

profile of v16, /device:TPU:1, one launch (start us, length us, event | category | flops | bytes accessed | tf_op | source)
XLA Modules:
  0.0 57.9 jit_solution(386846329416452784)
XLA Ops:
  0.0 1.3 %convert_element_type.19 = bf16[2,2,512,128]{3,2,1,0:T(8,128)(2,1)S(1)} convert(f32[2,2,512,128]{3,2,1,0:T(8,128)} %param.27) | non-fusion elementwise | flops 262144 | bytes 1572864 | tf_op jit(solution)/shard_map/convert_element_type | solution.py:560
  1.3 1.2 %copy.25 = bf16[2,2,128,4,128]{2,3,1,0,4:T(4,128)(2,1)} copy(bf16[2,2,128,4,128]{4,3,2,1,0:T(4,128)(2,1)S(1)} %bitcast.16) | data formatting | bytes 1048576 | tf_op jit(solution)/shard_map/convert_element_type | solution.py:560
  2.5 52.7 %shard_map.208 = (bf16[512,128]{1,0:T(8,128)(2,1)}, f32[64,8,128]{2,1,0:T(8,128)}) custom-call(bf16[512,128]{1,0:T(8,128)(2,1)} %refs_0_.1, bf16[512,128]{1,0:T(8,128)(2,1)} %refs_1_.1, f32[1,128]{1,0:T(1,128)} %bitcast.19, bf16[64,32,128]{2,1,0:T(8,128)(2,1)} %bitcast.15, bf16[1024,256]{1,0:T(8,128)(2,1)} %constant.32.clone.refs_4_, ...), custom_call_target="tpu_custom_call" | custom-call | tf_op jit(solution)/shard_map/pallas_call | solution.py:488
  55.2 1.0 %copy.29 = f32[16,8,4,128]{3,1,2,0:T(8,128)S(1)} copy(f32[16,8,4,128]{3,2,1,0:T(4,128)} %bitcast.18) | data formatting | bytes 524288
  56.2 0.0 copy-start
  56.2 0.0 copy-start.1
  56.2 0.0 copy-start.2
  56.2 0.1 copy.26
  56.3 0.7 %copy-done = bf16[512,128]{1,0:T(8,128)(2,1)S(1)} copy-done((bf16[512,128]{1,0:T(8,128)(2,1)S(1)}, bf16[512,128]{1,0:T(8,128)(2,1)}, u32[]{:S(2)}) %copy-start) | copy-done | bytes 131096
  57.1 0.1 copy-done.1
  57.1 0.0 copy-done.2
  57.1 0.7 %multiply_convert_fusion = bf16[512,128]{1,0:T(8,128)(2,1)} fusion(f32[512,128]{1,0:T(8,128)S(1)} %copy.26, bf16[512,128]{1,0:T(8,128)(2,1)S(1)} %copy-done.1, bf16[512,128]{1,0:T(8,128)(2,1)S(1)} %copy-done, f32[128]{0:T(128)S(1)} %copy-done.2), kind=kLoop, calls=%fused_computation.1 | loop fusion | flops 393216 | bytes 655872 | tf_op jit(solution)/shard_map/convert_element_type | solution.py:569
Async XLA Ops:
  56.2 0.9 %copy-start = (bf16[512,128]{1,0:T(8,128)(2,1)S(1)}, bf16[512,128]{1,0:T(8,128)(2,1)}, u32[]{:S(2)}) copy-start(bf16[512,128]{1,0:T(8,128)(2,1)} %param.24) | copy-start | bytes 393220
  56.2 1.0 %copy-start.1 = (bf16[512,128]{1,0:T(8,128)(2,1)S(1)}, bf16[512,128]{1,0:T(8,128)(2,1)}, u32[]{:S(2)}) copy-start(bf16[512,128]{1,0:T(8,128)(2,1)} %get-tuple-element.8) | copy-start | bytes 393220
  56.2 1.0 %copy-start.2 = (f32[128]{0:T(128)S(1)}, f32[128]{0:T(128)}, u32[]{:S(2)}) copy-start(f32[128]{0:T(128)} %param.26) | copy-start | bytes 1540

commit v17 on v16

--- a/solution.py
+++ b/solution.py
@@ -309,11 +309,13 @@
 
 
 def dot3(left, right):
-    l_hi, l_lo = left if isinstance(left, tuple) else split(left)
-    r_hi, r_lo = right if isinstance(right, tuple) else split(right)
-    out = jnp.dot(l_hi, r_hi, preferred_element_type=jnp.float32)
-    out = out + jnp.dot(l_hi, r_lo, preferred_element_type=jnp.float32)
-    return out + jnp.dot(l_lo, r_hi, preferred_element_type=jnp.float32)
+    if isinstance(left, tuple):
+        d_hi, d_lo = split(right)
+        out = jnp.dot(left[0], d_hi, preferred_element_type=jnp.float32)
+        return out + jnp.dot(left[0], d_lo, preferred_element_type=jnp.float32)
+    d_hi, d_lo = split(left)
+    out = jnp.dot(d_hi, right[0], preferred_element_type=jnp.float32)
+    return out + jnp.dot(d_lo, right[0], preferred_element_type=jnp.float32)
 
 
 def whole_kernel(*refs):
@@ -433,8 +435,7 @@
     boths = []
     for chan in range(pair):
         signal_cols = cols[chan].astype(jnp.bfloat16)
-        both = jnp.dot(st_hi[...], signal_cols, preferred_element_type=jnp.float32)
-        boths.append(both + jnp.dot(st_lo[...], signal_cols, preferred_element_type=jnp.float32))
+        boths.append(jnp.dot(st_hi[...], signal_cols, preferred_element_type=jnp.float32))
 
     cos_twist, sin_twist = tc_ref[...], ts_ref[...]
     own_rows = first_len // count

time: 58 us -> 56.7 us (0.978)
  Pallas kernels: 52.7 us -> 51.4 us
    pallas_call x1, Pallas kernels: 52.7 us -> 51.4 us  [whole(): pl.pallas_call(whole_kernel, out_shape=(jax.ShapeDtypeStruct((length, wid...]
where the time goes in v17:
time: 56.7 us; the launch traced here: 56.5 us
  Pallas kernels  51.4 us (91%)
  local copies, waits for them, and re-layouts  3.06 us (5%)
  other arithmetic  2 us (4%)
    pallas_call x1, Pallas kernels, whole(): pl.pallas_call(whole_kernel, out_shape=(jax.ShapeDtypeStruct((length, wid...  51.4 us
    unnamed x7, local copies, waits for them, and re-layouts  1.79 us
    convert_element_type x1, other arithmetic, local(): spec_rows = jnp.transpose(spec_rows, (4, 0, 1, 3, 2)).astype(jnp.bfloat16)  1.29 us
    convert_element_type x1, local copies, waits for them, and re-layouts, local(): spec_rows = jnp.transpose(spec_rows, (4, 0, 1, 3, 2)).astype(jnp.bfloat16)  1.15 us

profile of v17, /device:TPU:1, one launch (start us, length us, event | category | flops | bytes accessed | tf_op | source)
XLA Modules:
  0.0 56.5 jit_solution(6419782956270753039)
XLA Ops:
  0.0 1.3 %convert_element_type.19 = bf16[2,2,512,128]{3,2,1,0:T(8,128)(2,1)S(1)} convert(f32[2,2,512,128]{3,2,1,0:T(8,128)} %param.27) | non-fusion elementwise | flops 262144 | bytes 1572864 | tf_op jit(solution)/shard_map/convert_element_type | solution.py:561
  1.3 1.2 %copy.25 = bf16[2,2,128,4,128]{2,3,1,0,4:T(4,128)(2,1)} copy(bf16[2,2,128,4,128]{4,3,2,1,0:T(4,128)(2,1)S(1)} %bitcast.16) | data formatting | bytes 1048576 | tf_op jit(solution)/shard_map/convert_element_type | solution.py:561
  2.5 51.4 %shard_map.208 = (bf16[512,128]{1,0:T(8,128)(2,1)}, f32[64,8,128]{2,1,0:T(8,128)}) custom-call(bf16[512,128]{1,0:T(8,128)(2,1)} %refs_0_.1, bf16[512,128]{1,0:T(8,128)(2,1)} %refs_1_.1, f32[1,128]{1,0:T(1,128)} %bitcast.19, bf16[64,32,128]{2,1,0:T(8,128)(2,1)} %bitcast.15, bf16[1024,256]{1,0:T(8,128)(2,1)} %constant.32.clone.refs_4_, ...), custom_call_target="tpu_custom_call" | custom-call | tf_op jit(solution)/shard_map/pallas_call | solution.py:489
  53.8 1.0 %copy.29 = f32[16,8,4,128]{3,1,2,0:T(8,128)S(1)} copy(f32[16,8,4,128]{3,2,1,0:T(4,128)} %bitcast.18) | data formatting | bytes 524288
  54.8 0.0 copy-start
  54.8 0.0 copy-start.1
  54.8 0.0 copy-start.2
  54.8 0.1 copy.26
  55.0 0.7 %copy-done = bf16[512,128]{1,0:T(8,128)(2,1)S(1)} copy-done((bf16[512,128]{1,0:T(8,128)(2,1)S(1)}, bf16[512,128]{1,0:T(8,128)(2,1)}, u32[]{:S(2)}) %copy-start) | copy-done | bytes 131096
  55.7 0.1 copy-done.1
  55.8 0.0 copy-done.2
  55.8 0.7 %multiply_convert_fusion = bf16[512,128]{1,0:T(8,128)(2,1)} fusion(f32[512,128]{1,0:T(8,128)S(1)} %copy.26, bf16[512,128]{1,0:T(8,128)(2,1)S(1)} %copy-done.1, bf16[512,128]{1,0:T(8,128)(2,1)S(1)} %copy-done, f32[128]{0:T(128)S(1)} %copy-done.2), kind=kLoop, calls=%fused_computation.1 | loop fusion | flops 393216 | bytes 655872 | tf_op jit(solution)/shard_map/convert_element_type | solution.py:570
Async XLA Ops:
  54.8 0.9 %copy-start = (bf16[512,128]{1,0:T(8,128)(2,1)S(1)}, bf16[512,128]{1,0:T(8,128)(2,1)}, u32[]{:S(2)}) copy-start(bf16[512,128]{1,0:T(8,128)(2,1)} %param.24) | copy-start | bytes 393220
  54.8 1.0 %copy-start.1 = (bf16[512,128]{1,0:T(8,128)(2,1)S(1)}, bf16[512,128]{1,0:T(8,128)(2,1)}, u32[]{:S(2)}) copy-start(bf16[512,128]{1,0:T(8,128)(2,1)} %get-tuple-element.8) | copy-start | bytes 393220
  54.8 1.0 %copy-start.2 = (f32[128]{0:T(128)S(1)}, f32[128]{0:T(128)}, u32[]{:S(2)}) copy-start(f32[128]{0:T(128)} %param.26) | copy-start | bytes 1540

commit v18 on v17

--- a/solution.py
+++ b/solution.py
@@ -37,270 +37,12 @@
     return jnp.einsum(spec, left, right, precision=PRECISE, preferred_element_type=jnp.float32)
 
 
-def exchange_kernel(src_ref, dst_ref, send_sem, recv_sem, own_sem):
-    count = src_ref.shape[0]
-    me = lax.axis_index("seq")
-    mesh_ids = pl.DeviceIdType.MESH
-    barrier = pltpu.get_barrier_semaphore()
-
-    def greet(step, carry):
-        peer = lax.rem(me + step, count)
-        pl.semaphore_signal(barrier, inc=1, device_id={"seq": peer}, device_id_type=mesh_ids)
-        return carry
-
-    lax.fori_loop(1, count, greet, 0, unroll=True)
-    pl.semaphore_wait(barrier, count - 1)
-    own = pltpu.make_async_copy(src_ref.at[me], dst_ref.at[me], own_sem)
-    own.start()
-
-    def remote(step):
-        peer = lax.rem(me + step, count)
-        return pltpu.make_async_remote_copy(
-            src_ref.at[peer],
-            dst_ref.at[me],
-            send_sem.at[step],
-            recv_sem.at[step],
-            device_id={"seq": peer},
-            device_id_type=mesh_ids,
-        )
-
-    def send(step, carry):
-        remote(step).start()
-        return carry
-
-    lax.fori_loop(1, count, send, 0, unroll=True)
-
-    def finish(step, carry):
-        copy = remote(step)
-        copy.wait_send()
-        copy.wait_recv()
-        return carry
-
-    lax.fori_loop(1, count, finish, 0, unroll=True)
-    own.wait()
-
-
-def exchange(blocks, tag):
-    count = blocks.shape[0]
-    vmem = pl.BlockSpec(memory_space=pltpu.VMEM)
-    return pl.pallas_call(
-        exchange_kernel,
-        out_shape=jax.ShapeDtypeStruct(blocks.shape, blocks.dtype),
-        in_specs=[vmem],
-        out_specs=vmem,
-        scratch_shapes=[
-            pltpu.SemaphoreType.DMA((count,)),
-            pltpu.SemaphoreType.DMA((count,)),
-            pltpu.SemaphoreType.DMA,
-        ],
-        compiler_params=pltpu.CompilerParams(collective_id=tag, has_side_effects=True),
-    )(blocks)
-
-
-def front_kernel(
-    feat_ref, gate_ref, gain_ref, spec_ref,
-    sig_out, sig_recv, spec_recv,
-    sq_mine, sq_recv, sig_turn, sig_send, spec_sems, sig_sems, chan_sems, own_sems,
-):
-    count = spec_ref.shape[0]
-    chans = sq_recv.shape[0]
-    me = lax.axis_index("seq")
-    mine = lax.axis_index("chan")
-    mesh_ids = pl.DeviceIdType.MESH
-    barrier = pltpu.get_barrier_semaphore()
-
-    def greet(step, carry):
-        peer = lax.rem(me + step, count)
-        pl.semaphore_signal(barrier, inc=1, device_id={"seq": peer}, device_id_type=mesh_ids)
-        return carry
-
-    lax.fori_loop(1, count, greet, 0, unroll=True)
-    for step in range(1, chans):
-        peer = lax.rem(mine + step, chans)
-        pl.semaphore_signal(barrier, inc=1, device_id={"chan": peer}, device_id_type=mesh_ids)
-    pl.semaphore_wait(barrier, count + chans - 2)
-
-    def spec_copy(step):
-        peer = lax.rem(me + step, count)
-        return pltpu.make_async_remote_copy(
-            spec_ref.at[peer],
-            spec_recv.at[me],
-            spec_sems.at[0, step],
-            spec_sems.at[1, step],
-            device_id={"seq": peer},
-            device_id_type=mesh_ids,
-        )
-
-    spec_own = pltpu.make_async_copy(spec_ref.at[me], spec_recv.at[me], own_sems.at[0])
-    spec_own.start()
-
-    def spec_send(step, carry):
-        spec_copy(step).start()
-        return carry
-
-    lax.fori_loop(1, count, spec_send, 0, unroll=True)
-
-    feat = feat_ref[...].astype(jnp.float32)
-    part = jnp.sum(jnp.transpose(feat * feat), axis=0, keepdims=True)
-    sq_mine[...] = jnp.broadcast_to(part, sq_mine.shape)
-
-    def chan_copy(step):
-        peer = lax.rem(mine + step, chans)
-        return pltpu.make_async_remote_copy(
-            sq_mine,
-            sq_recv.at[mine],
-            chan_sems.at[0, step],
-            chan_sems.at[1, step],
-            device_id={"chan": peer},
-            device_id_type=mesh_ids,
-        )
-
-    for step in range(1, chans):
-        chan_copy(step).start()
-    for step in range(1, chans):
-        copy = chan_copy(step)
-        copy.wait_send()
-        copy.wait_recv()
-    total = part
-    for step in range(1, chans):
-        other = lax.rem(mine + step, chans)
-        total = total + sq_recv[other][0:1, :]
-    scale = lax.rsqrt(total / CHANNELS + 1e-06)
-    scale = jnp.transpose(jnp.broadcast_to(scale, (8, scale.shape[1])))[:, 0:1]
-    signal = (feat * scale * gain_ref[...] * gate_ref[...].astype(jnp.float32)).astype(jnp.bfloat16)
-    sig_out[...] = signal
-    wide = signal.astype(jnp.float32)
-    lanes = wide.shape[1]
-    pair = lanes // count
-    tiles = wide.shape[0] // lanes
-    chunk = pair * tiles
-    for tile in range(tiles):
-        sig_turn[...] = jnp.transpose(wide[lanes * tile:lanes * (tile + 1), :])
-        for chan in range(pair):
-            rows = sig_turn[pl.ds(chan, count, stride=pair), :]
-            sig_send[pl.ds(tiles * chan + tile, count, stride=chunk), :] = rows
-
-    def sig_rows(peer):
-        return sig_send.at[pl.ds(pl.multiple_of(peer * chunk, chunk), chunk)]
-
-    def sig_copy(step):
-        peer = lax.rem(me + step, count)
-        return pltpu.make_async_remote_copy(
-            sig_rows(peer),
-            sig_recv.at[me],
-            sig_sems.at[0, step],
-            sig_sems.at[1, step],
-            device_id={"seq": peer},
-            device_id_type=mesh_ids,
-        )
-
-    sig_own = pltpu.make_async_copy(sig_rows(me), sig_recv.at[me], own_sems.at[1])
-    sig_own.start()
-
-    def sig_start(step, carry):
-        sig_copy(step).start()
-        return carry
-
-    lax.fori_loop(1, count, sig_start, 0, unroll=True)
-
-    def sig_finish(step, carry):
-        copy = sig_copy(step)
-        copy.wait_send()
-        copy.wait_recv()
-        return carry
-
-    lax.fori_loop(1, count, sig_finish, 0, unroll=True)
-    sig_own.wait()
-
-    def spec_finish(step, carry):
-        copy = spec_copy(step)
-        copy.wait_send()
-        copy.wait_recv()
-        return carry
-
-    lax.fori_loop(1, count, spec_finish, 0, unroll=True)
-    spec_own.wait()
-
-
-def front(feat, gate, gain_row, spec_rows, chans):
-    count = spec_rows.shape[0]
-    length, width = feat.shape
-    pair = width // count
-    vmem = pl.BlockSpec(memory_space=pltpu.VMEM)
-    return pl.pallas_call(
-        front_kernel,
-        out_shape=(
-            jax.ShapeDtypeStruct((length, width), jnp.bfloat16),
-            jax.ShapeDtypeStruct((count, pair * length // 128, 128), jnp.float32),
-            jax.ShapeDtypeStruct(spec_rows.shape, spec_rows.dtype),
-        ),
-        in_specs=[vmem] * 4,
-        out_specs=(vmem, vmem, vmem),
-        scratch_shapes=[
-            pltpu.VMEM((8, length), jnp.float32),
-            pltpu.VMEM((chans, 8, length), jnp.float32),
-            pltpu.VMEM((128, 128), jnp.float32),
-            pltpu.VMEM((count * pair * length // 128, 128), jnp.float32),
-            pltpu.SemaphoreType.DMA((2, count)),
-            pltpu.SemaphoreType.DMA((2, count)),
-            pltpu.SemaphoreType.DMA((2, chans)),
-            pltpu.SemaphoreType.DMA((2,)),
-        ],
-        compiler_params=pltpu.CompilerParams(collective_id=0, has_side_effects=True),
-    )(feat, gate, gain_row, spec_rows)
-
-
 def bin_rows(seq_count):
     digit_order = reversed_digits(seq_count)
     stride = 2 * seq_count
     slots = np.arange(stride)
     low_bins = 2 * digit_order[slots // 2] + slots % 2
     return (low_bins[:, None] + stride * np.arange(ROW_GROUP)[None, :]).reshape(-1).astype(np.int32)
-
-
-def convolve(sig_cols, spec_chan, seq_count, tok_rows):
-    group = spec_chan.shape[0]
-    first_len, second_len = spec_chan.shape[2], spec_chan.shape[3]
-    half_first = first_len // 2
-    all_bins = first_len * second_len
-    row_bins = bin_rows(seq_count).astype(np.int64)
-    first_in = np.arange(half_first)
-    first_turn = (row_bins[:, None] * first_in[None, :]) % first_len * (2.0 * np.pi / first_len)
-    stacked_np = np.concatenate([np.cos(first_turn), np.sin(first_turn)], 0)
-    stacked = jnp.asarray(stacked_np.astype(np.float32))
-    signs = np.concatenate([np.ones(first_len), -np.ones(first_len)]) / all_bins
-    twist_turn = (row_bins[:, None] * np.arange(second_len)[None, :]) % all_bins * (2.0 * np.pi / all_bins)
-    cos_twist = jnp.asarray(np.cos(twist_turn).astype(np.float32))
-    sin_twist = jnp.asarray(np.sin(twist_turn).astype(np.float32))
-    second_in = jnp.arange(second_len, dtype=jnp.int32)
-    cos_second, sin_second = rotation(second_in[:, None] * second_in[None, :], second_len)
-    fwd_second = jnp.concatenate(
-        [jnp.concatenate([cos_second, -sin_second], 1), jnp.concatenate([sin_second, cos_second], 1)], 0
-    )
-    inv_second = jnp.concatenate(
-        [jnp.concatenate([cos_second, sin_second], 1), jnp.concatenate([-sin_second, cos_second], 1)], 0
-    )
-    last = stacked * jnp.asarray(signs.astype(np.float32))[:, None]
-
-    both = mm("rn,nm->rm", stacked, sig_cols)
-    along_cos, along_sin = both[:first_len], both[first_len:]
-    outs_re, outs_im = [], []
-    for chan in range(group):
-        lanes_of = slice(chan * second_len, (chan + 1) * second_len)
-        p_cos, p_sin = along_cos[:, lanes_of], along_sin[:, lanes_of]
-        twist_re = p_cos * cos_twist - p_sin * sin_twist
-        twist_im = -p_sin * cos_twist - p_cos * sin_twist
-        freq = mm("rn,nk->rk", jnp.concatenate([twist_re, twist_im], 1), fwd_second)
-        freq_re, freq_im = freq[:, :second_len], freq[:, second_len:]
-        filt_re, filt_im = spec_chan[chan, 0], spec_chan[chan, 1]
-        prod_re = freq_re * filt_re - freq_im * filt_im
-        prod_im = freq_re * filt_im + freq_im * filt_re
-        back = mm("rk,kn->rn", jnp.concatenate([prod_re, prod_im], 1), inv_second)
-        back_re, back_im = back[:, :second_len], back[:, second_len:]
-        outs_re.append(back_re * cos_twist - back_im * sin_twist)
-        outs_im.append(back_im * cos_twist + back_re * sin_twist)
-    untwisted = jnp.concatenate([jnp.concatenate(outs_re, 1), jnp.concatenate(outs_im, 1)], 0)
-    return mm("rn,rm->nm", last, untwisted)
 
 
 def split(value):
@@ -351,6 +93,9 @@
     for step in range(1, chans):
         peer = lax.rem(mine + step, chans)
         pl.semaphore_signal(barrier, inc=1, device_id={"chan": peer}, device_id_type=mesh_ids)
+    feat = feat_ref[...].astype(jnp.float32)
+    part = jnp.sum(jnp.transpose(feat * feat), axis=0, keepdims=True)
+    sq_mine[...] = jnp.broadcast_to(part, sq_mine.shape)
     pl.semaphore_wait(barrier, count + chans - 2)
 
     def seq_copy(source, target, sems, step):
@@ -374,14 +119,6 @@
             return carry
         lax.fori_loop(1, count, body, 0)
 
-    spec_src = lambda peer: spec_ref.at[peer]
-    spec_own = pltpu.make_async_copy(spec_ref.at[me], spec_recv.at[me], own_sems.at[0])
-    spec_own.start()
-    start_all(spec_src, spec_recv.at[me], spec_sems)
-
-    feat = feat_ref[...].astype(jnp.float32)
-    part = jnp.sum(jnp.transpose(feat * feat), axis=0, keepdims=True)
-    sq_mine[...] = jnp.broadcast_to(part, sq_mine.shape)
 
     def chan_copy(step):
         peer = lax.rem(mine + step, chans)
@@ -392,6 +129,10 @@
 
     for step in range(1, chans):
         chan_copy(step).start()
+    spec_src = lambda peer: spec_ref.at[peer]
+    spec_own = pltpu.make_async_copy(spec_ref.at[me], spec_recv.at[me], own_sems.at[0])
+    spec_own.start()
+    start_all(spec_src, spec_recv.at[me], spec_sems)
     for step in range(1, chans):
         copy = chan_copy(step)
         copy.wait_send()

time: 56.7 us -> 56.7 us (level)
  no operation moved by 1% of the time
where the time goes in v18:
time: 56.7 us; the launch traced here: 56.6 us
  Pallas kernels  51.4 us (91%)
  local copies, waits for them, and re-layouts  3.06 us (5%)
  other arithmetic  2 us (4%)
    pallas_call x1, Pallas kernels, whole(): pl.pallas_call(whole_kernel, out_shape=(jax.ShapeDtypeStruct((length, wid...  51.4 us
    unnamed x7, local copies, waits for them, and re-layouts  1.79 us
    convert_element_type x1, other arithmetic, local(): spec_rows = jnp.transpose(spec_rows, (4, 0, 1, 3, 2)).astype(jnp.bfloat16)  1.29 us
    convert_element_type x1, local copies, waits for them, and re-layouts, local(): spec_rows = jnp.transpose(spec_rows, (4, 0, 1, 3, 2)).astype(jnp.bfloat16)  1.15 us

profile of v18, /device:TPU:1, one launch (start us, length us, event | category | flops | bytes accessed | tf_op | source)
XLA Modules:
  0.0 56.6 jit_solution(13594232115564778254)
XLA Ops:
  0.0 1.3 %convert_element_type.19 = bf16[2,2,512,128]{3,2,1,0:T(8,128)(2,1)S(1)} convert(f32[2,2,512,128]{3,2,1,0:T(8,128)} %param.27) | non-fusion elementwise | flops 262144 | bytes 1572864 | tf_op jit(solution)/shard_map/convert_element_type | solution.py:302
  1.3 1.2 %copy.25 = bf16[2,2,128,4,128]{2,3,1,0,4:T(4,128)(2,1)} copy(bf16[2,2,128,4,128]{4,3,2,1,0:T(4,128)(2,1)S(1)} %bitcast.16) | data formatting | bytes 1048576 | tf_op jit(solution)/shard_map/convert_element_type | solution.py:302
  2.5 51.4 %shard_map.208 = (bf16[512,128]{1,0:T(8,128)(2,1)}, f32[64,8,128]{2,1,0:T(8,128)}) custom-call(bf16[512,128]{1,0:T(8,128)(2,1)} %refs_0_.1, bf16[512,128]{1,0:T(8,128)(2,1)} %refs_1_.1, f32[1,128]{1,0:T(1,128)} %bitcast.19, bf16[64,32,128]{2,1,0:T(8,128)(2,1)} %bitcast.15, bf16[1024,256]{1,0:T(8,128)(2,1)} %constant.32.clone.refs_4_, ...), custom_call_target="tpu_custom_call" | custom-call | tf_op jit(solution)/shard_map/pallas_call | solution.py:230
  53.9 1.0 %copy.29 = f32[16,8,4,128]{3,1,2,0:T(8,128)S(1)} copy(f32[16,8,4,128]{3,2,1,0:T(4,128)} %bitcast.18) | data formatting | bytes 524288
  54.9 0.0 copy-start
  54.9 0.0 copy-start.1
  54.9 0.0 copy-start.2
  54.9 0.1 copy.26
  55.0 0.7 %copy-done = bf16[512,128]{1,0:T(8,128)(2,1)S(1)} copy-done((bf16[512,128]{1,0:T(8,128)(2,1)S(1)}, bf16[512,128]{1,0:T(8,128)(2,1)}, u32[]{:S(2)}) %copy-start) | copy-done | bytes 131096
  55.8 0.1 copy-done.1
  55.8 0.0 copy-done.2
  55.8 0.7 %multiply_convert_fusion = bf16[512,128]{1,0:T(8,128)(2,1)} fusion(f32[512,128]{1,0:T(8,128)S(1)} %copy.26, bf16[512,128]{1,0:T(8,128)(2,1)S(1)} %copy-done.1, bf16[512,128]{1,0:T(8,128)(2,1)S(1)} %copy-done, f32[128]{0:T(128)S(1)} %copy-done.2), kind=kLoop, calls=%fused_computation.1 | loop fusion | flops 393216 | bytes 655872 | tf_op jit(solution)/shard_map/convert_element_type | solution.py:311
Async XLA Ops:
  54.9 0.9 %copy-start = (bf16[512,128]{1,0:T(8,128)(2,1)S(1)}, bf16[512,128]{1,0:T(8,128)(2,1)}, u32[]{:S(2)}) copy-start(bf16[512,128]{1,0:T(8,128)(2,1)} %param.24) | copy-start | bytes 393220
  54.9 1.0 %copy-start.1 = (bf16[512,128]{1,0:T(8,128)(2,1)S(1)}, bf16[512,128]{1,0:T(8,128)(2,1)}, u32[]{:S(2)}) copy-start(bf16[512,128]{1,0:T(8,128)(2,1)} %get-tuple-element.8) | copy-start | bytes 393220
  54.9 1.0 %copy-start.2 = (f32[128]{0:T(128)S(1)}, f32[128]{0:T(128)}, u32[]{:S(2)}) copy-start(f32[128]{0:T(128)} %param.26) | copy-start | bytes 1540

commit v19 on v18

--- a/solution.py
+++ b/solution.py
@@ -61,20 +61,20 @@
 
 
 def whole_kernel(*refs):
-    table_count = len(TABLE_NAMES) + 4
+    table_count = len(TABLE_NAMES) + 6
     held = refs[:table_count]
-    sig_out, res_recv = refs[table_count:table_count + 2]
-    (sq_mine, sq_recv, sig_turn, sig_send, sig_recv, spec_recv, cols, conv_one, conv_send,
-     spec_sems, sig_sems, res_sems, chan_sems, own_sems, table_sems) = refs[table_count + 2:table_count + 17]
+    gated_out = refs[table_count]
+    (sq_mine, sq_recv, sig_turn, sig_send, sig_recv, spec_recv, cols, conv_one, conv_send, res_recv,
+     spec_sems, sig_sems, res_sems, chan_sems, own_sems, table_sems) = refs[table_count + 1:table_count + 17]
     tables = refs[table_count + 17:]
     loads = [pltpu.make_async_copy(held[k], tables[k], table_sems.at[k]) for k in range(table_count)]
     for load in loads:
         load.start()
-    for load in loads[:4]:
+    for load in loads[:6]:
         load.wait()
-    loads = loads[4:]
-    feat_ref, gate_ref, gain_ref, spec_ref = tables[:4]
-    tables = tables[4:]
+    loads = loads[6:]
+    feat_ref, gate_ref, gain_ref, spec_ref, post_ref, skip_ref = tables[:6]
+    tables = tables[6:]
     (st_hi, st_lo, tc_ref, ts_ref, fa_hi, fa_lo, fb_hi, fb_lo, ia_hi, ia_lo, ib_hi, ib_lo,
      lc_hi, lc_lo, ls_hi, ls_lo) = tables
     count = spec_ref.shape[0]
@@ -144,7 +144,6 @@
     scale = lax.rsqrt(total / CHANNELS + 1e-06)
     scale = jnp.transpose(jnp.broadcast_to(scale, (8, scale.shape[1])))[:, 0:1]
     signal = (feat * scale * gain_ref[...] * gate_ref[...].astype(jnp.float32)).astype(jnp.bfloat16)
-    sig_out[...] = signal
     wide = signal.astype(jnp.float32)
     lanes = wide.shape[1]
     pair = lanes // count
@@ -211,30 +210,38 @@
             conv_send[pl.ds(tiles * chan + tile, count, stride=chunk), :] = rows
 
     res_src = rows_of(conv_send)
-    res_own = pltpu.make_async_copy(res_src(me), res_recv.at[me], own_sems.at[2])
+    res_dst = rows_of(res_recv)(me)
+    res_own = pltpu.make_async_copy(res_src(me), res_dst, own_sems.at[2])
     res_own.start()
-    start_all(res_src, res_recv.at[me], res_sems)
-    finish_all(res_src, res_recv.at[me], res_sems)
+    start_all(res_src, res_dst, res_sems)
+    finish_all(res_src, res_dst, res_sems)
     res_own.wait()
 
-
-def whole(features, pre_gate, gain_row, spec_rows, tables, chans):
+    skip = skip_ref[...]
+    for tile in range(tiles):
+        for chan in range(pair):
+            sig_turn[pl.ds(chan, count, stride=pair), :] = res_recv[pl.ds(tiles * chan + tile, count, stride=chunk), :]
+        block = jnp.transpose(sig_turn[...])
+        these = slice(lanes * tile, lanes * (tile + 1))
+        direct = signal[these, :].astype(jnp.float32)
+        gated = post_ref[these, :].astype(jnp.float32) * (block + skip * direct)
+        gated_out[these, :] = gated.astype(gated_out.dtype)
+
+
+def whole(features, pre_gate, gain_row, spec_rows, post_gate, skip_row, tables, chans):
     count = spec_rows.shape[0]
     length, width = features.shape
     pair = width // count
     lanes = 128
     chunk = pair * length // lanes
     vmem = pl.BlockSpec(memory_space=pltpu.VMEM)
-    operands = (features, pre_gate, gain_row, spec_rows) + tuple(tables)
+    operands = (features, pre_gate, gain_row, spec_rows, post_gate, skip_row) + tuple(tables)
     hbm = pl.BlockSpec(memory_space=pl.ANY)
     return pl.pallas_call(
         whole_kernel,
-        out_shape=(
-            jax.ShapeDtypeStruct((length, width), jnp.bfloat16),
-            jax.ShapeDtypeStruct((count, chunk, lanes), jnp.float32),
-        ),
+        out_shape=jax.ShapeDtypeStruct((length, width), jnp.bfloat16),
         in_specs=[hbm] * len(operands),
-        out_specs=(vmem, vmem),
+        out_specs=vmem,
         scratch_shapes=[
             pltpu.VMEM((8, length), jnp.float32),
             pltpu.VMEM((chans, 8, length), jnp.float32),
@@ -244,6 +251,7 @@
             pltpu.VMEM(spec_rows.shape, spec_rows.dtype),
             pltpu.VMEM((pair, count * chunk // pair, lanes), jnp.float32),
             pltpu.VMEM((count * chunk // pair, lanes), jnp.float32),
+            pltpu.VMEM((count * chunk, lanes), jnp.float32),
             pltpu.VMEM((count * chunk, lanes), jnp.float32),
             pltpu.SemaphoreType.DMA((2, count)),
             pltpu.SemaphoreType.DMA((2, count)),
@@ -301,14 +309,10 @@
     spec_rows = spectrum.reshape(2, 2, second_len, ROW_GROUP, chan_width)
     spec_rows = jnp.transpose(spec_rows, (4, 0, 1, 3, 2)).astype(jnp.bfloat16)
     spec_rows = spec_rows.reshape(seq_count, -1, second_len)
-    signal, result = whole(
+    return whole(
         features, pre_gate, norm_gain.reshape(1, chan_width), spec_rows,
-        dft_tables(seq_count, tok_rows), chans,
+        post_gate, skip_weight.reshape(1, chan_width), dft_tables(seq_count, tok_rows), chans,
     )
-    result = result.reshape(seq_count, group, tok_tiles, lanes)
-    result = jnp.transpose(result, (2, 3, 0, 1)).reshape(tok_rows, chan_width)
-    gated = post_gate.astype(jnp.float32) * (result + skip_weight * signal.astype(jnp.float32))
-    return gated.astype(jnp.bfloat16)
 
 
 def solution(mesh):

time: 56.7 us -> 55.7 us (0.982)
  other arithmetic: 2 us -> 1.29 us
    convert_element_type x1 -> x0, other arithmetic: 0.71 us -> none  [local(): return gated.astype(jnp.bfloat16)]
    unnamed x7 -> x1, local copies, waits for them, and re-layouts: 1.79 us -> 1.57 us
where the time goes in v19:
time: 55.7 us; the launch traced here: 55.6 us
  Pallas kernels  51.6 us (93%)
  local copies, waits for them, and re-layouts  2.7 us (5%)
  other arithmetic  1.29 us (2%)
    pallas_call x1, Pallas kernels, whole(): pl.pallas_call(whole_kernel, out_shape=jax.ShapeDtypeStruct((length, widt...  51.6 us
    unnamed x1, local copies, waits for them, and re-layouts  1.57 us
    convert_element_type x1, other arithmetic, local(): spec_rows = jnp.transpose(spec_rows, (4, 0, 1, 3, 2)).astype(jnp.bfloat16)  1.29 us
    convert_element_type x1, local copies, waits for them, and re-layouts, local(): spec_rows = jnp.transpose(spec_rows, (4, 0, 1, 3, 2)).astype(jnp.bfloat16)  1.13 us

profile of v19, /device:TPU:1, one launch (start us, length us, event | category | flops | bytes accessed | tf_op | source)
XLA Modules:
  0.0 55.6 jit_solution(17064451571075187652)
XLA Ops:
  0.0 1.3 %convert_element_type.9 = bf16[2,2,512,128]{3,2,1,0:T(8,128)(2,1)S(1)} convert(f32[2,2,512,128]{3,2,1,0:T(8,128)} %param.27) | non-fusion elementwise | flops 262144 | bytes 1572864 | tf_op jit(solution)/shard_map/convert_element_type | solution.py:310
  1.3 1.1 %copy.23 = bf16[2,2,128,4,128]{2,3,1,0,4:T(4,128)(2,1)} copy(bf16[2,2,128,4,128]{4,3,2,1,0:T(4,128)(2,1)S(1)} %bitcast.7) | data formatting | bytes 1048576 | tf_op jit(solution)/shard_map/convert_element_type | solution.py:310
  2.4 51.6 %shard_map.208 = bf16[512,128]{1,0:T(8,128)(2,1)} custom-call(bf16[512,128]{1,0:T(8,128)(2,1)} %refs_0_.1, bf16[512,128]{1,0:T(8,128)(2,1)} %refs_1_.1, f32[1,128]{1,0:T(1,128)} %bitcast.8, bf16[64,32,128]{2,1,0:T(8,128)(2,1)} %bitcast.6, bf16[512,128]{1,0:T(8,128)(2,1)} %refs_4_.1, f32[1,128]{1,0:T(1,128)} %bitcast.9, ...), custom_call_target="tpu_custom_call" | custom-call | tf_op jit(solution)/shard_map/pallas_call | solution.py:240
  54.1 1.6 %copy.25 = bf16[512,128]{1,0:T(8,128)(2,1)} copy(bf16[512,128]{1,0:T(8,128)(2,1)} %shard_map.208) | data formatting | bytes 262144

commit v20 on v19

--- a/solution.py
+++ b/solution.py
@@ -70,8 +70,7 @@
     loads = [pltpu.make_async_copy(held[k], tables[k], table_sems.at[k]) for k in range(table_count)]
     for load in loads:
         load.start()
-    for load in loads[:6]:
-        load.wait()
+    inputs = loads[:6]
     loads = loads[6:]
     feat_ref, gate_ref, gain_ref, spec_ref, post_ref, skip_ref = tables[:6]
     tables = tables[6:]
@@ -93,6 +92,7 @@
     for step in range(1, chans):
         peer = lax.rem(mine + step, chans)
         pl.semaphore_signal(barrier, inc=1, device_id={"chan": peer}, device_id_type=mesh_ids)
+    inputs[0].wait()
     feat = feat_ref[...].astype(jnp.float32)
     part = jnp.sum(jnp.transpose(feat * feat), axis=0, keepdims=True)
     sq_mine[...] = jnp.broadcast_to(part, sq_mine.shape)
@@ -129,6 +129,7 @@
 
     for step in range(1, chans):
         chan_copy(step).start()
+    inputs[3].wait()
     spec_src = lambda peer: spec_ref.at[peer]
     spec_own = pltpu.make_async_copy(spec_ref.at[me], spec_recv.at[me], own_sems.at[0])
     spec_own.start()
@@ -141,6 +142,8 @@
     for step in range(1, chans):
         other = lax.rem(mine + step, chans)
         total = total + sq_recv[other][0:1, :]
+    inputs[1].wait()
+    inputs[2].wait()
     scale = lax.rsqrt(total / CHANNELS + 1e-06)
     scale = jnp.transpose(jnp.broadcast_to(scale, (8, scale.shape[1])))[:, 0:1]
     signal = (feat * scale * gain_ref[...] * gate_ref[...].astype(jnp.float32)).astype(jnp.bfloat16)
@@ -217,6 +220,8 @@
     finish_all(res_src, res_dst, res_sems)
     res_own.wait()
 
+    inputs[4].wait()
+    inputs[5].wait()
     skip = skip_ref[...]
     for tile in range(tiles):
         for chan in range(pair):

time: 55.7 us -> 54.8 us (0.984)
  Pallas kernels: 51.6 us -> 50.7 us
    pallas_call x1, Pallas kernels: 51.6 us -> 50.7 us  [whole(): pl.pallas_call(whole_kernel, out_shape=jax.ShapeDtypeStruct((length, widt...]
where the time goes in v20:
time: 54.8 us; the launch traced here: 54.7 us
  Pallas kernels  50.7 us (93%)
  local copies, waits for them, and re-layouts  2.7 us (5%)
  other arithmetic  1.29 us (2%)
    pallas_call x1, Pallas kernels, whole(): pl.pallas_call(whole_kernel, out_shape=jax.ShapeDtypeStruct((length, widt...  50.7 us
    unnamed x1, local copies, waits for them, and re-layouts  1.57 us
    convert_element_type x1, other arithmetic, local(): spec_rows = jnp.transpose(spec_rows, (4, 0, 1, 3, 2)).astype(jnp.bfloat16)  1.29 us
    convert_element_type x1, local copies, waits for them, and re-layouts, local(): spec_rows = jnp.transpose(spec_rows, (4, 0, 1, 3, 2)).astype(jnp.bfloat16)  1.13 us

profile of v20, /device:TPU:1, one launch (start us, length us, event | category | flops | bytes accessed | tf_op | source)
XLA Modules:
  0.0 54.7 jit_solution(5884125441061993871)
XLA Ops:
  0.0 1.3 %convert_element_type.9 = bf16[2,2,512,128]{3,2,1,0:T(8,128)(2,1)S(1)} convert(f32[2,2,512,128]{3,2,1,0:T(8,128)} %param.27) | non-fusion elementwise | flops 262144 | bytes 1572864 | tf_op jit(solution)/shard_map/convert_element_type | solution.py:315
  1.3 1.1 %copy.23 = bf16[2,2,128,4,128]{2,3,1,0,4:T(4,128)(2,1)} copy(bf16[2,2,128,4,128]{4,3,2,1,0:T(4,128)(2,1)S(1)} %bitcast.7) | data formatting | bytes 1048576 | tf_op jit(solution)/shard_map/convert_element_type | solution.py:315
  2.4 50.7 %shard_map.208 = bf16[512,128]{1,0:T(8,128)(2,1)} custom-call(bf16[512,128]{1,0:T(8,128)(2,1)} %refs_0_.1, bf16[512,128]{1,0:T(8,128)(2,1)} %refs_1_.1, f32[1,128]{1,0:T(1,128)} %bitcast.8, bf16[64,32,128]{2,1,0:T(8,128)(2,1)} %bitcast.6, bf16[512,128]{1,0:T(8,128)(2,1)} %refs_4_.1, f32[1,128]{1,0:T(1,128)} %bitcast.9, ...), custom_call_target="tpu_custom_call" | custom-call | tf_op jit(solution)/shard_map/pallas_call | solution.py:245
  53.1 1.6 %copy.25 = bf16[512,128]{1,0:T(8,128)(2,1)} copy(bf16[512,128]{1,0:T(8,128)(2,1)} %shard_map.208) | data formatting | bytes 262144

commit v21 on v20

--- a/solution.py
+++ b/solution.py
@@ -129,11 +129,6 @@
 
     for step in range(1, chans):
         chan_copy(step).start()
-    inputs[3].wait()
-    spec_src = lambda peer: spec_ref.at[peer]
-    spec_own = pltpu.make_async_copy(spec_ref.at[me], spec_recv.at[me], own_sems.at[0])
-    spec_own.start()
-    start_all(spec_src, spec_recv.at[me], spec_sems)
     for step in range(1, chans):
         copy = chan_copy(step)
         copy.wait_send()
@@ -164,6 +159,11 @@
     sig_own = pltpu.make_async_copy(rows_of(sig_send)(me), rows_of(sig_recv)(me), own_sems.at[1])
     sig_own.start()
     start_all(rows_of(sig_send), rows_of(sig_recv)(me), sig_sems)
+    inputs[3].wait()
+    spec_src = lambda peer: spec_ref.at[peer]
+    spec_own = pltpu.make_async_copy(spec_ref.at[me], spec_recv.at[me], own_sems.at[0])
+    spec_own.start()
+    start_all(spec_src, spec_recv.at[me], spec_sems)
     finish_all(rows_of(sig_send), rows_of(sig_recv)(me), sig_sems)
     sig_own.wait()
 

time: 54.8 us -> 57.1 us (1.042)
  Pallas kernels: 50.7 us -> 53 us
    pallas_call x1, Pallas kernels: 50.7 us -> 53 us  [whole(): pl.pallas_call(whole_kernel, out_shape=jax.ShapeDtypeStruct((length, widt...]
where the time goes in v21:
time: 57.1 us; the launch traced here: 57 us
  Pallas kernels  53 us (93%)
  local copies, waits for them, and re-layouts  2.7 us (5%)
  other arithmetic  1.29 us (2%)
    pallas_call x1, Pallas kernels, whole(): pl.pallas_call(whole_kernel, out_shape=jax.ShapeDtypeStruct((length, widt...  53 us
    unnamed x1, local copies, waits for them, and re-layouts  1.57 us
    convert_element_type x1, other arithmetic, local(): spec_rows = jnp.transpose(spec_rows, (4, 0, 1, 3, 2)).astype(jnp.bfloat16)  1.29 us

profile of v21, /device:TPU:1, one launch (start us, length us, event | category | flops | bytes accessed | tf_op | source)
XLA Modules:
  0.0 57.0 jit_solution(14849896237161754486)
XLA Ops:
  0.0 1.3 %convert_element_type.9 = bf16[2,2,512,128]{3,2,1,0:T(8,128)(2,1)S(1)} convert(f32[2,2,512,128]{3,2,1,0:T(8,128)} %param.27) | non-fusion elementwise | flops 262144 | bytes 1572864 | tf_op jit(solution)/shard_map/convert_element_type | solution.py:315
  1.3 1.1 %copy.23 = bf16[2,2,128,4,128]{2,3,1,0,4:T(4,128)(2,1)} copy(bf16[2,2,128,4,128]{4,3,2,1,0:T(4,128)(2,1)S(1)} %bitcast.7) | data formatting | bytes 1048576 | tf_op jit(solution)/shard_map/convert_element_type | solution.py:315
  2.4 53.0 %shard_map.208 = bf16[512,128]{1,0:T(8,128)(2,1)} custom-call(bf16[512,128]{1,0:T(8,128)(2,1)} %refs_0_.1, bf16[512,128]{1,0:T(8,128)(2,1)} %refs_1_.1, f32[1,128]{1,0:T(1,128)} %bitcast.8, bf16[64,32,128]{2,1,0:T(8,128)(2,1)} %bitcast.6, bf16[512,128]{1,0:T(8,128)(2,1)} %refs_4_.1, f32[1,128]{1,0:T(1,128)} %bitcast.9, ...), custom_call_target="tpu_custom_call" | custom-call | tf_op jit(solution)/shard_map/pallas_call | solution.py:245
  55.5 1.6 %copy.25 = bf16[512,128]{1,0:T(8,128)(2,1)} copy(bf16[512,128]{1,0:T(8,128)(2,1)} %shard_map.208) | data formatting | bytes 262144

commit v22 on v20

--- a/solution.py
+++ b/solution.py
@@ -65,8 +65,8 @@
     held = refs[:table_count]
     gated_out = refs[table_count]
     (sq_mine, sq_recv, sig_turn, sig_send, sig_recv, spec_recv, cols, conv_one, conv_send, res_recv,
-     spec_sems, sig_sems, res_sems, chan_sems, own_sems, table_sems) = refs[table_count + 1:table_count + 17]
-    tables = refs[table_count + 17:]
+     wire_out, wire_in, spec_sems, sig_sems, res_sems, chan_sems, own_sems, table_sems) = refs[table_count + 1:table_count + 19]
+    tables = refs[table_count + 19:]
     loads = [pltpu.make_async_copy(held[k], tables[k], table_sems.at[k]) for k in range(table_count)]
     for load in loads:
         load.start()
@@ -161,11 +161,13 @@
     def rows_of(buffer):
         return lambda peer: buffer.at[pl.ds(pl.multiple_of(peer * chunk, chunk), chunk)]
 
-    sig_own = pltpu.make_async_copy(rows_of(sig_send)(me), rows_of(sig_recv)(me), own_sems.at[1])
+    wire_out[...] = sig_send[...].astype(wire_out.dtype)
+    sig_own = pltpu.make_async_copy(rows_of(wire_out)(me), rows_of(wire_in)(me), own_sems.at[1])
     sig_own.start()
-    start_all(rows_of(sig_send), rows_of(sig_recv)(me), sig_sems)
-    finish_all(rows_of(sig_send), rows_of(sig_recv)(me), sig_sems)
+    start_all(rows_of(wire_out), rows_of(wire_in)(me), sig_sems)
+    finish_all(rows_of(wire_out), rows_of(wire_in)(me), sig_sems)
     sig_own.wait()
+    sig_recv[...] = wire_in[...].astype(jnp.float32)
 
     for chan in range(pair):
         for tile in range(tiles):
@@ -258,6 +260,8 @@
             pltpu.VMEM((count * chunk // pair, lanes), jnp.float32),
             pltpu.VMEM((count * chunk, lanes), jnp.float32),
             pltpu.VMEM((count * chunk, lanes), jnp.float32),
+            pltpu.VMEM((count * chunk, lanes), jnp.bfloat16),
+            pltpu.VMEM((count * chunk, lanes), jnp.bfloat16),
             pltpu.SemaphoreType.DMA((2, count)),
             pltpu.SemaphoreType.DMA((2, count)),
             pltpu.SemaphoreType.DMA((2, count)),

time: 54.8 us -> 53 us (0.967)
  Pallas kernels: 50.7 us -> 48.9 us
    pallas_call x1, Pallas kernels: 50.7 us -> 48.9 us  [whole(): pl.pallas_call(whole_kernel, out_shape=jax.ShapeDtypeStruct((length, widt...]
where the time goes in v22:
time: 53 us; the launch traced here: 52.9 us
  Pallas kernels  48.9 us (92%)
  local copies, waits for them, and re-layouts  2.7 us (5%)
  other arithmetic  1.29 us (2%)
    pallas_call x1, Pallas kernels, whole(): pl.pallas_call(whole_kernel, out_shape=jax.ShapeDtypeStruct((length, widt...  48.9 us
    unnamed x1, local copies, waits for them, and re-layouts  1.57 us
    convert_element_type x1, other arithmetic, local(): spec_rows = jnp.transpose(spec_rows, (4, 0, 1, 3, 2)).astype(jnp.bfloat16)  1.29 us
    convert_element_type x1, local copies, waits for them, and re-layouts, local(): spec_rows = jnp.transpose(spec_rows, (4, 0, 1, 3, 2)).astype(jnp.bfloat16)  1.13 us

profile of v22, /device:TPU:1, one launch (start us, length us, event | category | flops | bytes accessed | tf_op | source)
XLA Modules:
  0.0 52.9 jit_solution(8947084894007145400)
XLA Ops:
  0.0 1.3 %convert_element_type.9 = bf16[2,2,512,128]{3,2,1,0:T(8,128)(2,1)S(1)} convert(f32[2,2,512,128]{3,2,1,0:T(8,128)} %param.27) | non-fusion elementwise | flops 262144 | bytes 1572864 | tf_op jit(solution)/shard_map/convert_element_type | solution.py:319
  1.3 1.1 %copy.23 = bf16[2,2,128,4,128]{2,3,1,0,4:T(4,128)(2,1)} copy(bf16[2,2,128,4,128]{4,3,2,1,0:T(4,128)(2,1)S(1)} %bitcast.7) | data formatting | bytes 1048576 | tf_op jit(solution)/shard_map/convert_element_type | solution.py:319
  2.4 48.9 %shard_map.208 = bf16[512,128]{1,0:T(8,128)(2,1)} custom-call(bf16[512,128]{1,0:T(8,128)(2,1)} %refs_0_.1, bf16[512,128]{1,0:T(8,128)(2,1)} %refs_1_.1, f32[1,128]{1,0:T(1,128)} %bitcast.8, bf16[64,32,128]{2,1,0:T(8,128)(2,1)} %bitcast.6, bf16[512,128]{1,0:T(8,128)(2,1)} %refs_4_.1, f32[1,128]{1,0:T(1,128)} %bitcast.9, ...), custom_call_target="tpu_custom_call" | custom-call | tf_op jit(solution)/shard_map/pallas_call | solution.py:247
  51.3 1.6 %copy.25 = bf16[512,128]{1,0:T(8,128)(2,1)} copy(bf16[512,128]{1,0:T(8,128)(2,1)} %shard_map.208) | data formatting | bytes 262144

commit v23 on v22

--- a/solution.py
+++ b/solution.py
@@ -65,8 +65,9 @@
     held = refs[:table_count]
     gated_out = refs[table_count]
     (sq_mine, sq_recv, sig_turn, sig_send, sig_recv, spec_recv, cols, conv_one, conv_send, res_recv,
-     wire_out, wire_in, spec_sems, sig_sems, res_sems, chan_sems, own_sems, table_sems) = refs[table_count + 1:table_count + 19]
-    tables = refs[table_count + 19:]
+     wire_out, wire_in, res_out, res_in, spec_sems, sig_sems, res_sems, chan_sems, own_sems, table_sems) = (
+        refs[table_count + 1:table_count + 21])
+    tables = refs[table_count + 21:]
     loads = [pltpu.make_async_copy(held[k], tables[k], table_sems.at[k]) for k in range(table_count)]
     for load in loads:
         load.start()
@@ -214,13 +215,15 @@
             rows = conv_one[pl.ds(tile, count, stride=tiles), :]
             conv_send[pl.ds(tiles * chan + tile, count, stride=chunk), :] = rows
 
-    res_src = rows_of(conv_send)
-    res_dst = rows_of(res_recv)(me)
+    res_out[...] = conv_send[...].astype(res_out.dtype)
+    res_src = rows_of(res_out)
+    res_dst = rows_of(res_in)(me)
     res_own = pltpu.make_async_copy(res_src(me), res_dst, own_sems.at[2])
     res_own.start()
     start_all(res_src, res_dst, res_sems)
     finish_all(res_src, res_dst, res_sems)
     res_own.wait()
+    res_recv[...] = res_in[...].astype(jnp.float32)
 
     inputs[4].wait()
     inputs[5].wait()
@@ -262,6 +265,8 @@
             pltpu.VMEM((count * chunk, lanes), jnp.float32),
             pltpu.VMEM((count * chunk, lanes), jnp.bfloat16),
             pltpu.VMEM((count * chunk, lanes), jnp.bfloat16),
+            pltpu.VMEM((count * chunk, lanes), jnp.bfloat16),
+            pltpu.VMEM((count * chunk, lanes), jnp.bfloat16),
             pltpu.SemaphoreType.DMA((2, count)),
             pltpu.SemaphoreType.DMA((2, count)),
             pltpu.SemaphoreType.DMA((2, count)),

time: 53 us -> 50.7 us (0.957)
  Pallas kernels: 48.9 us -> 46.5 us
    pallas_call x1, Pallas kernels: 48.9 us -> 46.5 us  [whole(): pl.pallas_call(whole_kernel, out_shape=jax.ShapeDtypeStruct((length, widt...]
where the time goes in v23:
time: 50.7 us; the launch traced here: 50.5 us
  Pallas kernels  46.5 us (92%)
  local copies, waits for them, and re-layouts  2.7 us (5%)
  other arithmetic  1.29 us (3%)
    pallas_call x1, Pallas kernels, whole(): pl.pallas_call(whole_kernel, out_shape=jax.ShapeDtypeStruct((length, widt...  46.5 us
    unnamed x1, local copies, waits for them, and re-layouts  1.57 us
    convert_element_type x1, other arithmetic, local(): spec_rows = jnp.transpose(spec_rows, (4, 0, 1, 3, 2)).astype(jnp.bfloat16)  1.29 us
    convert_element_type x1, local copies, waits for them, and re-layouts, local(): spec_rows = jnp.transpose(spec_rows, (4, 0, 1, 3, 2)).astype(jnp.bfloat16)  1.13 us

profile of v23, /device:TPU:1, one launch (start us, length us, event | category | flops | bytes accessed | tf_op | source)
XLA Modules:
  0.0 50.5 jit_solution(14574934830986498964)
XLA Ops:
  0.0 1.3 %convert_element_type.9 = bf16[2,2,512,128]{3,2,1,0:T(8,128)(2,1)S(1)} convert(f32[2,2,512,128]{3,2,1,0:T(8,128)} %param.27) | non-fusion elementwise | flops 262144 | bytes 1572864 | tf_op jit(solution)/shard_map/convert_element_type | solution.py:324
  1.3 1.1 %copy.23 = bf16[2,2,128,4,128]{2,3,1,0,4:T(4,128)(2,1)} copy(bf16[2,2,128,4,128]{4,3,2,1,0:T(4,128)(2,1)S(1)} %bitcast.7) | data formatting | bytes 1048576 | tf_op jit(solution)/shard_map/convert_element_type | solution.py:324
  2.4 46.5 %shard_map.208 = bf16[512,128]{1,0:T(8,128)(2,1)} custom-call(bf16[512,128]{1,0:T(8,128)(2,1)} %refs_0_.1, bf16[512,128]{1,0:T(8,128)(2,1)} %refs_1_.1, f32[1,128]{1,0:T(1,128)} %bitcast.8, bf16[64,32,128]{2,1,0:T(8,128)(2,1)} %bitcast.6, bf16[512,128]{1,0:T(8,128)(2,1)} %refs_4_.1, f32[1,128]{1,0:T(1,128)} %bitcast.9, ...), custom_call_target="tpu_custom_call" | custom-call | tf_op jit(solution)/shard_map/pallas_call | solution.py:250
  49.0 1.6 %copy.25 = bf16[512,128]{1,0:T(8,128)(2,1)} copy(bf16[512,128]{1,0:T(8,128)(2,1)} %shard_map.208) | data formatting | bytes 262144

commit v24 on v23

--- a/solution.py
+++ b/solution.py
@@ -52,12 +52,8 @@
 
 def dot3(left, right):
     if isinstance(left, tuple):
-        d_hi, d_lo = split(right)
-        out = jnp.dot(left[0], d_hi, preferred_element_type=jnp.float32)
-        return out + jnp.dot(left[0], d_lo, preferred_element_type=jnp.float32)
-    d_hi, d_lo = split(left)
-    out = jnp.dot(d_hi, right[0], preferred_element_type=jnp.float32)
-    return out + jnp.dot(d_lo, right[0], preferred_element_type=jnp.float32)
+        return jnp.dot(left[0], right.astype(jnp.bfloat16), preferred_element_type=jnp.float32)
+    return jnp.dot(left.astype(jnp.bfloat16), right[0], preferred_element_type=jnp.float32)
 
 
 def whole_kernel(*refs):

time: 50.7 us -> 49.5 us (0.976)
  Pallas kernels: 46.5 us -> 45.4 us
    pallas_call x1, Pallas kernels: 46.5 us -> 45.4 us  [whole(): pl.pallas_call(whole_kernel, out_shape=jax.ShapeDtypeStruct((length, widt...]
where the time goes in v24:
time: 49.5 us; the launch traced here: 49.4 us
  Pallas kernels  45.4 us (92%)
  local copies, waits for them, and re-layouts  2.7 us (5%)
  other arithmetic  1.29 us (3%)
    pallas_call x1, Pallas kernels, whole(): pl.pallas_call(whole_kernel, out_shape=jax.ShapeDtypeStruct((length, widt...  45.4 us
    unnamed x1, local copies, waits for them, and re-layouts  1.57 us
    convert_element_type x1, other arithmetic, local(): spec_rows = jnp.transpose(spec_rows, (4, 0, 1, 3, 2)).astype(jnp.bfloat16)  1.29 us
    convert_element_type x1, local copies, waits for them, and re-layouts, local(): spec_rows = jnp.transpose(spec_rows, (4, 0, 1, 3, 2)).astype(jnp.bfloat16)  1.13 us

profile of v24, /device:TPU:1, one launch (start us, length us, event | category | flops | bytes accessed | tf_op | source)
XLA Modules:
  0.0 49.4 jit_solution(18292870831172030624)
XLA Ops:
  0.0 1.3 %convert_element_type.9 = bf16[2,2,512,128]{3,2,1,0:T(8,128)(2,1)S(1)} convert(f32[2,2,512,128]{3,2,1,0:T(8,128)} %param.27) | non-fusion elementwise | flops 262144 | bytes 1572864 | tf_op jit(solution)/shard_map/convert_element_type | solution.py:320
  1.3 1.1 %copy.23 = bf16[2,2,128,4,128]{2,3,1,0,4:T(4,128)(2,1)} copy(bf16[2,2,128,4,128]{4,3,2,1,0:T(4,128)(2,1)S(1)} %bitcast.7) | data formatting | bytes 1048576 | tf_op jit(solution)/shard_map/convert_element_type | solution.py:320
  2.4 45.4 %shard_map.208 = bf16[512,128]{1,0:T(8,128)(2,1)} custom-call(bf16[512,128]{1,0:T(8,128)(2,1)} %refs_0_.1, bf16[512,128]{1,0:T(8,128)(2,1)} %refs_1_.1, f32[1,128]{1,0:T(1,128)} %bitcast.8, bf16[64,32,128]{2,1,0:T(8,128)(2,1)} %bitcast.6, bf16[512,128]{1,0:T(8,128)(2,1)} %refs_4_.1, f32[1,128]{1,0:T(1,128)} %bitcast.9, ...), custom_call_target="tpu_custom_call" | custom-call | tf_op jit(solution)/shard_map/pallas_call | solution.py:246
  47.8 1.6 %copy.25 = bf16[512,128]{1,0:T(8,128)(2,1)} copy(bf16[512,128]{1,0:T(8,128)(2,1)} %shard_map.208) | data formatting | bytes 262144

commit v25 on v24

--- a/solution.py
+++ b/solution.py
@@ -61,9 +61,9 @@
     held = refs[:table_count]
     gated_out = refs[table_count]
     (sq_mine, sq_recv, sig_turn, sig_send, sig_recv, spec_recv, cols, conv_one, conv_send, res_recv,
-     wire_out, wire_in, res_out, res_in, spec_sems, sig_sems, res_sems, chan_sems, own_sems, table_sems) = (
-        refs[table_count + 1:table_count + 21])
-    tables = refs[table_count + 21:]
+     wire_out, wire_in, res_out, res_in, spec_send, spec_sems, sig_sems, res_sems, chan_sems, own_sems, table_sems) = (
+        refs[table_count + 1:table_count + 22])
+    tables = refs[table_count + 22:]
     loads = [pltpu.make_async_copy(held[k], tables[k], table_sems.at[k]) for k in range(table_count)]
     for load in loads:
         load.start()
@@ -127,8 +127,9 @@
     for step in range(1, chans):
         chan_copy(step).start()
     inputs[3].wait()
-    spec_src = lambda peer: spec_ref.at[peer]
-    spec_own = pltpu.make_async_copy(spec_ref.at[me], spec_recv.at[me], own_sems.at[0])
+    spec_send[...] = spec_ref[...].astype(spec_send.dtype)
+    spec_src = lambda peer: spec_send.at[peer]
+    spec_own = pltpu.make_async_copy(spec_send.at[me], spec_recv.at[me], own_sems.at[0])
     spec_own.start()
     start_all(spec_src, spec_recv.at[me], spec_sems)
     for step in range(1, chans):
@@ -254,7 +255,7 @@
             pltpu.VMEM((lanes, lanes), jnp.float32),
             pltpu.VMEM((count * chunk, lanes), jnp.float32),
             pltpu.VMEM((count * chunk, lanes), jnp.float32),
-            pltpu.VMEM(spec_rows.shape, spec_rows.dtype),
+            pltpu.VMEM(spec_rows.shape, jnp.bfloat16),
             pltpu.VMEM((pair, count * chunk // pair, lanes), jnp.float32),
             pltpu.VMEM((count * chunk // pair, lanes), jnp.float32),
             pltpu.VMEM((count * chunk, lanes), jnp.float32),
@@ -263,6 +264,7 @@
             pltpu.VMEM((count * chunk, lanes), jnp.bfloat16),
             pltpu.VMEM((count * chunk, lanes), jnp.bfloat16),
             pltpu.VMEM((count * chunk, lanes), jnp.bfloat16),
+            pltpu.VMEM(spec_rows.shape, jnp.bfloat16),
             pltpu.SemaphoreType.DMA((2, count)),
             pltpu.SemaphoreType.DMA((2, count)),
             pltpu.SemaphoreType.DMA((2, count)),
@@ -317,8 +319,7 @@
     tok_tiles = tok_rows // lanes
 
     spec_rows = spectrum.reshape(2, 2, second_len, ROW_GROUP, chan_width)
-    spec_rows = jnp.transpose(spec_rows, (4, 0, 1, 3, 2)).astype(jnp.bfloat16)
-    spec_rows = spec_rows.reshape(seq_count, -1, second_len)
+    spec_rows = jnp.transpose(spec_rows, (4, 0, 1, 3, 2)).reshape(seq_count, -1, second_len)
     return whole(
         features, pre_gate, norm_gain.reshape(1, chan_width), spec_rows,
         post_gate, skip_weight.reshape(1, chan_width), dft_tables(seq_count, tok_rows), chans,

time: 49.5 us -> 49.5 us (level)
  other arithmetic: 1.29 us -> 0 us
  local copies, waits for them, and re-layouts: 2.7 us -> 3.88 us
    reshape x0 -> x1, local copies, waits for them, and re-layouts: none -> 2.31 us  [local(): spec_rows = spectrum.reshape(2, 2, second_len, ROW_GROUP, chan_width)]
    convert_element_type x1 -> x0, other arithmetic: 1.29 us -> none  [local(): spec_rows = jnp.transpose(spec_rows, (4, 0, 1, 3, 2)).astype(jnp.bfloat16)]
    convert_element_type x1 -> x0, local copies, waits for them, and re-layouts: 1.13 us -> none  [local(): spec_rows = jnp.transpose(spec_rows, (4, 0, 1, 3, 2)).astype(jnp.bfloat16)]
where the time goes in v25:
time: 49.5 us; the launch traced here: 49.4 us
  Pallas kernels  45.5 us (92%)
  local copies, waits for them, and re-layouts  3.88 us (8%)
    pallas_call x1, Pallas kernels, whole(): pl.pallas_call(whole_kernel, out_shape=jax.ShapeDtypeStruct((length, widt...  45.5 us
    reshape x1, local copies, waits for them, and re-layouts, local(): spec_rows = spectrum.reshape(2, 2, second_len, ROW_GROUP, chan_width)  2.31 us
    unnamed x1, local copies, waits for them, and re-layouts  1.57 us

profile of v25, /device:TPU:1, one launch (start us, length us, event | category | flops | bytes accessed | tf_op | source)
XLA Modules:
  0.0 49.4 jit_solution(1778287792919463094)
XLA Ops:
  0.0 2.3 %copy.23 = f32[2,2,128,4,128]{2,3,1,0,4:T(4,128)} copy(f32[2,2,128,4,128]{4,3,2,1,0:T(4,128)} %bitcast.7) | data formatting | bytes 2097152 | tf_op jit(solution)/shard_map/reshape | solution.py:321
  2.3 45.5 %shard_map.208 = bf16[512,128]{1,0:T(8,128)(2,1)} custom-call(bf16[512,128]{1,0:T(8,128)(2,1)} %refs_0_.1, bf16[512,128]{1,0:T(8,128)(2,1)} %refs_1_.1, f32[1,128]{1,0:T(1,128)} %bitcast.8, f32[64,32,128]{2,1,0:T(8,128)} %bitcast.6, bf16[512,128]{1,0:T(8,128)(2,1)} %refs_4_.1, f32[1,128]{1,0:T(1,128)} %bitcast.9, bf16[1024,256]{1,0:T(8,128)(2,1)} %constant.32.clone.refs_6_, ...), custom_call_target="tpu_custom_call" | custom-call | tf_op jit(solution)/shard_map/pallas_call | solution.py:247
  47.8 1.6 %copy.25 = bf16[512,128]{1,0:T(8,128)(2,1)} copy(bf16[512,128]{1,0:T(8,128)(2,1)} %shard_map.208) | data formatting | bytes 262144

commit v26 on v25

--- a/solution.py
+++ b/solution.py
@@ -93,6 +93,8 @@
     feat = feat_ref[...].astype(jnp.float32)
     part = jnp.sum(jnp.transpose(feat * feat), axis=0, keepdims=True)
     sq_mine[...] = jnp.broadcast_to(part, sq_mine.shape)
+    inputs[3].wait()
+    spec_send[...] = spec_ref[...].astype(spec_send.dtype)
     pl.semaphore_wait(barrier, count + chans - 2)
 
     def seq_copy(source, target, sems, step):
@@ -126,8 +128,6 @@
 
     for step in range(1, chans):
         chan_copy(step).start()
-    inputs[3].wait()
-    spec_send[...] = spec_ref[...].astype(spec_send.dtype)
     spec_src = lambda peer: spec_send.at[peer]
     spec_own = pltpu.make_async_copy(spec_send.at[me], spec_recv.at[me], own_sems.at[0])
     spec_own.start()

time: 49.5 us -> 49.3 us (level)
  no operation moved by 1% of the time
where the time goes in v26:
time: 49.3 us; the launch traced here: 49.2 us
  Pallas kernels  45.3 us (92%)
  local copies, waits for them, and re-layouts  3.88 us (8%)
    pallas_call x1, Pallas kernels, whole(): pl.pallas_call(whole_kernel, out_shape=jax.ShapeDtypeStruct((length, widt...  45.3 us
    reshape x1, local copies, waits for them, and re-layouts, local(): spec_rows = spectrum.reshape(2, 2, second_len, ROW_GROUP, chan_width)  2.31 us
    unnamed x1, local copies, waits for them, and re-layouts  1.57 us

profile of v26, /device:TPU:1, one launch (start us, length us, event | category | flops | bytes accessed | tf_op | source)
XLA Modules:
  0.0 49.2 jit_solution(11157150380167531645)
XLA Ops:
  0.0 2.3 %copy.23 = f32[2,2,128,4,128]{2,3,1,0,4:T(4,128)} copy(f32[2,2,128,4,128]{4,3,2,1,0:T(4,128)} %bitcast.7) | data formatting | bytes 2097152 | tf_op jit(solution)/shard_map/reshape | solution.py:321
  2.3 45.3 %shard_map.208 = bf16[512,128]{1,0:T(8,128)(2,1)} custom-call(bf16[512,128]{1,0:T(8,128)(2,1)} %refs_0_.1, bf16[512,128]{1,0:T(8,128)(2,1)} %refs_1_.1, f32[1,128]{1,0:T(1,128)} %bitcast.8, f32[64,32,128]{2,1,0:T(8,128)} %bitcast.6, bf16[512,128]{1,0:T(8,128)(2,1)} %refs_4_.1, f32[1,128]{1,0:T(1,128)} %bitcast.9, bf16[1024,256]{1,0:T(8,128)(2,1)} %constant.32.clone.refs_6_, ...), custom_call_target="tpu_custom_call" | custom-call | tf_op jit(solution)/shard_map/pallas_call | solution.py:247
  47.7 1.6 %copy.25 = bf16[512,128]{1,0:T(8,128)(2,1)} copy(bf16[512,128]{1,0:T(8,128)(2,1)} %shard_map.208) | data formatting | bytes 262144

commit v27 on v26

--- a/solution.py
+++ b/solution.py
@@ -10,8 +10,7 @@
 
 CHANNELS = 512
 ROW_GROUP = 4
-TABLE_NAMES = ("st_hi", "st_lo", "tc", "ts", "fa_hi", "fa_lo", "fb_hi", "fb_lo", "ia_hi", "ia_lo", "ib_hi", "ib_lo",
-               "lc_hi", "lc_lo", "ls_hi", "ls_lo")
+TABLE_NAMES = ("st", "tc", "ts", "fa", "fb", "ia", "ib", "lc", "ls")
 HIGH_DIGIT = 8
 
 
@@ -71,8 +70,7 @@
     loads = loads[6:]
     feat_ref, gate_ref, gain_ref, spec_ref, post_ref, skip_ref = tables[:6]
     tables = tables[6:]
-    (st_hi, st_lo, tc_ref, ts_ref, fa_hi, fa_lo, fb_hi, fb_lo, ia_hi, ia_lo, ib_hi, ib_lo,
-     lc_hi, lc_lo, ls_hi, ls_lo) = tables
+    (st_hi, tc_ref, ts_ref, fa_hi, fb_hi, ia_hi, ib_hi, lc_hi, ls_hi) = tables
     count = spec_ref.shape[0]
     chans = sq_recv.shape[0]
     me = lax.axis_index("seq")
@@ -188,7 +186,7 @@
         p_sin = boths[chan][first_len:]
         twist_re = p_cos * cos_twist - p_sin * sin_twist
         twist_im = -p_sin * cos_twist - p_cos * sin_twist
-        freqs.append(dot3(twist_re, (fa_hi[...], fa_lo[...])) + dot3(twist_im, (fb_hi[...], fb_lo[...])))
+        freqs.append(dot3(twist_re, (fa_hi[...],)) + dot3(twist_im, (fb_hi[...],)))
 
     finish_all(spec_src, spec_recv.at[me], spec_sems)
     spec_own.wait()
@@ -203,11 +201,11 @@
         filt_re, filt_im = filt
         prod_re = freq_re * filt_re - freq_im * filt_im
         prod_im = freq_re * filt_im + freq_im * filt_re
-        back = dot3(prod_re, (ia_hi[...], ia_lo[...])) + dot3(prod_im, (ib_hi[...], ib_lo[...]))
+        back = dot3(prod_re, (ia_hi[...],)) + dot3(prod_im, (ib_hi[...],))
         back_re, back_im = back[:, :lanes], back[:, lanes:]
         untwist_re = back_re * cos_twist - back_im * sin_twist
         untwist_im = back_im * cos_twist + back_re * sin_twist
-        conv_one[...] = dot3((lc_hi[...], lc_lo[...]), untwist_re) + dot3((ls_hi[...], ls_lo[...]), untwist_im)
+        conv_one[...] = dot3((lc_hi[...],), untwist_re) + dot3((ls_hi[...],), untwist_im)
         for tile in range(tiles):
             rows = conv_one[pl.ds(tile, count, stride=tiles), :]
             conv_send[pl.ds(tiles * chan + tile, count, stride=chunk), :] = rows
@@ -294,9 +292,7 @@
     cos_second, sin_second = np.cos(second_turn), np.sin(second_turn)
 
     def pair_of(array):
-        array = array.astype(np.float32)
-        high = array.astype(jnp.bfloat16)
-        return [jnp.asarray(high), jnp.asarray((array - high.astype(np.float32)).astype(jnp.bfloat16))]
+        return [jnp.asarray(array.astype(np.float32).astype(jnp.bfloat16))]
 
     tables = pair_of(np.concatenate([cos_first, sin_first], 0))
     tables += [jnp.asarray(np.cos(twist_turn).astype(np.float32)), jnp.asarray(np.sin(twist_turn).astype(np.float32))]

time: 49.3 us -> 49.3 us (level)
  no operation moved by 1% of the time
where the time goes in v27:
time: 49.3 us; the launch traced here: 49.1 us
  Pallas kernels  45.3 us (92%)
  local copies, waits for them, and re-layouts  3.88 us (8%)
    pallas_call x1, Pallas kernels, whole(): pl.pallas_call(whole_kernel, out_shape=jax.ShapeDtypeStruct((length, widt...  45.3 us
    reshape x1, local copies, waits for them, and re-layouts, local(): spec_rows = spectrum.reshape(2, 2, second_len, ROW_GROUP, chan_width)  2.31 us
    unnamed x1, local copies, waits for them, and re-layouts  1.57 us

profile of v27, /device:TPU:1, one launch (start us, length us, event | category | flops | bytes accessed | tf_op | source)
XLA Modules:
  0.0 49.1 jit_solution(9912920969926290530)
XLA Ops:
  0.0 2.3 %copy.16 = f32[2,2,128,4,128]{2,3,1,0,4:T(4,128)} copy(f32[2,2,128,4,128]{4,3,2,1,0:T(4,128)} %bitcast.7) | data formatting | bytes 2097152 | tf_op jit(solution)/shard_map/reshape | solution.py:317
  2.3 45.3 %shard_map.145 = bf16[512,128]{1,0:T(8,128)(2,1)} custom-call(bf16[512,128]{1,0:T(8,128)(2,1)} %refs_0_.1, bf16[512,128]{1,0:T(8,128)(2,1)} %refs_1_.1, f32[1,128]{1,0:T(1,128)} %bitcast.8, f32[64,32,128]{2,1,0:T(8,128)} %bitcast.6, bf16[512,128]{1,0:T(8,128)(2,1)} %refs_4_.1, f32[1,128]{1,0:T(1,128)} %bitcast.9, bf16[1024,256]{1,0:T(8,128)(2,1)} %constant.18.clone.refs_6_, ...), custom_call_target="tpu_custom_call" | custom-call | tf_op jit(solution)/shard_map/pallas_call | solution.py:245
  47.6 1.6 %copy.18 = bf16[512,128]{1,0:T(8,128)(2,1)} copy(bf16[512,128]{1,0:T(8,128)(2,1)} %shard_map.145) | data formatting | bytes 262144

commit v28 on v27

--- a/solution.py
+++ b/solution.py
@@ -129,7 +129,11 @@
     spec_src = lambda peer: spec_send.at[peer]
     spec_own = pltpu.make_async_copy(spec_send.at[me], spec_recv.at[me], own_sems.at[0])
     spec_own.start()
-    start_all(spec_src, spec_recv.at[me], spec_sems)
+    z_step = HIGH_DIGIT
+    z_count = count // z_step
+    far_first = sorted(range(1, count), key=lambda s: -min(s // z_step, z_count - s // z_step))
+    for step in far_first:
+        seq_copy(spec_src, spec_recv.at[me], spec_sems, step).start()
     for step in range(1, chans):
         copy = chan_copy(step)
         copy.wait_send()

time: 49.3 us -> 48.9 us (level)
  no operation moved by 1% of the time
where the time goes in v28:
time: 48.9 us; the launch traced here: 48.8 us
  Pallas kernels  44.9 us (92%)
  local copies, waits for them, and re-layouts  3.88 us (8%)
    pallas_call x1, Pallas kernels, whole(): pl.pallas_call(whole_kernel, out_shape=jax.ShapeDtypeStruct((length, widt...  44.9 us
    reshape x1, local copies, waits for them, and re-layouts, local(): spec_rows = spectrum.reshape(2, 2, second_len, ROW_GROUP, chan_width)  2.31 us
    unnamed x1, local copies, waits for them, and re-layouts  1.57 us

profile of v28, /device:TPU:1, one launch (start us, length us, event | category | flops | bytes accessed | tf_op | source)
XLA Modules:
  0.0 48.8 jit_solution(6499612064656965374)
XLA Ops:
  0.0 2.3 %copy.16 = f32[2,2,128,4,128]{2,3,1,0,4:T(4,128)} copy(f32[2,2,128,4,128]{4,3,2,1,0:T(4,128)} %bitcast.7) | data formatting | bytes 2097152 | tf_op jit(solution)/shard_map/reshape | solution.py:321
  2.3 44.9 %shard_map.145 = bf16[512,128]{1,0:T(8,128)(2,1)} custom-call(bf16[512,128]{1,0:T(8,128)(2,1)} %refs_0_.1, bf16[512,128]{1,0:T(8,128)(2,1)} %refs_1_.1, f32[1,128]{1,0:T(1,128)} %bitcast.8, f32[64,32,128]{2,1,0:T(8,128)} %bitcast.6, bf16[512,128]{1,0:T(8,128)(2,1)} %refs_4_.1, f32[1,128]{1,0:T(1,128)} %bitcast.9, bf16[1024,256]{1,0:T(8,128)(2,1)} %constant.18.clone.refs_6_, ...), custom_call_target="tpu_custom_call" | custom-call | tf_op jit(solution)/shard_map/pallas_call | solution.py:249
  47.2 1.6 %copy.18 = bf16[512,128]{1,0:T(8,128)(2,1)} copy(bf16[512,128]{1,0:T(8,128)(2,1)} %shard_map.145) | data formatting | bytes 262144

commit v29 on v27

--- a/solution.py
+++ b/solution.py
@@ -10,7 +10,7 @@
 
 CHANNELS = 512
 ROW_GROUP = 4
-TABLE_NAMES = ("st", "tc", "ts", "fa", "fb", "ia", "ib", "lc", "ls")
+TABLE_NAMES = ("st", "tc", "ts", "fab", "iab", "lc", "ls")
 HIGH_DIGIT = 8
 
 
@@ -70,7 +70,7 @@
     loads = loads[6:]
     feat_ref, gate_ref, gain_ref, spec_ref, post_ref, skip_ref = tables[:6]
     tables = tables[6:]
-    (st_hi, tc_ref, ts_ref, fa_hi, fb_hi, ia_hi, ib_hi, lc_hi, ls_hi) = tables
+    (st_hi, tc_ref, ts_ref, fab_hi, iab_hi, lc_hi, ls_hi) = tables
     count = spec_ref.shape[0]
     chans = sq_recv.shape[0]
     me = lax.axis_index("seq")
@@ -186,7 +186,7 @@
         p_sin = boths[chan][first_len:]
         twist_re = p_cos * cos_twist - p_sin * sin_twist
         twist_im = -p_sin * cos_twist - p_cos * sin_twist
-        freqs.append(dot3(twist_re, (fa_hi[...],)) + dot3(twist_im, (fb_hi[...],)))
+        freqs.append(dot3(jnp.concatenate([twist_re, twist_im], axis=1), (fab_hi[...],)))
 
     finish_all(spec_src, spec_recv.at[me], spec_sems)
     spec_own.wait()
@@ -201,7 +201,7 @@
         filt_re, filt_im = filt
         prod_re = freq_re * filt_re - freq_im * filt_im
         prod_im = freq_re * filt_im + freq_im * filt_re
-        back = dot3(prod_re, (ia_hi[...],)) + dot3(prod_im, (ib_hi[...],))
+        back = dot3(jnp.concatenate([prod_re, prod_im], axis=1), (iab_hi[...],))
         back_re, back_im = back[:, :lanes], back[:, lanes:]
         untwist_re = back_re * cos_twist - back_im * sin_twist
         untwist_im = back_im * cos_twist + back_re * sin_twist
@@ -296,10 +296,12 @@
 
     tables = pair_of(np.concatenate([cos_first, sin_first], 0))
     tables += [jnp.asarray(np.cos(twist_turn).astype(np.float32)), jnp.asarray(np.sin(twist_turn).astype(np.float32))]
-    tables += pair_of(np.concatenate([cos_second, -sin_second], 1))
-    tables += pair_of(np.concatenate([sin_second, cos_second], 1))
-    tables += pair_of(np.concatenate([cos_second, sin_second], 1))
-    tables += pair_of(np.concatenate([-sin_second, cos_second], 1))
+    fwd_a = np.concatenate([cos_second, -sin_second], 1)
+    fwd_b = np.concatenate([sin_second, cos_second], 1)
+    tables += pair_of(np.concatenate([fwd_a, fwd_b], 0))
+    inv_a = np.concatenate([cos_second, sin_second], 1)
+    inv_b = np.concatenate([-sin_second, cos_second], 1)
+    tables += pair_of(np.concatenate([inv_a, inv_b], 0))
     tables += pair_of(cos_first.T / all_bins)
     tables += pair_of(-sin_first.T / all_bins)
     return tables

time: 49.3 us -> 48.9 us (level)
  no operation moved by 1% of the time
where the time goes in v29:
time: 48.9 us; the launch traced here: 48.8 us
  Pallas kernels  44.9 us (92%)
  local copies, waits for them, and re-layouts  3.88 us (8%)
    pallas_call x1, Pallas kernels, whole(): pl.pallas_call(whole_kernel, out_shape=jax.ShapeDtypeStruct((length, widt...  44.9 us
    reshape x1, local copies, waits for them, and re-layouts, local(): spec_rows = spectrum.reshape(2, 2, second_len, ROW_GROUP, chan_width)  2.31 us
    unnamed x1, local copies, waits for them, and re-layouts  1.57 us

profile of v29, /device:TPU:1, one launch (start us, length us, event | category | flops | bytes accessed | tf_op | source)
XLA Modules:
  0.0 48.8 jit_solution(1327191549222901189)
XLA Ops:
  0.0 2.3 %copy.14 = f32[2,2,128,4,128]{2,3,1,0,4:T(4,128)} copy(f32[2,2,128,4,128]{4,3,2,1,0:T(4,128)} %bitcast.7) | data formatting | bytes 2097152 | tf_op jit(solution)/shard_map/reshape | solution.py:319
  2.3 44.9 %shard_map.127 = bf16[512,128]{1,0:T(8,128)(2,1)} custom-call(bf16[512,128]{1,0:T(8,128)(2,1)} %refs_0_.1, bf16[512,128]{1,0:T(8,128)(2,1)} %refs_1_.1, f32[1,128]{1,0:T(1,128)} %bitcast.8, f32[64,32,128]{2,1,0:T(8,128)} %bitcast.6, bf16[512,128]{1,0:T(8,128)(2,1)} %refs_4_.1, f32[1,128]{1,0:T(1,128)} %bitcast.9, bf16[1024,256]{1,0:T(8,128)(2,1)} %constant.14.clone.refs_6_, ...), custom_call_target="tpu_custom_call" | custom-call | tf_op jit(solution)/shard_map/pallas_call | solution.py:245
  47.3 1.6 %copy.16 = bf16[512,128]{1,0:T(8,128)(2,1)} copy(bf16[512,128]{1,0:T(8,128)(2,1)} %shard_map.127) | data formatting | bytes 262144
